TPU v7x, 32 devices: a whole 2x2x4 slice. The times are simulated.
32 devices in a mesh: blk: 16 (over z, y, x), rhs: 2 (over core).
Axes of the slice: x: 2, y: 2, z: 4, core: 2. Of those that a mesh axis runs over, the one named last changes fastest.
Arguments:
- panel: int32 [1], replicated, may hold values from 0 to 19
- strips: bfloat16 [2, 6, 4096, 1024], P(None, None, 'blk'), may hold values from -0.078125 to 0.078125
- dinv_rows: bfloat16 [6, 4096, 1024], P(None, 'blk'), as said below
- fwd_state: float32 [6, 4096, 1024], P(None, 'blk', 'rhs'), may hold values from -6 to 6
- back_state: float32 [6, 4096, 1024], P(None, 'blk', 'rhs'), may hold values from -6 to 6
Outputs:
- fwd_out: float32 [6, 4096, 1024], P(None, 'blk', 'rhs')
- back_out: float32 [6, 4096, 1024], P(None, 'blk', 'rhs')
Inputs may be any that keep to these rules, and one draw needn't show every extreme that they name: `dinv_rows`: E_k transposed is lower triangular, with its diagonal between 0.5 and 1.5.
All inputs are finite; a program needn't handle non-finite values.
Results may differ from a plain program's by a relative error of at most 0.0015.
Values may be sent and summed in bfloat16 or wider, within the bound.
No kernel may reach another device: no remote copies, remote signals or barrier semaphores. Data moves between devices by JAX's collectives and lax.ppermute only.
A program may use at most 64 MiB of HBM per device.

v0:
```python
import functools

import jax
import jax.numpy as jnp
from jax import lax
from jax.experimental import pallas as pl
from jax.experimental.pallas import tpu as pltpu
from jax.sharding import PartitionSpec as P

BF = jnp.bfloat16
HF = jnp.float16
F32 = jnp.float32
SUM_SCALE = 4.0
MIB = 1024 * 1024

NN = (((1,), (0,)), ((), ()))


def mm(a, b, dims):
    return lax.dot_general(a, b, dims, preferred_element_type=F32)


def plain_body(panel, strips, dinv_rows, fwd_state, back_state):
    tiles, span, columns = fwd_state.shape
    width = strips.shape[3]
    per_panel = width // span
    blocks = lax.axis_size("blk")
    device = lax.axis_index("blk")
    start = panel[0]
    slots = jnp.arange(tiles, dtype=jnp.int32)
    block_of = (slots * blocks + device) // per_panel

    def locate(k):
        offset = jnp.mod(device - per_panel * k, blocks)
        holds = offset < per_panel
        local = jnp.clip((per_panel * k + offset) // blocks, 0, tiles - 1)
        return (holds, local, jnp.minimum(offset, per_panel - 1))

    def forward(k, which, state):
        holds, local, offset = locate(k)
        strip = strips[which]
        current = lax.dynamic_index_in_dim(state, local, 0, keepdims=False).astype(BF)
        inv_tile = lax.dynamic_index_in_dim(dinv_rows, local, 0, keepdims=False)
        partial_rows = lax.dot_general(
            inv_tile, current, (((0,), (0,)), ((), ())), preferred_element_type=F32
        )
        partial_rows = jnp.where(holds, partial_rows, 0.0)
        later = (block_of > k)[:, None, None]
        solved = lax.psum(partial_rows, "blk")
        delta = jnp.einsum(
            "atw,wc->atc", strip, solved.astype(BF), preferred_element_type=F32
        )
        state = state - jnp.where(later, delta, 0.0)
        own_tile = lax.dynamic_slice_in_dim(solved, offset * span, span, 0)
        placed = lax.dynamic_update_index_in_dim(state, own_tile, local, 0)
        return jnp.where(holds, placed, state)

    def backward(k, which, state):
        holds, local, offset = locate(k)
        strip = strips[which]
        known = jnp.where((block_of > k)[:, None, None], state, 0.0).astype(BF)
        term = -jnp.einsum("atw,atc->wc", strip, known, preferred_element_type=F32)
        current = lax.dynamic_index_in_dim(state, local, 0, keepdims=False)
        placed_rows = lax.dynamic_update_slice_in_dim(
            jnp.zeros((width, columns), F32), current, offset * span, 0
        )
        term = term + jnp.where(holds, placed_rows, 0.0)
        summed = lax.psum(term, "blk").astype(BF)
        inv_tile = lax.dynamic_index_in_dim(dinv_rows, local, 0, keepdims=False)
        solved_tile = jnp.dot(inv_tile, summed, preferred_element_type=F32)
        placed = lax.dynamic_update_index_in_dim(state, solved_tile, local, 0)
        return jnp.where(holds, placed, state)

    fwd_out = forward(start, 0, fwd_state)
    fwd_out = forward(start + 1, 1, fwd_out)
    back_out = backward(start + 1, 1, back_state)
    back_out = backward(start, 0, back_out)
    return (fwd_out, back_out)


SLOT, OWNS, PANEL, PLANE, CHIP, CORE, KEEP, IS_A, FIRST, LOW = range(10)


def scalars(values):
    lane = lax.broadcasted_iota(jnp.int32, (16,), 0)
    out = jnp.zeros((16,), jnp.int32)
    for i, value in enumerate(values):
        out = jnp.where(lane == i, value.astype(jnp.int32), out)
    return out


def call(kernel, name, s, grid, ins, outs, shapes, arrays, scratch=(), aliases=None, limit=63):
    return pl.pallas_call(
        kernel,
        grid_spec=pltpu.PrefetchScalarGridSpec(
            num_scalar_prefetch=1, grid=grid, in_specs=ins, out_specs=outs, scratch_shapes=list(scratch)
        ),
        out_shape=shapes,
        input_output_aliases=aliases or {},
        compiler_params=pltpu.CompilerParams(vmem_limit_bytes=limit * MIB),
        name=name,
    )(s, *arrays)


def whole(*shape):
    return pl.BlockSpec(shape, lambda i, s: (0,) * len(shape), pipeline_mode=pl.Buffered(1))


def shaped(dtype, *shape):
    return jax.ShapeDtypeStruct(shape, dtype)


def prep_kernel(s, e_ref, w_ref, f_ref, *outs):
    half, width = e_ref.shape[1:]
    quarter = (outs[0].shape[1] - width) // 2
    for d in (1, 2, 3):
        at = pl.ds(pl.multiple_of((s[CHIP] ^ d) * quarter, quarter), quarter)
        high, low = split(f_ref[0, :, at])
        for out, matrix, f in ((outs[d - 1], e_ref[0], high), (outs[d + 2], w_ref[0, 0], low)):
            out[:, :width] = matrix
            out[:, width:width + quarter] = f[:half]
            out[:, width + quarter:] = f[half:]


def prep(s, strips, dinv_rows, fwd_state):
    tiles, span, columns = fwd_state.shape
    width = strips.shape[3]
    half, quarter = span // 2, columns // 4
    outs = call(
        prep_kernel, "prep", s, (1,),
        [
            pl.BlockSpec((1, half, width), lambda i, s: (s[SLOT], s[CORE], 0)),
            pl.BlockSpec((1, 1, half, width), lambda i, s: (0, s[SLOT], s[CORE], 0)),
            pl.BlockSpec((1, span, columns), lambda i, s: (s[SLOT], 0, 0)),
        ],
        [whole(half, width + 2 * quarter)] * 6,
        [shaped(BF, half, width + 2 * quarter)] * 6,
        (dinv_rows, strips, fwd_state),
    )
    return outs[:3], outs[3:]


def later(s, slot):
    return 4 * slot + s[PLANE] > s[PANEL] + 1


def sums_kernel(own, s, w_ref, b_ref, out_ref, *copies):
    a = pl.program_id(0)
    _, span, columns = b_ref.shape

    @pl.when(a == 0)
    def _():
        out_ref[...] = jnp.zeros_like(out_ref)

    for copy in copies:
        copy[...] = b_ref[...]

    @pl.when(later(s, 2 * a + 1))
    def _():
        b = b_ref[...].reshape(2 * span, columns) * SUM_SCALE
        row = lax.broadcasted_iota(jnp.int32, b.shape, 0)
        b = jnp.where((row >= span) | later(s, 2 * a), b, 0.0)
        out_ref[...] += mm(b.T.astype(BF), w_ref[0].reshape(2 * span, -1), NN)

    if own:
        @pl.when((a == s[SLOT] // 2) & (s[OWNS] == 1))
        def _():
            at = pl.ds(pl.multiple_of(s[CHIP] * span, span), span)
            out_ref[:, at] = out_ref[:, at] - (b_ref[s[SLOT] % 2] * SUM_SCALE).T


def sums(s, own, strips, back_state):
    tiles, span, columns = back_state.shape
    width = strips.shape[3]

    def which(s):
        return s[KEEP] if own else 1 - s[KEEP]

    def at(a, s):
        return jnp.maximum(a, s[FIRST] // 2)

    tile = pl.BlockSpec((2, span, columns), lambda a, s: (a if own else at(a, s), 0, 0))
    return call(
        functools.partial(sums_kernel, own), "sums", s, (tiles // 2,),
        [pl.BlockSpec((1, 2, span, width), lambda a, s: (which(s), at(a, s), 0, 0)), tile],
        [whole(columns, width)] + [tile] * own,
        [shaped(F32, columns, width)] + [shaped(F32, *back_state.shape)] * own,
        (strips, back_state),
    )


HBM = pl.BlockSpec(memory_space=pltpu.HBM)


def fetch(sems, pairs):
    copies = [pltpu.make_async_copy(a, b, sems.at[i]) for i, (a, b) in enumerate(pairs)]
    for copy in copies:
        copy.start()
    for copy in copies:
        copy.wait()


def halves(full, d, mine, other, core):
    half, width = mine.shape[0], full.shape[2]
    return [
        (mine.at[:, :width], full.at[d, pl.ds(pl.multiple_of(core * half, half), half), :]),
        (other.at[:, :width], full.at[d, pl.ds(pl.multiple_of((1 - core) * half, half), half), :]),
    ]


def block(full, d, mine, width):
    half, quarter = mine.shape[0], full.shape[2]
    return [
        (mine.at[:, width:width + quarter], full.at[d, :half, :]),
        (mine.at[:, width + quarter:], full.at[d, half:, :]),
    ]


def own_f(s, f, quarter):
    at = pl.ds(pl.multiple_of(s[CHIP] * quarter, quarter), quarter)
    return f.at[s[SLOT], :, at]


def split(x):
    high = x.astype(BF)
    return high, (x - high.astype(F32)).astype(BF)


def first_kernel(s, f, own, m1, m2, m3, o1, o2, o3, hi, lo, e, fv, hv, sems):
    _, quarter = fv.shape
    width = e.shape[2]
    pairs = [(own_f(s, f, quarter), fv), (own.at[s[SLOT]], e.at[0])]
    for d, mine, other in ((1, m1, o1), (2, m2, o2), (3, m3, o3)):
        pairs += halves(e, d, mine, other, s[CORE]) + block(hv, d, mine, width)
    fetch(sems, pairs)
    x = mm(fv[...].T.astype(BF), e[0], NN)
    for d in (1, 2, 3):
        x += mm(hv[d].astype(F32).T.astype(BF), e[d], NN)
    hi[...], lo[...] = split(x.T)


def second_kernel(
    s, f, strips, xp, e, m1, m2, m3, n1, n2, n3, o1, o2, o3, lo_a, hi, lo, w, fv, hv, gv, xv, ev, lv, sems
):
    _, quarter = fv.shape
    width = w.shape[2]
    pairs = [(own_f(s, f, quarter), fv), (xp, xv), (e, ev), (lo_a, lv), (strips.at[0, s[SLOT]], w.at[0])]
    for d, first, mine, other in ((1, m1, n1, o1), (2, m2, n2, o2), (3, m3, n3, o3)):
        pairs += halves(w, d, mine, other, s[CORE])
        pairs += block(hv, d, first, width) + block(gv, d, mine, width)
    fetch(sems, pairs)
    x = jnp.zeros((quarter, width), F32)
    for d in range(4):
        old = fv[...] if d == 0 else hv[d].astype(F32) + gv[d].astype(F32)
        new = old - mm(w[d], xv[...], NN)
        x += mm(new.T.astype(BF), ev[d], NN)
    high, low = split(x.T)
    hi[...] = high

    @pl.when(s[IS_A] == 1)
    def _():
        lo[...] = lv[...]

    @pl.when(s[IS_A] == 0)
    def _():
        lo[...] = low


def third_kernel(s, part, far, e, w, y, r, pv, rv, ev, wv, sems):
    fetch(sems, [(part, pv), (far, rv), (e, ev), (w, wv)])
    rest = ((pv[...] + rv[...]) * (-1.0 / SUM_SCALE)).T.astype(BF)
    back = jnp.zeros(r.shape, F32)
    for d in range(4):
        yq = mm(ev[d], rest, NN)
        y[s[CHIP] ^ d] = yq
        back += mm(yq.T.astype(BF), wv[d], NN)
    r[...] = back


def fourth_kernel(s, part, far, r, e, y_b, y, pv, rv, bv, ev, sems):
    @pl.when(s[IS_A] == 0)
    def _():
        fetch(sems, [(y_b, y)])

    @pl.when(s[IS_A] == 1)
    def _():
        fetch(sems, [(part, pv), (far, rv), (r, bv), (e, ev)])
        rest = ((pv[...] + rv[...]) * (-1.0 / SUM_SCALE) - bv[...]).T.astype(BF)
        for d in range(4):
            y[s[CHIP] ^ d] = mm(ev[d], rest, NN)


def fill(x_full, pieces, chip):
    for d, piece in enumerate(pieces):
        quarter = piece.shape[1]
        x_full[:, pl.ds(pl.multiple_of((chip ^ d) * quarter, quarter), quarter)] = piece[...]


def subtract(s, a, f_ref, w_ref, x_full, out_ref):
    _, span, width = w_ref.shape[1:]
    delta = mm(w_ref[0].reshape(2 * span, width), x_full[...], NN)
    for j in range(2):
        rest = f_ref[j] - delta[j * span:(j + 1) * span]
        out_ref[j] = jnp.where(later(s, 2 * a + j), rest, f_ref[j])


def update_one_kernel(s, f_ref, w_ref, x0, x1, x2, x3, out_ref, x_full):
    a = pl.program_id(0)

    @pl.when(a == 0)
    def _():
        fill(x_full, (x0, x1, x2, x3), s[CHIP])

    @pl.when(later(s, 2 * a + 1))
    def _():
        subtract(s, a, f_ref, w_ref, x_full, out_ref)

    @pl.when(jnp.logical_not(later(s, 2 * a + 1)))
    def _():
        out_ref[...] = f_ref[...]


def update_two_kernel(s, f_ref, w_ref, x0, x1, x2, x3, p0, p1, p2, p3, lo_ref, out_ref, x_full):
    a = pl.program_id(0)
    span = f_ref.shape[1]
    quarter = lo_ref.shape[2]

    @pl.when(a == 0)
    def _():
        fill(x_full, (x0, x1, x2, x3), s[CHIP])

    @pl.when(later(s, 2 * a + 1))
    def _():
        subtract(s, a, f_ref, w_ref, x_full, out_ref)

    @pl.when((a == s[LOW]) & jnp.logical_not(later(s, 2 * a + 1)))
    def _():
        out_ref[...] = f_ref[...]

    def solved(pieces):
        at = pl.ds(pl.multiple_of(s[CHIP] * span, span), span)
        for d, piece in enumerate(pieces):
            q = s[CHIP] ^ d
            x = piece[at, :].astype(F32) + lo_ref[q].astype(F32)
            out_ref[s[SLOT] % 2, :, pl.ds(pl.multiple_of(q * quarter, quarter), quarter)] = x

    own = (a == s[SLOT] // 2) & (s[OWNS] == 1)

    @pl.when(own & (s[IS_A] == 1))
    def _():
        solved((p0, p1, p2, p3))

    @pl.when(own & (s[IS_A] == 0))
    def _():
        solved((x0, x1, x2, x3))


def update(kernel, which, low, s, state, strips, pieces, own=(), aliases=None):
    tiles, span, columns = state.shape
    width = strips.shape[3]
    tile = pl.BlockSpec((2, span, columns), lambda a, s: (jnp.maximum(a, low(s)), 0, 0))
    return call(
        kernel, "update", s, (tiles // 2,),
        [tile, pl.BlockSpec((1, 2, span, width), lambda a, s: (which, jnp.maximum(a, s[FIRST] // 2), 0, 0))]
        + [whole(*x.shape) for x in (*pieces, *own)],
        tile, shaped(F32, *state.shape),
        (state, strips, *pieces, *own),
        scratch=[pltpu.VMEM((width, columns), BF)],
        aliases=aliases,
    )


def place_kernel(s, copy_ref, y_ref, out_ref):
    quarter = y_ref.shape[2]

    @pl.when(s[OWNS] == 1)
    def _():
        for q in range(4):
            out_ref[0, :, q * quarter:(q + 1) * quarter] = y_ref[q]

    @pl.when(s[OWNS] == 0)
    def _():
        out_ref[...] = copy_ref[...]


def place(s, copy, y):
    tiles, span, columns = copy.shape
    tile = pl.BlockSpec((1, span, columns), lambda i, s: (s[SLOT], 0, 0))
    return call(
        place_kernel, "place", s, (1,), [tile, whole(*y.shape)], tile,
        shaped(F32, *copy.shape), (copy, y), aliases={1: 0},
    )


def after(x, *waits):
    return lax.optimization_barrier((x,) + waits)[0]


def after_all(xs, *waits):
    return lax.optimization_barrier(tuple(xs) + waits)[:len(xs)]


def plane_body(panel, strips, dinv_rows, fwd_state, back_state):
    tiles, span, columns = fwd_state.shape
    width = strips.shape[3]
    half, quarter = span // 2, columns // 4
    device = lax.axis_index("blk")
    plane, chip, core = device // 4, device % 4, lax.axis_index("rhs")
    start = panel[0]
    home = lax.rem(start, 4)
    is_a = plane == home
    is_b = plane == lax.rem(start + 1, 4)
    groups = [[4 * z + j for j in range(4)] for z in range(4)]

    def exchange(x):
        return lax.all_to_all(x, "blk", 0, 0, axis_index_groups=groups, tiled=True)

    def permute(x, to):
        return lax.ppermute(x, "blk", [(i, to(i)) for i in range(16)])

    def up(x):
        return permute(x, lambda i: (i + 4) % 16)

    def down(x):
        return permute(x, lambda i: (i + 12) % 16)

    def across(x):
        return permute(x, lambda i: i ^ 8)

    def deal(xs):
        return [permute(x, lambda i, d=d: i ^ d) for d, x in zip((1, 2, 3), xs)]

    def gather(x):
        return deal([x] * 3)

    def swap(x):
        return lax.ppermute(x, "rhs", [(0, 1), (1, 0)])

    slot = start // 4 + jnp.where(is_b & (home == 3), 1, 0)
    first_later = jnp.clip((start + 5 - plane) // 4, 0, tiles - 1)
    low = jnp.minimum(first_later, jnp.where(is_a | is_b, slot, tiles - 1)) // 2
    keep = lax.rem(plane + start + 1, 2) == 0
    s = scalars([slot, is_a | is_b, start, plane, chip, core, keep, is_a, first_later, low])

    piece = shaped(BF, width, quarter)
    piece32 = shaped(F32, quarter, width)
    matrix = shaped(BF, 4, span, width)
    blocks = shaped(F32, 4, span, quarter)
    blocks16 = shaped(BF, 4, span, quarter)
    own = shaped(F32, span, quarter)

    def small(kernel, name, shapes, arrays, buffers, copies):
        return call(
            kernel, name, s, (1,), [HBM] * len(arrays), [whole(*x.shape) for x in shapes], shapes, arrays,
            scratch=[pltpu.VMEM(x.shape, x.dtype) for x in buffers] + [pltpu.SemaphoreType.DMA((copies,))],
        )

    (sent,) = sums(s, 0, strips, back_state)
    sent = sent.astype(HF)
    got = permute(sent, lambda i: i ^ 4)

    to_e, to_w = prep(after(s, sent), strips, dinv_rows, fwd_state)
    m = deal(to_e)
    kept, copy = sums(after(s, *to_e), 1, strips, back_state)
    m = after_all(m, kept)
    m_other = [swap(x) for x in m]
    n = deal(to_w)
    hi_p, lo_p, e = small(
        first_kernel, "first", [piece, piece, matrix], (fwd_state, dinv_rows, *m, *m_other), [own, blocks16], 14
    )
    below = up(hi_p)

    pair = (after(kept, hi_p) + got.astype(F32)).astype(HF)
    parts = exchange(pair).reshape(4, quarter, width)

    xp = jnp.where(is_a, hi_p, below)
    xp_far = across(xp)
    n_other = [swap(x) for x in n]
    hi_q, lo, w = small(
        second_kernel, "second", [piece, piece, matrix],
        (fwd_state, strips, xp, e, *m, *n, *n_other, lo_p), [own, blocks16, blocks16, piece, matrix, piece], 23,
    )
    part = jnp.sum(parts.astype(F32), axis=0)
    part16 = part.astype(HF)

    def last(first):
        source = (first + 1) % 4

        def send(x, *pairs):
            return lax.ppermute(x, "blk", [(4 * a + j, 4 * b + j) for a, b in pairs for j in range(4)])

        def run(x, xp, part):
            far = send(part, (first ^ 2, first), (source ^ 2, source))
            got = [send(x, (source, z)) for z in range(4) if z != source]
            return jnp.where(is_b, x, sum(got)), gather(xp), far.astype(F32)

        return run

    xp = jnp.where(is_a | is_b, xp, xp_far)
    xq, xp_rest, far = lax.switch(home, [last(z) for z in range(4)], hi_q, xp, part16)
    xp_all = [xp] + xp_rest
    xq_all = [xq] + gather(xq)

    y_b, r = small(
        third_kernel, "third", [blocks, piece32], (part, far, e, w),
        [piece32, piece32, matrix, matrix], 4,
    )
    r = down(r)
    lo_own = exchange(after(lo, y_b)).reshape(4, span, quarter)
    state = update(update_one_kernel, 0, lambda s: 0, after(s, y_b), fwd_state, strips, xp_all)
    (y,) = small(
        fourth_kernel, "fourth", [blocks], (part, far, r, e, after(y_b, state, *xq_all)),
        [piece32, piece32, piece32, matrix], 4,
    )
    y_own = exchange(y.reshape(4 * span, quarter)).reshape(4, span, quarter)
    fwd_out = update(
        update_two_kernel, 1, lambda s: s[LOW], after(s, y), state, strips, xq_all, (*xp_all, lo_own), {1: 0}
    )
    back_out = place(s, copy, y_own)
    return fwd_out, back_out


def body(panel, strips, dinv_rows, fwd_state, back_state):
    tiles, span, columns = fwd_state.shape
    width = strips.shape[3]
    blocks = lax.axis_size("blk")
    regular = (
        blocks == 16
        and lax.axis_size("rhs") == 2
        and width == 4 * span
        and span % 256 == 0
        and columns % 512 == 0
        and tiles % 2 == 0
    )
    chosen = plane_body if regular else plain_body
    return chosen(panel, strips, dinv_rows, fwd_state, back_state)


def solution(mesh):
    return jax.shard_map(
        body,
        mesh=mesh,
        in_specs=(
            P(),
            P(None, None, "blk", None),
            P(None, "blk", None),
            P(None, "blk", "rhs"),
            P(None, "blk", "rhs"),
        ),
        out_specs=(P(None, "blk", "rhs"), P(None, "blk", "rhs")),
        check_vma=False,
    )
```

profile of v0, /device:TPU:0, one launch (start us, length us, event | category | flops | bytes accessed | tf_op | source)
XLA Modules:
  0.0 138.0 jit_solution(556593448886927379)
XLA Ops:
  1.9 6.0 %sums.2 = f32[512,1024]{1,0:T(8,128)} custom-call(s32[16]{0:T(128)} %compare_select_fusion.9.s, bf16[2,6,256,1024]{3,2,1,0:T(8,128)(2,1)} %w_ref.9, f32[6,256,512]{2,1,0:T(8,128)} %b_ref.3), custom_call_target="tpu_custom_call" | custom-call | tf_op jit(solution)/shard_map/sums/pallas_call | solution.py:93
  7.9 2.7 %convert_element_type.49 = f16[512,1024]{1,0:T(8,128)(2,1)} convert(f32[512,1024]{1,0:T(8,128)} %sums.2) | non-fusion elementwise | flops 524288 | bytes 3145728 | tf_op jit(solution)/shard_map/convert_element_type | solution.py:459
  10.7 3.0 %collective-permute-start.34 = (f16[512,1024]{1,0:T(8,128)(2,1)}, f16[512,1024]{1,0:T(8,128)(2,1)}, u32[]{:S(2)}, u32[]{:S(2)}) collective-permute-start(f16[512,1024]{1,0:T(8,128)(2,1)} %convert_element_type.49), channel_id=1, source_target_pairs={{0,8},{2,10},{4,12},{6,14},{8,0},{10,2},{12,4},{14,6},{16,24},{18,... | collective-permute-start | bytes 3145736 | tf_op jit(solution)/shard_map/ppermute | solution.py:419
  13.7 3.2 %prep.1 = (bf16[128,1280]{1,0:T(8,128)(2,1)}, bf16[128,1280]{1,0:T(8,128)(2,1)}, bf16[128,1280]{1,0:T(8,128)(2,1)}, bf16[128,1280]{1,0:T(8,128)(2,1)}, bf16[128,...) custom-call(s32[16]{0:T(128)} %compare_select_fusion.9.s, bf16[6,256,1024]{2,1,0:T(8,128)(2,1)} %own.1, ...), custom_call_target="tpu_custom_call" | custom-call | tf_op jit(solution)/shard_map/prep/pallas_call | solution.py:93
  16.9 1.5 %collective-permute-start.28 = (bf16[128,1280]{1,0:T(8,128)(2,1)}, bf16[128,1280]{1,0:T(8,128)(2,1)S(1)}, u32[]{:S(2)}, u32[]{:S(2)}) collective-permute-start(bf16[128,1280]{1,0:T(8,128)(2,1)} %get-tuple-element.96), channel_id=1, source_target_pairs={{0,2},{2,0},{4,6},{6,4},{8,10},{10,8},{12,14},{14,12},{16,18},{18,... | collective-permute-start | bytes 983048 | tf_op jit(solution)/shard_map/ppermute | solution.py:419
  18.4 1.5 %collective-permute-start.29 = (bf16[128,1280]{1,0:T(8,128)(2,1)}, bf16[128,1280]{1,0:T(8,128)(2,1)S(1)}, u32[]{:S(2)}, u32[]{:S(2)}) collective-permute-start(bf16[128,1280]{1,0:T(8,128)(2,1)} %get-tuple-element.97), channel_id=1, source_target_pairs={{0,4},{2,6},{4,0},{6,2},{8,12},{10,14},{12,8},{14,10},{16,20},{18,... | collective-permute-start | bytes 983048 | tf_op jit(solution)/shard_map/ppermute | solution.py:419
  20.4 7.1 %sums.3 = (f32[512,1024]{1,0:T(8,128)}, f32[6,256,512]{2,1,0:T(8,128)}) custom-call(s32[16]{0:T(128)} %compare_select_fusion.9.s, bf16[2,6,256,1024]{3,2,1,0:T(8,128)(2,1)} %w_ref.9, f32[6,256,512]{2,1,0:T(8,128)} %b_ref.3), custom_call_target="tpu_custom_call" | custom-call | tf_op jit(solution)/shard_map/sums/pallas_call | solution.py:93
  27.7 6.8 %collective-permute-done.29.m2 = bf16[128,1280]{1,0:T(8,128)(2,1)S(1)} collective-permute-done((bf16[128,1280]{1,0:T(8,128)(2,1)}, bf16[128,1280]{1,0:T(8,128)(2,1)S(1)}, u32[]{:S(2)}, u32[]{:S(2)}) %collective-permute-start.29) | collective-permute-done | bytes 327712 | tf_op jit(solution)/shard_map/ppermute | solution.py:419
  36.3 1.5 %collective-permute-start.37 = (bf16[128,1280]{1,0:T(8,128)(2,1)}, bf16[128,1280]{1,0:T(8,128)(2,1)}, u32[]{:S(2)}, u32[]{:S(2)}) collective-permute-start(bf16[128,1280]{1,0:T(8,128)(2,1)} %get-tuple-element.108), channel_id=1, source_target_pairs={{0,4},{2,6},{4,0},{6,2},{8,12},{10,14},{12,8},{14,10},{16,20},{18,... | collective-permute-start | bytes 983048 | tf_op jit(solution)/shard_map/ppermute | solution.py:419
  39.7 4.6 %first.1 = (bf16[1024,128]{1,0:T(8,128)(2,1)}, bf16[1024,128]{1,0:T(8,128)(2,1)}, bf16[4,256,1024]{2,1,0:T(8,128)(2,1)}) custom-call(s32[16]{0:T(128)} %compare_select_fusion.9.s, f32[6,256,512]{2,1,0:T(8,128)} %f_ref.3, bf16[6,256,1024]{2,1,0:T(8,128)(2,1)} %own.1, bf16[128,1280]{1,0:T(8,128)(2,1)} %copy-done.3, bf16[128,1280]{1,0:T(8,128)(2,1)} %copy-done.4, ...), custom_call_target="tpu_custom_call" | custom-call | tf_op jit(solution)/shard_map/first/pallas_call | solution.py:93
  44.8 3.2 %add_convert_fusion = f16[512,1024]{1,0:T(8,128)(2,1)} fusion(f32[512,1024]{1,0:T(8,128)} %get-tuple-element.105, f16[512,1024]{1,0:T(8,128)(2,1)} %collective-permute-done.34), kind=kLoop, calls=%fused_computation.5 | loop fusion | flops 1572864 | bytes 4194304 | tf_op jit(solution)/shard_map/convert_element_type | solution.py:473
  48.0 4.2 %all-to-all-start = ((f16[4,128,1024]{2,1,0:T(8,128)(2,1)}), f16[4,128,1024]{2,1,0:T(8,128)(2,1)}, u32[]{:S(2)}, u32[]{:S(2)}) async-start(f16[4,128,1024]{2,1,0:T(8,128)(2,1)} %bitcast.1), calls=%async_computation | async-start | bytes 2097152 | tf_op jit(solution)/shard_map/all_to_all | solution.py:416
  54.5 1.8 %collective-permute-start.42 = (bf16[1024,128]{1,0:T(8,128)(2,1)S(1)}, bf16[1024,128]{1,0:T(8,128)(2,1)S(1)}, u32[]{:S(2)}, u32[]{:S(2)}) collective-permute-start(bf16[1024,128]{1,0:T(8,128)(2,1)S(1)} %broadcast_select_fusion.1.xp), channel_id=1, source_target_pairs={{0,16},{2,18},{4,20},{6,22},{8,24},{10,26},{12,28},{14,30},{16,0},... | collective-permute-start | bytes 786440 | tf_op jit(solution)/shard_map/ppermute | solution.py:419
  57.2 6.4 %second.1 = (bf16[1024,128]{1,0:T(8,128)(2,1)S(1)}, bf16[1024,128]{1,0:T(8,128)(2,1)}, bf16[4,256,1024]{2,1,0:T(8,128)(2,1)}) custom-call(s32[16]{0:T(128)} %compare_select_fusion.9.s, f32[6,256,512]{2,1,0:T(8,128)} %f_ref.3, bf16[2,6,256,1024]{3,2,1,0:T(8,128)(2,1)} %w_ref.9, bf16[1024,128]{1,0:T(8,128)(2,1)} %copy-done.1, ...), custom_call_target="tpu_custom_call" | custom-call | tf_op jit(solution)/shard_map/second/pallas_call | solution.py:93
  63.6 5.3 %collective-permute-done.42 = bf16[1024,128]{1,0:T(8,128)(2,1)S(1)} collective-permute-done((bf16[1024,128]{1,0:T(8,128)(2,1)S(1)}, bf16[1024,128]{1,0:T(8,128)(2,1)S(1)}, u32[]{:S(2)}, u32[]{:S(2)}) %collective-permute-start.42) | collective-permute-done | bytes 262176 | tf_op jit(solution)/shard_map/ppermute | solution.py:419
  69.6 1.5 %convert_reduce_fusion.part = f32[128,1024]{1,0:T(8,128)S(1)} fusion(f16[4,128,1024]{2,1,0:T(8,128)(2,1)} %all-to-all-done), kind=kLoop, calls=%fused_computation.4 | loop fusion | flops 917504 | bytes 1572864 | tf_op jit(solution)/shard_map/reduce_sum | solution.py:483
  71.9 24.3 %conditional.4 = (bf16[1024,128]{1,0:T(8,128)(2,1)}, bf16[1024,128]{1,0:T(8,128)(2,1)}, bf16[1024,128]{1,0:T(8,128)(2,1)}, bf16[1024,128]{1,0:T(8,128)(2,1)}, f32[128,1024]{1,0:T(8,128)S(1)}) conditional(s32[]{:T(128)} %clamp.3, (pred[]{:T(512)}, bf16[1024,128]{1,0:T(8,128)(2,1)S(1)}, bf16[1024,128]{1,0:T(8,128)(2,1)}, ...), branch_computations={%region_1.2_spmd, %region_2.3_spmd, %region_3.4_spmd, %region_4.5_... | conditional | flops 524288 | bytes 9437505
  71.9 2.4 %collective-permute-start.20 = (f16[128,1024]{1,0:T(8,128)(2,1)S(1)}, f16[128,1024]{1,0:T(8,128)(2,1)S(1)}, u32[]{:S(2)}, u32[]{:S(2)}) collective-permute-start(f16[128,1024]{1,0:T(8,128)(2,1)S(1)} %get-tuple-element.57), channel_id=1, source_target_pairs={{0,16},{2,18},{4,20},{6,22},{8,24},{10,26},{12,28},{14,30},{1,17},... | collective-permute-start | bytes 786440 | tf_op jit(solution)/shard_map/cond/branch_2_fun/ppermute | solution.py:490
  77.0 2.1 %collective-permute-start.19 = (bf16[1024,128]{1,0:T(8,128)(2,1)}, bf16[1024,128]{1,0:T(8,128)(2,1)}, u32[]{:S(2)}, u32[]{:S(2)}) collective-permute-start(bf16[1024,128]{1,0:T(8,128)(2,1)} %get-tuple-element.56), channel_id=1, source_target_pairs={{0,6},{2,4},{4,2},{6,0},{8,14},{10,12},{12,10},{14,8},{16,22},{18,... | collective-permute-start | bytes 786440 | tf_op jit(solution)/shard_map/cond/branch_2_fun/ppermute | solution.py:419
  79.2 1.3 collective-permute-start.18
  80.5 1.7 %collective-permute-start.17 = (bf16[1024,128]{1,0:T(8,128)(2,1)}, bf16[1024,128]{1,0:T(8,128)(2,1)}, u32[]{:S(2)}, u32[]{:S(2)}) collective-permute-start(bf16[1024,128]{1,0:T(8,128)(2,1)} %get-tuple-element.56), channel_id=1, source_target_pairs={{0,2},{2,0},{4,6},{6,4},{8,10},{10,8},{12,14},{14,12},{16,18},{18,... | collective-permute-start | bytes 786440 | tf_op jit(solution)/shard_map/cond/branch_2_fun/ppermute | solution.py:419
  82.2 13.3 %collective-permute-done.14 = bf16[1024,128]{1,0:T(8,128)(2,1)S(1)} collective-permute-done((bf16[1024,128]{1,0:T(8,128)(2,1)S(1)}, bf16[1024,128]{1,0:T(8,128)(2,1)S(1)}, u32[]{:S(2)}, u32[]{:S(2)}) %collective-permute-start.14) | collective-permute-done | bytes 262176 | tf_op jit(solution)/shard_map/cond/branch_2_fun/ppermute | solution.py:490
  96.2 5.5 %third.1 = (f32[4,256,128]{2,1,0:T(8,128)}, f32[128,1024]{1,0:T(8,128)}) custom-call(s32[16]{0:T(128)} %compare_select_fusion.9.s, f32[128,1024]{1,0:T(8,128)} %copy-done, f32[128,1024]{1,0:T(8,128)S(1)} %get-tuple-element.132.far, bf16[4,256,1024]{2,1,0:T(8,128)(2,1)} %get-tuple-element.106.e, bf16[4,256,1024]{2,1,0:T(8,128)(2,1)} %get-tuple-element.113.w), custom_call_target="tpu_custom_call" | custom-call | tf_op jit(solution)/shard_map/third/pallas_call | solution.py:93
  101.7 2.9 %collective-permute-start.43 = (f32[128,1024]{1,0:T(8,128)}, f32[128,1024]{1,0:T(8,128)}, u32[]{:S(2)}, u32[]{:S(2)}) collective-permute-start(f32[128,1024]{1,0:T(8,128)} %get-tuple-element.114), channel_id=1, source_target_pairs={{0,24},{2,26},{4,28},{6,30},{8,0},{10,2},{12,4},{14,6},{16,8},{18,... | collective-permute-start | bytes 1572872 | tf_op jit(solution)/shard_map/ppermute | solution.py:419
  104.7 2.4 %collective-permute-start.46 = (bf16[1024,128]{1,0:T(8,128)(2,1)}, bf16[1024,128]{1,0:T(8,128)(2,1)}, u32[]{:S(2)}, u32[]{:S(2)}) collective-permute-start(bf16[1024,128]{1,0:T(8,128)(2,1)} %get-tuple-element.120.x0), channel_id=1, source_target_pairs={{0,6},{2,4},{4,2},{6,0},{8,14},{10,12},{12,10},{14,8},{16,22},{18,... | collective-permute-start | bytes 786440 | tf_op jit(solution)/shard_map/ppermute | solution.py:419
  108.2 3.7 %all-to-all-start.1 = ((bf16[4,256,128]{2,1,0:T(8,128)(2,1)}), bf16[4,256,128]{2,1,0:T(8,128)(2,1)S(1)}, u32[]{:S(2)}, u32[]{:S(2)}) async-start(bf16[4,256,128]{2,1,0:T(8,128)(2,1)} %bitcast.11), calls=%async_computation.1 | async-start | bytes 524288 | tf_op jit(solution)/shard_map/all_to_all | solution.py:416
  111.9 6.8 %update.2.f_ref = f32[6,256,512]{2,1,0:T(8,128)} custom-call(s32[16]{0:T(128)} %compare_select_fusion.9.s, f32[6,256,512]{2,1,0:T(8,128)} %f_ref.3, bf16[2,6,256,1024]{3,2,1,0:T(8,128)(2,1)} %w_ref.9, bf16[1024,128]{1,0:T(8,128)(2,1)} %broadcast_select_fusion.x0.p0, bf16[1024,128]{1,0:T(8,128)(2,1)} %get-tuple-element.117.x1.p1, ...), custom_call_target="tpu_custom_call" | custom-call | tf_op jit(solution)/shard_map/update/pallas_call | solution.py:93
  118.7 1.4 %collective-permute-done.45.x2 = bf16[1024,128]{1,0:T(8,128)(2,1)} collective-permute-done((bf16[1024,128]{1,0:T(8,128)(2,1)}, bf16[1024,128]{1,0:T(8,128)(2,1)}, u32[]{:S(2)}, u32[]{:S(2)}) %collective-permute-start.45) | collective-permute-done | bytes 262176 | tf_op jit(solution)/shard_map/ppermute | solution.py:419
  120.8 2.5 %fourth.1 = f32[4,256,128]{2,1,0:T(8,128)} custom-call(s32[16]{0:T(128)} %compare_select_fusion.9.s, f32[128,1024]{1,0:T(8,128)} %copy-done, f32[128,1024]{1,0:T(8,128)S(1)} %get-tuple-element.132.far, f32[128,1024]{1,0:T(8,128)} %collective-permute-done.43.r, bf16[4,256,1024]{2,1,0:T(8,128)(2,1)} %get-tuple-element.106.e, f32[4,256,128]{2,1,0:T(8,128)} %get-tuple-element.121.y_b), custom_call_target="tpu_custom_call" | custom-call | tf_op jit(solution)/shard_map/fourth/pallas_call | solution.py:93
  123.3 3.5 %all-to-all-start.2 = ((f32[4,256,128]{2,1,0:T(8,128)}), f32[4,256,128]{2,1,0:T(8,128)S(1)}, u32[]{:S(2)}, u32[]{:S(2)}) async-start(f32[4,256,128]{2,1,0:T(8,128)} %fourth.1), calls=%async_computation.2 | async-start | bytes 1048576 | tf_op jit(solution)/shard_map/all_to_all | solution.py:416
  126.8 6.4 %update.3 = f32[6,256,512]{2,1,0:T(8,128)} custom-call(s32[16]{0:T(128)} %compare_select_fusion.9.s, f32[6,256,512]{2,1,0:T(8,128)} %update.2.f_ref, bf16[2,6,256,1024]{3,2,1,0:T(8,128)(2,1)} %w_ref.9, bf16[1024,128]{1,0:T(8,128)(2,1)} %get-tuple-element.120.x0, bf16[1024,128]{1,0:T(8,128)(2,1)} %collective-permute-done.44.x1, ...), custom_call_target="tpu_custom_call", output_to_operand_aliasing={{}: (1, {})} | custom-call | tf_op jit(solution)/shard_map/update/pallas_call | solution.py:93
  135.3 2.7 %place.1 = f32[6,256,512]{2,1,0:T(8,128)} custom-call(s32[16]{0:T(128)} %compare_select_fusion.9.s, f32[6,256,512]{2,1,0:T(8,128)} %get-tuple-element.125.copy_ref, f32[4,256,128]{2,1,0:T(8,128)} %copy-done.2), custom_call_target="tpu_custom_call", output_to_operand_aliasing={{}: (1, {})} | custom-call | tf_op jit(solution)/shard_map/place/pallas_call | solution.py:93
  (72 shorter events, 17.4 us)
Async XLA Ops:
  10.7 34.1 %collective-permute-start.34 = (f16[512,1024]{1,0:T(8,128)(2,1)}, f16[512,1024]{1,0:T(8,128)(2,1)}, u32[]{:S(2)}, u32[]{:S(2)}) collective-permute-start(f16[512,1024]{1,0:T(8,128)(2,1)} %convert_element_type.49), channel_id=1, source_target_pairs={{0,8},{2,10},{4,12},{6,14},{8,0},{10,2},{12,4},{14,6},{16,24},{18,... | collective-permute-start | bytes 3145736 | tf_op jit(solution)/shard_map/ppermute | solution.py:419
  16.9 10.8 %collective-permute-start.28 = (bf16[128,1280]{1,0:T(8,128)(2,1)}, bf16[128,1280]{1,0:T(8,128)(2,1)S(1)}, u32[]{:S(2)}, u32[]{:S(2)}) collective-permute-start(bf16[128,1280]{1,0:T(8,128)(2,1)} %get-tuple-element.96), channel_id=1, source_target_pairs={{0,2},{2,0},{4,6},{6,4},{8,10},{10,8},{12,14},{14,12},{16,18},{18,... | collective-permute-start | bytes 983048 | tf_op jit(solution)/shard_map/ppermute | solution.py:419
  18.4 16.1 %collective-permute-start.29 = (bf16[128,1280]{1,0:T(8,128)(2,1)}, bf16[128,1280]{1,0:T(8,128)(2,1)S(1)}, u32[]{:S(2)}, u32[]{:S(2)}) collective-permute-start(bf16[128,1280]{1,0:T(8,128)(2,1)} %get-tuple-element.97), channel_id=1, source_target_pairs={{0,4},{2,6},{4,0},{6,2},{8,12},{10,14},{12,8},{14,10},{16,20},{18,... | collective-permute-start | bytes 983048 | tf_op jit(solution)/shard_map/ppermute | solution.py:419
  19.9 14.6 %collective-permute-start.30 = (bf16[128,1280]{1,0:T(8,128)(2,1)}, bf16[128,1280]{1,0:T(8,128)(2,1)S(1)}, u32[]{:S(2)}, u32[]{:S(2)}) collective-permute-start(bf16[128,1280]{1,0:T(8,128)(2,1)} %get-tuple-element.98), channel_id=1, source_target_pairs={{0,6},{2,4},{4,2},{6,0},{8,14},{10,12},{12,10},{14,8},{16,22},{18,... | collective-permute-start | bytes 983048 | tf_op jit(solution)/shard_map/ppermute | solution.py:419
  27.7 11.9 %copy-start.3 = (bf16[128,1280]{1,0:T(8,128)(2,1)}, bf16[128,1280]{1,0:T(8,128)(2,1)S(1)}, u32[]{:S(2)}) copy-start(bf16[128,1280]{1,0:T(8,128)(2,1)S(1)} %collective-permute-done.28.m1) | copy-start | bytes 983044
  34.5 5.2 %copy-start.4 = (bf16[128,1280]{1,0:T(8,128)(2,1)}, bf16[128,1280]{1,0:T(8,128)(2,1)S(1)}, u32[]{:S(2)}) copy-start(bf16[128,1280]{1,0:T(8,128)(2,1)S(1)} %collective-permute-done.29.m2) | copy-start | bytes 983044
  34.5 1.8 %collective-permute-start.31 = (bf16[128,1280]{1,0:T(8,128)(2,1)S(1)}, bf16[128,1280]{1,0:T(8,128)(2,1)S(1)}, u32[]{:S(2)}, u32[]{:S(2)}) collective-permute-start(bf16[128,1280]{1,0:T(8,128)(2,1)S(1)} %collective-permute-done.28.m1), channel_id=1, source_target_pairs={{0,1},{1,0},{2,3},{3,2},{4,5},{5,4},{6,7},{7,6},{8,9},{9,8},{10,11... | collective-permute-start | bytes 983048 | tf_op jit(solution)/shard_map/ppermute | solution.py:437
  34.6 3.1 %collective-permute-start.32 = (bf16[128,1280]{1,0:T(8,128)(2,1)S(1)}, bf16[128,1280]{1,0:T(8,128)(2,1)S(1)}, u32[]{:S(2)}, u32[]{:S(2)}) collective-permute-start(bf16[128,1280]{1,0:T(8,128)(2,1)S(1)} %collective-permute-done.29.m2), channel_id=1, source_target_pairs={{0,1},{1,0},{2,3},{3,2},{4,5},{5,4},{6,7},{7,6},{8,9},{9,8},{10,11... | collective-permute-start | bytes 983048 | tf_op jit(solution)/shard_map/ppermute | solution.py:437
  35.1 4.6 %collective-permute-start.33 = (bf16[128,1280]{1,0:T(8,128)(2,1)S(1)}, bf16[128,1280]{1,0:T(8,128)(2,1)}, u32[]{:S(2)}, u32[]{:S(2)}) collective-permute-start(bf16[128,1280]{1,0:T(8,128)(2,1)S(1)} %collective-permute-done.30.m3), channel_id=1, source_target_pairs={{0,1},{1,0},{2,3},{3,2},{4,5},{5,4},{6,7},{7,6},{8,9},{9,8},{10,11... | collective-permute-start | bytes 983048 | tf_op jit(solution)/shard_map/ppermute | solution.py:437
  35.2 17.0 %collective-permute-start.36 = (bf16[128,1280]{1,0:T(8,128)(2,1)}, bf16[128,1280]{1,0:T(8,128)(2,1)}, u32[]{:S(2)}, u32[]{:S(2)}) collective-permute-start(bf16[128,1280]{1,0:T(8,128)(2,1)} %get-tuple-element.107), channel_id=1, source_target_pairs={{0,2},{2,0},{4,6},{6,4},{8,10},{10,8},{12,14},{14,12},{16,18},{18,... | collective-permute-start | bytes 983048 | tf_op jit(solution)/shard_map/ppermute | solution.py:419
  36.3 16.1 %collective-permute-start.37 = (bf16[128,1280]{1,0:T(8,128)(2,1)}, bf16[128,1280]{1,0:T(8,128)(2,1)}, u32[]{:S(2)}, u32[]{:S(2)}) collective-permute-start(bf16[128,1280]{1,0:T(8,128)(2,1)} %get-tuple-element.108), channel_id=1, source_target_pairs={{0,4},{2,6},{4,0},{6,2},{8,12},{10,14},{12,8},{14,10},{16,20},{18,... | collective-permute-start | bytes 983048 | tf_op jit(solution)/shard_map/ppermute | solution.py:419
  38.5 15.0 %collective-permute-start.38 = (bf16[128,1280]{1,0:T(8,128)(2,1)}, bf16[128,1280]{1,0:T(8,128)(2,1)}, u32[]{:S(2)}, u32[]{:S(2)}) collective-permute-start(bf16[128,1280]{1,0:T(8,128)(2,1)} %get-tuple-element.109), channel_id=1, source_target_pairs={{0,6},{2,4},{4,2},{6,0},{8,14},{10,12},{12,10},{14,8},{16,22},{18,... | collective-permute-start | bytes 983048 | tf_op jit(solution)/shard_map/ppermute | solution.py:419
  44.3 10.2 %copy-start.12 = (bf16[1024,128]{1,0:T(8,128)(2,1)S(1)}, bf16[1024,128]{1,0:T(8,128)(2,1)}, u32[]{:S(2)}) copy-start(bf16[1024,128]{1,0:T(8,128)(2,1)} %get-tuple-element.104) | copy-start | bytes 786436
  44.3 10.2 %collective-permute-start.35 = (bf16[1024,128]{1,0:T(8,128)(2,1)}, bf16[1024,128]{1,0:T(8,128)(2,1)S(1)}, u32[]{:S(2)}, u32[]{:S(2)}) collective-permute-start(bf16[1024,128]{1,0:T(8,128)(2,1)} %get-tuple-element.104), channel_id=1, source_target_pairs={{0,8},{2,10},{4,12},{6,14},{8,16},{10,18},{12,20},{14,22},{16,24},... | collective-permute-start | bytes 786440 | tf_op jit(solution)/shard_map/ppermute | solution.py:419
  48.0 21.7 %all-to-all-start = ((f16[4,128,1024]{2,1,0:T(8,128)(2,1)}), f16[4,128,1024]{2,1,0:T(8,128)(2,1)}, u32[]{:S(2)}, u32[]{:S(2)}) async-start(f16[4,128,1024]{2,1,0:T(8,128)(2,1)} %bitcast.1), calls=%async_computation | async-start | bytes 2097152 | tf_op jit(solution)/shard_map/all_to_all | solution.py:416
  52.2 4.0 %collective-permute-start.39 = (bf16[128,1280]{1,0:T(8,128)(2,1)}, bf16[128,1280]{1,0:T(8,128)(2,1)S(1)}, u32[]{:S(2)}, u32[]{:S(2)}) collective-permute-start(bf16[128,1280]{1,0:T(8,128)(2,1)} %collective-permute-done.36.n1), channel_id=1, source_target_pairs={{0,1},{1,0},{2,3},{3,2},{4,5},{5,4},{6,7},{7,6},{8,9},{9,8},{10,11... | collective-permute-start | bytes 983048 | tf_op jit(solution)/shard_map/ppermute | solution.py:437
  52.3 3.9 %collective-permute-start.40 = (bf16[128,1280]{1,0:T(8,128)(2,1)}, bf16[128,1280]{1,0:T(8,128)(2,1)S(1)}, u32[]{:S(2)}, u32[]{:S(2)}) collective-permute-start(bf16[128,1280]{1,0:T(8,128)(2,1)} %collective-permute-done.37.n2), channel_id=1, source_target_pairs={{0,1},{1,0},{2,3},{3,2},{4,5},{5,4},{6,7},{7,6},{8,9},{9,8},{10,11... | collective-permute-start | bytes 983048 | tf_op jit(solution)/shard_map/ppermute | solution.py:437
  53.5 2.7 %collective-permute-start.41 = (bf16[128,1280]{1,0:T(8,128)(2,1)}, bf16[128,1280]{1,0:T(8,128)(2,1)S(1)}, u32[]{:S(2)}, u32[]{:S(2)}) collective-permute-start(bf16[128,1280]{1,0:T(8,128)(2,1)} %collective-permute-done.38.n3), channel_id=1, source_target_pairs={{0,1},{1,0},{2,3},{3,2},{4,5},{5,4},{6,7},{7,6},{8,9},{9,8},{10,11... | collective-permute-start | bytes 983048 | tf_op jit(solution)/shard_map/ppermute | solution.py:437
  54.5 14.4 %collective-permute-start.42 = (bf16[1024,128]{1,0:T(8,128)(2,1)S(1)}, bf16[1024,128]{1,0:T(8,128)(2,1)S(1)}, u32[]{:S(2)}, u32[]{:S(2)}) collective-permute-start(bf16[1024,128]{1,0:T(8,128)(2,1)S(1)} %broadcast_select_fusion.1.xp), channel_id=1, source_target_pairs={{0,16},{2,18},{4,20},{6,22},{8,24},{10,26},{12,28},{14,30},{16,0},... | collective-permute-start | bytes 786440 | tf_op jit(solution)/shard_map/ppermute | solution.py:419
  71.9 7.2 %collective-permute-start.20 = (f16[128,1024]{1,0:T(8,128)(2,1)S(1)}, f16[128,1024]{1,0:T(8,128)(2,1)S(1)}, u32[]{:S(2)}, u32[]{:S(2)}) collective-permute-start(f16[128,1024]{1,0:T(8,128)(2,1)S(1)} %get-tuple-element.57), channel_id=1, source_target_pairs={{0,16},{2,18},{4,20},{6,22},{8,24},{10,26},{12,28},{14,30},{1,17},... | collective-permute-start | bytes 786440 | tf_op jit(solution)/shard_map/cond/branch_2_fun/ppermute | solution.py:490
  74.3 6.1 %collective-permute-start.16 = (bf16[1024,128]{1,0:T(8,128)(2,1)S(1)}, bf16[1024,128]{1,0:T(8,128)(2,1)S(1)}, u32[]{:S(2)}, u32[]{:S(2)}) collective-permute-start(bf16[1024,128]{1,0:T(8,128)(2,1)S(1)} %get-tuple-element.55), channel_id=1, source_target_pairs={{24,16},{26,18},{28,20},{30,22},{25,17},{27,19},{29,21},{31,23}} | collective-permute-start | bytes 786440 | tf_op jit(solution)/shard_map/cond/branch_2_fun/ppermute | solution.py:490
  75.0 7.2 %collective-permute-start.15 = (bf16[1024,128]{1,0:T(8,128)(2,1)S(1)}, bf16[1024,128]{1,0:T(8,128)(2,1)S(1)}, u32[]{:S(2)}, u32[]{:S(2)}) collective-permute-start(bf16[1024,128]{1,0:T(8,128)(2,1)S(1)} %get-tuple-element.55), channel_id=1, source_target_pairs={{24,8},{26,10},{28,12},{30,14},{25,9},{27,11},{29,13},{31,15}} | collective-permute-start | bytes 786440 | tf_op jit(solution)/shard_map/cond/branch_2_fun/ppermute | solution.py:490
  75.7 19.7 %collective-permute-start.14 = (bf16[1024,128]{1,0:T(8,128)(2,1)S(1)}, bf16[1024,128]{1,0:T(8,128)(2,1)S(1)}, u32[]{:S(2)}, u32[]{:S(2)}) collective-permute-start(bf16[1024,128]{1,0:T(8,128)(2,1)S(1)} %get-tuple-element.55), channel_id=1, source_target_pairs={{24,0},{26,2},{28,4},{30,6},{25,1},{27,3},{29,5},{31,7}} | collective-permute-start | bytes 786440 | tf_op jit(solution)/shard_map/cond/branch_2_fun/ppermute | solution.py:490
  77.0 19.2 %collective-permute-start.19 = (bf16[1024,128]{1,0:T(8,128)(2,1)}, bf16[1024,128]{1,0:T(8,128)(2,1)}, u32[]{:S(2)}, u32[]{:S(2)}) collective-permute-start(bf16[1024,128]{1,0:T(8,128)(2,1)} %get-tuple-element.56), channel_id=1, source_target_pairs={{0,6},{2,4},{4,2},{6,0},{8,14},{10,12},{12,10},{14,8},{16,22},{18,... | collective-permute-start | bytes 786440 | tf_op jit(solution)/shard_map/cond/branch_2_fun/ppermute | solution.py:419
  79.2 17.0 %collective-permute-start.18 = (bf16[1024,128]{1,0:T(8,128)(2,1)}, bf16[1024,128]{1,0:T(8,128)(2,1)}, u32[]{:S(2)}, u32[]{:S(2)}) collective-permute-start(bf16[1024,128]{1,0:T(8,128)(2,1)} %get-tuple-element.56), channel_id=1, source_target_pairs={{0,4},{2,6},{4,0},{6,2},{8,12},{10,14},{12,8},{14,10},{16,20},{18,... | collective-permute-start | bytes 786440 | tf_op jit(solution)/shard_map/cond/branch_2_fun/ppermute | solution.py:419
  80.5 15.8 %collective-permute-start.17 = (bf16[1024,128]{1,0:T(8,128)(2,1)}, bf16[1024,128]{1,0:T(8,128)(2,1)}, u32[]{:S(2)}, u32[]{:S(2)}) collective-permute-start(bf16[1024,128]{1,0:T(8,128)(2,1)} %get-tuple-element.56), channel_id=1, source_target_pairs={{0,2},{2,0},{4,6},{6,4},{8,10},{10,8},{12,14},{14,12},{16,18},{18,... | collective-permute-start | bytes 786440 | tf_op jit(solution)/shard_map/cond/branch_2_fun/ppermute | solution.py:419
  101.7 19.0 %collective-permute-start.43 = (f32[128,1024]{1,0:T(8,128)}, f32[128,1024]{1,0:T(8,128)}, u32[]{:S(2)}, u32[]{:S(2)}) collective-permute-start(f32[128,1024]{1,0:T(8,128)} %get-tuple-element.114), channel_id=1, source_target_pairs={{0,24},{2,26},{4,28},{6,30},{8,0},{10,2},{12,4},{14,6},{16,8},{18,... | collective-permute-start | bytes 1572872 | tf_op jit(solution)/shard_map/ppermute | solution.py:419
  104.7 14.0 %collective-permute-start.46 = (bf16[1024,128]{1,0:T(8,128)(2,1)}, bf16[1024,128]{1,0:T(8,128)(2,1)}, u32[]{:S(2)}, u32[]{:S(2)}) collective-permute-start(bf16[1024,128]{1,0:T(8,128)(2,1)} %get-tuple-element.120.x0), channel_id=1, source_target_pairs={{0,6},{2,4},{4,2},{6,0},{8,14},{10,12},{12,10},{14,8},{16,22},{18,... | collective-permute-start | bytes 786440 | tf_op jit(solution)/shard_map/ppermute | solution.py:419
  107.1 12.9 %collective-permute-start.45 = (bf16[1024,128]{1,0:T(8,128)(2,1)}, bf16[1024,128]{1,0:T(8,128)(2,1)}, u32[]{:S(2)}, u32[]{:S(2)}) collective-permute-start(bf16[1024,128]{1,0:T(8,128)(2,1)} %get-tuple-element.120.x0), channel_id=1, source_target_pairs={{0,4},{2,6},{4,0},{6,2},{8,12},{10,14},{12,8},{14,10},{16,20},{18,... | collective-permute-start | bytes 786440 | tf_op jit(solution)/shard_map/ppermute | solution.py:419
  107.7 13.1 %collective-permute-start.44 = (bf16[1024,128]{1,0:T(8,128)(2,1)}, bf16[1024,128]{1,0:T(8,128)(2,1)}, u32[]{:S(2)}, u32[]{:S(2)}) collective-permute-start(bf16[1024,128]{1,0:T(8,128)(2,1)} %get-tuple-element.120.x0), channel_id=1, source_target_pairs={{0,2},{2,0},{4,6},{6,4},{8,10},{10,8},{12,14},{14,12},{16,18},{18,... | collective-permute-start | bytes 786440 | tf_op jit(solution)/shard_map/ppermute | solution.py:419
  108.2 15.1 %all-to-all-start.1 = ((bf16[4,256,128]{2,1,0:T(8,128)(2,1)}), bf16[4,256,128]{2,1,0:T(8,128)(2,1)S(1)}, u32[]{:S(2)}, u32[]{:S(2)}) async-start(bf16[4,256,128]{2,1,0:T(8,128)(2,1)} %bitcast.11), calls=%async_computation.1 | async-start | bytes 524288 | tf_op jit(solution)/shard_map/all_to_all | solution.py:416
  123.3 11.1 %all-to-all-start.2 = ((f32[4,256,128]{2,1,0:T(8,128)}), f32[4,256,128]{2,1,0:T(8,128)S(1)}, u32[]{:S(2)}, u32[]{:S(2)}) async-start(f32[4,256,128]{2,1,0:T(8,128)} %fourth.1), calls=%async_computation.2 | async-start | bytes 1048576 | tf_op jit(solution)/shard_map/all_to_all | solution.py:416
  (10 other events, 17.7 us)
where the time goes:
time: 139 us; the launch traced here: 138 us
  Pallas kernels  51.2 us (37%)
  starting transfers between devices  41.7 us (30%)
  waiting for transfers between devices  30.6 us (22%)
  other arithmetic  9.55 us (7%)
  local copies, waits for them, and re-layouts  3.25 us (2%)
  between operations  1.61 us (1%)
    pallas_call x10, Pallas kernels, call(): pl.pallas_call(kernel, grid_spec=pltpu.PrefetchScalarGridSpec(num_scalar_...  51.2 us
    ppermute x16, starting transfers between devices, permute(): return lax.ppermute(x, 'blk', [(i, to(i)) for i in range(16)])  24.1 us
    ppermute x16, waiting for transfers between devices, permute(): return lax.ppermute(x, 'blk', [(i, to(i)) for i in range(16)])  16.1 us
    ppermute x4, waiting for transfers between devices, send(): lax.ppermute(x, 'blk', [(4 * a + j, 4 * b + j) for a, b in pairs for j in...  13.3 us
    all_to_all x3, starting transfers between devices, exchange(): return lax.all_to_all(x, 'blk', 0, 0, axis_index_groups=groups, tiled=True)  11.4 us
    ppermute x4, starting transfers between devices, send(): lax.ppermute(x, 'blk', [(4 * a + j, 4 * b + j) for a, b in pairs for j in...  5.05 us
    unnamed x26, local copies, waits for them, and re-layouts  3.25 us
    convert_element_type x1, other arithmetic, plane_body(): pair = (after(kept, hi_p) + got.astype(F32)).astype(HF)  3.18 us
  transfers between devices with their start and end apart: 29, of which 9 were waited for; matrix products, arithmetic and copies ran while one was open for 3% of the time, Pallas kernels for 27%

commit v1 on v0

--- a/solution.py
+++ b/solution.py
@@ -78,7 +78,7 @@
     return (fwd_out, back_out)
 
 
-SLOT, OWNS, PANEL, PLANE, CHIP, CORE, KEEP, IS_A, FIRST, LOW = range(10)
+SLOT, OWNS, PANEL, PLANE, CHIP, CORE, KEEP, IS_A = range(8)
 
 
 def scalars(values):
@@ -100,6 +100,9 @@
         compiler_params=pltpu.CompilerParams(vmem_limit_bytes=limit * MIB),
         name=name,
     )(s, *arrays)
+
+
+HBM = pl.BlockSpec(memory_space=pltpu.HBM)
 
 
 def whole(*shape):
@@ -144,60 +147,81 @@
     return 4 * slot + s[PLANE] > s[PANEL] + 1
 
 
-def sums_kernel(own, s, w_ref, b_ref, out_ref, *copies):
-    a = pl.program_id(0)
-    _, span, columns = b_ref.shape
-
-    @pl.when(a == 0)
-    def _():
-        out_ref[...] = jnp.zeros_like(out_ref)
-
-    for copy in copies:
-        copy[...] = b_ref[...]
-
-    @pl.when(later(s, 2 * a + 1))
-    def _():
-        b = b_ref[...].reshape(2 * span, columns) * SUM_SCALE
-        row = lax.broadcasted_iota(jnp.int32, b.shape, 0)
-        b = jnp.where((row >= span) | later(s, 2 * a), b, 0.0)
-        out_ref[...] += mm(b.T.astype(BF), w_ref[0].reshape(2 * span, -1), NN)
+def sums_kernel(own, s, strips, state, out_ref, *rest):
+    copies, (bv, wv, sb, sw, so) = rest[:own], rest[own:]
+    tiles, span, _ = bv.shape
+    which = s[KEEP] if own else 1 - s[KEEP]
+
+    def rows(a):
+        return pltpu.make_async_copy(state.at[a], bv.at[a], sb.at[a])
+
+    def strip(a):
+        return pltpu.make_async_copy(strips.at[which, a], wv.at[a], sw.at[a])
+
+    def back(a):
+        return pltpu.make_async_copy(bv.at[a], copies[0].at[a], so.at[a])
+
+    for a in range(tiles):
+        if own:
+            rows(a).start()
+
+        @pl.when(later(s, a))
+        def _(a=a):
+            if not own:
+                rows(a).start()
+            strip(a).start()
+
+    out_ref[...] = jnp.zeros_like(out_ref)
+    for a in range(tiles):
+        if own:
+            rows(a).wait()
+            back(a).start()
+
+        @pl.when(later(s, a))
+        def _(a=a):
+            if not own:
+                rows(a).wait()
+            strip(a).wait()
+            out_ref[...] += mm((bv[a] * SUM_SCALE).T.astype(BF), wv[a], NN)
 
     if own:
-        @pl.when((a == s[SLOT] // 2) & (s[OWNS] == 1))
+        @pl.when(s[OWNS] == 1)
         def _():
             at = pl.ds(pl.multiple_of(s[CHIP] * span, span), span)
-            out_ref[:, at] = out_ref[:, at] - (b_ref[s[SLOT] % 2] * SUM_SCALE).T
+            out_ref[:, at] = out_ref[:, at] - (bv[s[SLOT]] * SUM_SCALE).T
+
+        for a in range(tiles):
+            back(a).wait()
 
 
 def sums(s, own, strips, back_state):
     tiles, span, columns = back_state.shape
     width = strips.shape[3]
-
-    def which(s):
-        return s[KEEP] if own else 1 - s[KEEP]
-
-    def at(a, s):
-        return jnp.maximum(a, s[FIRST] // 2)
-
-    tile = pl.BlockSpec((2, span, columns), lambda a, s: (a if own else at(a, s), 0, 0))
     return call(
-        functools.partial(sums_kernel, own), "sums", s, (tiles // 2,),
-        [pl.BlockSpec((1, 2, span, width), lambda a, s: (which(s), at(a, s), 0, 0)), tile],
-        [whole(columns, width)] + [tile] * own,
+        functools.partial(sums_kernel, own), "sums", s, (1,),
+        [HBM] * 2,
+        [whole(columns, width)] + [HBM] * own,
         [shaped(F32, columns, width)] + [shaped(F32, *back_state.shape)] * own,
         (strips, back_state),
-    )
-
-
-HBM = pl.BlockSpec(memory_space=pltpu.HBM)
-
-
-def fetch(sems, pairs):
+        scratch=[pltpu.VMEM((tiles, span, columns), F32), pltpu.VMEM((tiles, span, width), BF)]
+        + [pltpu.SemaphoreType.DMA((tiles,))] * 3,
+    )
+
+
+def begin(sems, pairs):
     copies = [pltpu.make_async_copy(a, b, sems.at[i]) for i, (a, b) in enumerate(pairs)]
     for copy in copies:
         copy.start()
+    return copies
+
+
+def finish(copies):
     for copy in copies:
         copy.wait()
+
+
+def fetch(sems, pairs):
+    finish(begin(sems, pairs))
 
 
 def halves(full, d, mine, other, core):
@@ -232,30 +256,35 @@
     pairs = [(own_f(s, f, quarter), fv), (own.at[s[SLOT]], e.at[0])]
     for d, mine, other in ((1, m1, o1), (2, m2, o2), (3, m3, o3)):
         pairs += halves(e, d, mine, other, s[CORE]) + block(hv, d, mine, width)
-    fetch(sems, pairs)
+    copies = begin(sems, pairs)
+    finish(copies[:2])
     x = mm(fv[...].T.astype(BF), e[0], NN)
     for d in (1, 2, 3):
+        finish(copies[4 * d - 2:4 * d + 2])
         x += mm(hv[d].astype(F32).T.astype(BF), e[d], NN)
     hi[...], lo[...] = split(x.T)
 
 
 def second_kernel(
-    s, f, strips, xp, e, m1, m2, m3, n1, n2, n3, o1, o2, o3, lo_a, hi, lo, w, fv, hv, gv, xv, ev, lv, sems
+    s, f, strips, xp, e, m1, m2, m3, n1, n2, n3, o1, o2, o3, lo_a, hi, lo, fv, hv, gv, xv, ev, wv, lv, sems
 ):
     _, quarter = fv.shape
-    width = w.shape[2]
-    pairs = [(own_f(s, f, quarter), fv), (xp, xv), (e, ev), (lo_a, lv), (strips.at[0, s[SLOT]], w.at[0])]
+    width = wv.shape[2]
+    pairs = [(xp, xv), (own_f(s, f, quarter), fv), (strips.at[0, s[SLOT]], wv.at[0]), (e.at[0], ev.at[0])]
     for d, first, mine, other in ((1, m1, n1, o1), (2, m2, n2, o2), (3, m3, n3, o3)):
-        pairs += halves(w, d, mine, other, s[CORE])
-        pairs += block(hv, d, first, width) + block(gv, d, mine, width)
-    fetch(sems, pairs)
+        pairs += halves(wv, d, mine, other, s[CORE])
+        pairs += block(hv, d, first, width) + block(gv, d, mine, width) + [(e.at[d], ev.at[d])]
+    pairs += [(lo_a, lv)]
+    copies = begin(sems, pairs)
     x = jnp.zeros((quarter, width), F32)
     for d in range(4):
+        finish(copies[:4] if d == 0 else copies[7 * d - 3:7 * d + 4])
         old = fv[...] if d == 0 else hv[d].astype(F32) + gv[d].astype(F32)
-        new = old - mm(w[d], xv[...], NN)
+        new = old - mm(wv[d], xv[...], NN)
         x += mm(new.T.astype(BF), ev[d], NN)
     high, low = split(x.T)
     hi[...] = high
+    finish(copies[25:])
 
     @pl.when(s[IS_A] == 1)
     def _():
@@ -266,129 +295,157 @@
         lo[...] = low
 
 
-def third_kernel(s, part, far, e, w, y, r, pv, rv, ev, wv, sems):
-    fetch(sems, [(part, pv), (far, rv), (e, ev), (w, wv)])
+def third_kernel(s, part, far, e, strips, n1, n2, n3, o1, o2, o3, y, r, pv, rv, ev, wv, sems):
+    pairs = [(part, pv), (far, rv), (e.at[0], ev.at[0]), (strips.at[0, s[SLOT]], wv.at[0])]
+    for d, mine, other in ((1, n1, o1), (2, n2, o2), (3, n3, o3)):
+        pairs += halves(wv, d, mine, other, s[CORE]) + [(e.at[d], ev.at[d])]
+    copies = begin(sems, pairs)
+    finish(copies[:2])
     rest = ((pv[...] + rv[...]) * (-1.0 / SUM_SCALE)).T.astype(BF)
     back = jnp.zeros(r.shape, F32)
     for d in range(4):
+        finish(copies[2:4] if d == 0 else copies[3 * d + 1:3 * d + 4])
         yq = mm(ev[d], rest, NN)
-        y[s[CHIP] ^ d] = yq
+        y[d] = yq
         back += mm(yq.T.astype(BF), wv[d], NN)
     r[...] = back
 
 
-def fourth_kernel(s, part, far, r, e, y_b, y, pv, rv, bv, ev, sems):
+def fourth_kernel(s, part, far, r, e, y_b, y0, y1, y2, y3, pv, rv, bv, ev, sems):
+    outs = (y0, y1, y2, y3)
+
     @pl.when(s[IS_A] == 0)
     def _():
-        fetch(sems, [(y_b, y)])
+        fetch(sems, [(y_b.at[d], y) for d, y in enumerate(outs)])
 
     @pl.when(s[IS_A] == 1)
     def _():
-        fetch(sems, [(part, pv), (far, rv), (r, bv), (e, ev)])
+        copies = begin(sems, [(part, pv), (far, rv), (r, bv)] + [(e.at[d], ev.at[d]) for d in range(4)])
+        finish(copies[:3])
         rest = ((pv[...] + rv[...]) * (-1.0 / SUM_SCALE) - bv[...]).T.astype(BF)
-        for d in range(4):
-            y[s[CHIP] ^ d] = mm(ev[d], rest, NN)
-
-
-def fill(x_full, pieces, chip):
-    for d, piece in enumerate(pieces):
-        quarter = piece.shape[1]
-        x_full[:, pl.ds(pl.multiple_of((chip ^ d) * quarter, quarter), quarter)] = piece[...]
-
-
-def subtract(s, a, f_ref, w_ref, x_full, out_ref):
-    _, span, width = w_ref.shape[1:]
-    delta = mm(w_ref[0].reshape(2 * span, width), x_full[...], NN)
-    for j in range(2):
-        rest = f_ref[j] - delta[j * span:(j + 1) * span]
-        out_ref[j] = jnp.where(later(s, 2 * a + j), rest, f_ref[j])
-
-
-def update_one_kernel(s, f_ref, w_ref, x0, x1, x2, x3, out_ref, x_full):
-    a = pl.program_id(0)
-
-    @pl.when(a == 0)
-    def _():
-        fill(x_full, (x0, x1, x2, x3), s[CHIP])
-
-    @pl.when(later(s, 2 * a + 1))
-    def _():
-        subtract(s, a, f_ref, w_ref, x_full, out_ref)
-
-    @pl.when(jnp.logical_not(later(s, 2 * a + 1)))
-    def _():
-        out_ref[...] = f_ref[...]
-
-
-def update_two_kernel(s, f_ref, w_ref, x0, x1, x2, x3, p0, p1, p2, p3, lo_ref, out_ref, x_full):
-    a = pl.program_id(0)
-    span = f_ref.shape[1]
-    quarter = lo_ref.shape[2]
-
-    @pl.when(a == 0)
-    def _():
-        fill(x_full, (x0, x1, x2, x3), s[CHIP])
-
-    @pl.when(later(s, 2 * a + 1))
-    def _():
-        subtract(s, a, f_ref, w_ref, x_full, out_ref)
-
-    @pl.when((a == s[LOW]) & jnp.logical_not(later(s, 2 * a + 1)))
-    def _():
-        out_ref[...] = f_ref[...]
-
-    def solved(pieces):
-        at = pl.ds(pl.multiple_of(s[CHIP] * span, span), span)
-        for d, piece in enumerate(pieces):
-            q = s[CHIP] ^ d
-            x = piece[at, :].astype(F32) + lo_ref[q].astype(F32)
-            out_ref[s[SLOT] % 2, :, pl.ds(pl.multiple_of(q * quarter, quarter), quarter)] = x
-
-    own = (a == s[SLOT] // 2) & (s[OWNS] == 1)
-
-    @pl.when(own & (s[IS_A] == 1))
-    def _():
-        solved((p0, p1, p2, p3))
-
-    @pl.when(own & (s[IS_A] == 0))
-    def _():
-        solved((x0, x1, x2, x3))
-
-
-def update(kernel, which, low, s, state, strips, pieces, own=(), aliases=None):
+        for d, y in enumerate(outs):
+            finish(copies[3 + d:4 + d])
+            y[...] = mm(ev[d], rest, NN)
+
+
+def gathered(s, x_full, pieces):
+    quarter = pieces[0].shape[1]
+    return [
+        (x, x_full.at[:, pl.ds(pl.multiple_of((s[CHIP] ^ d) * quarter, quarter), quarter)])
+        for d, x in enumerate(pieces)
+    ]
+
+
+def update_one_kernel(s, f, strips, x0, x1, x2, x3, out, fv, wv, xv, sf, sw, so, sx):
+    tiles = fv.shape[0]
+
+    def state(a):
+        return pltpu.make_async_copy(f.at[a], fv.at[a], sf.at[a])
+
+    def strip(a):
+        return pltpu.make_async_copy(strips.at[0, a], wv.at[a], sw.at[a])
+
+    def back(a):
+        return pltpu.make_async_copy(fv.at[a], out.at[a], so.at[a])
+
+    x = begin(sx, gathered(s, xv, (x0, x1, x2, x3)))
+    for a in range(tiles):
+        state(a).start()
+        pl.when(later(s, a))(strip(a).start)
+    finish(x)
+    for a in range(tiles):
+        state(a).wait()
+
+        @pl.when(later(s, a))
+        def _(a=a):
+            strip(a).wait()
+            fv[a] = fv[a] - mm(wv[a], xv[...], NN)
+
+        back(a).start()
+    for a in range(tiles):
+        back(a).wait()
+
+
+def update_two_kernel(
+    s, f, strips, x0, x1, x2, x3, p0, p1, p2, p3, lo, out, fv, wv, xv, sf, sw, so, sx, pv, lv, sp
+):
+    tiles, span, columns = fv.shape
+    quarter = columns // 4
+    rows = pl.ds(pl.multiple_of(s[CHIP] * span, span), span)
+
+    def state(a):
+        return pltpu.make_async_copy(f.at[a], fv.at[a], sf.at[a])
+
+    def strip(a):
+        return pltpu.make_async_copy(strips.at[1, a], wv.at[a], sw.at[a])
+
+    def back(a):
+        return pltpu.make_async_copy(fv.at[a], out.at[a], so.at[a])
+
+    x = begin(sx, gathered(s, xv, (x0, x1, x2, x3)))
+    for a in range(tiles):
+        @pl.when(later(s, a))
+        def _(a=a):
+            state(a).start()
+            strip(a).start()
+
+    own = begin(sp, gathered(s, pv, [p.at[rows, :] for p in (p0, p1, p2, p3)]) + [(lo, lv)])
+    finish(x)
+    for a in range(tiles):
+        @pl.when(later(s, a))
+        def _(a=a):
+            state(a).wait()
+            strip(a).wait()
+            fv[a] = fv[a] - mm(wv[a], xv[...], NN)
+            back(a).start()
+
+    finish(own)
+    for a in range(tiles):
+        @pl.when((s[SLOT] == a) & (s[OWNS] == 1))
+        def _(a=a):
+            solved = jnp.where(s[IS_A] == 1, pv[...].astype(F32), xv[rows, :].astype(F32))
+            for q in range(4):
+                at = slice(q * quarter, (q + 1) * quarter)
+                fv[a, :, at] = solved[:, at] + lv[q].astype(F32)
+            back(a).start()
+            back(a).wait()
+
+        @pl.when(later(s, a))
+        def _(a=a):
+            back(a).wait()
+
+
+def update(kernel, s, state, strips, pieces, own=(), aliases=None):
     tiles, span, columns = state.shape
     width = strips.shape[3]
-    tile = pl.BlockSpec((2, span, columns), lambda a, s: (jnp.maximum(a, low(s)), 0, 0))
+    dma = pltpu.SemaphoreType.DMA
+    more = []
+    if own:
+        more = [pltpu.VMEM((span, columns), BF), pltpu.VMEM(own[-1].shape, BF), dma((5,))]
     return call(
-        kernel, "update", s, (tiles // 2,),
-        [tile, pl.BlockSpec((1, 2, span, width), lambda a, s: (which, jnp.maximum(a, s[FIRST] // 2), 0, 0))]
-        + [whole(*x.shape) for x in (*pieces, *own)],
-        tile, shaped(F32, *state.shape),
+        kernel, "update", s, (1,), [HBM] * (2 + len(pieces) + len(own)), HBM, shaped(F32, *state.shape),
         (state, strips, *pieces, *own),
-        scratch=[pltpu.VMEM((width, columns), BF)],
+        scratch=[
+            pltpu.VMEM(state.shape, F32), pltpu.VMEM(strips.shape[1:], BF), pltpu.VMEM((width, columns), BF),
+            dma((tiles,)), dma((tiles,)), dma((tiles,)), dma((4,)),
+        ] + more,
         aliases=aliases,
     )
 
 
-def place_kernel(s, copy_ref, y_ref, out_ref):
-    quarter = y_ref.shape[2]
-
+def place_kernel(s, copy, y0, y1, y2, y3, out, tile, sems):
     @pl.when(s[OWNS] == 1)
     def _():
-        for q in range(4):
-            out_ref[0, :, q * quarter:(q + 1) * quarter] = y_ref[q]
-
-    @pl.when(s[OWNS] == 0)
-    def _():
-        out_ref[...] = copy_ref[...]
-
-
-def place(s, copy, y):
-    tiles, span, columns = copy.shape
-    tile = pl.BlockSpec((1, span, columns), lambda i, s: (s[SLOT], 0, 0))
+        fetch(sems, gathered(s, tile, (y0, y1, y2, y3)))
+        fetch(sems, [(tile, out.at[s[SLOT]])])
+
+
+def place(s, copy, pieces):
+    _, span, columns = copy.shape
     return call(
-        place_kernel, "place", s, (1,), [tile, whole(*y.shape)], tile,
-        shaped(F32, *copy.shape), (copy, y), aliases={1: 0},
+        place_kernel, "place", s, (1,), [HBM] * 5, HBM, shaped(F32, *copy.shape), (copy, *pieces),
+        scratch=[pltpu.VMEM((span, columns), F32), pltpu.SemaphoreType.DMA((4,))],
+        aliases={1: 0}, limit=8,
     )
 
 
@@ -437,10 +494,8 @@
         return lax.ppermute(x, "rhs", [(0, 1), (1, 0)])
 
     slot = start // 4 + jnp.where(is_b & (home == 3), 1, 0)
-    first_later = jnp.clip((start + 5 - plane) // 4, 0, tiles - 1)
-    low = jnp.minimum(first_later, jnp.where(is_a | is_b, slot, tiles - 1)) // 2
     keep = lax.rem(plane + start + 1, 2) == 0
-    s = scalars([slot, is_a | is_b, start, plane, chip, core, keep, is_a, first_later, low])
+    s = scalars([slot, is_a | is_b, start, plane, chip, core, keep, is_a])
 
     piece = shaped(BF, width, quarter)
     piece32 = shaped(F32, quarter, width)
@@ -449,10 +504,11 @@
     blocks16 = shaped(BF, 4, span, quarter)
     own = shaped(F32, span, quarter)
 
-    def small(kernel, name, shapes, arrays, buffers, copies):
+    def small(kernel, name, shapes, arrays, buffers, copies, limit=63):
         return call(
             kernel, name, s, (1,), [HBM] * len(arrays), [whole(*x.shape) for x in shapes], shapes, arrays,
             scratch=[pltpu.VMEM(x.shape, x.dtype) for x in buffers] + [pltpu.SemaphoreType.DMA((copies,))],
+            limit=limit,
         )
 
     (sent,) = sums(s, 0, strips, back_state)
@@ -476,9 +532,9 @@
     xp = jnp.where(is_a, hi_p, below)
     xp_far = across(xp)
     n_other = [swap(x) for x in n]
-    hi_q, lo, w = small(
-        second_kernel, "second", [piece, piece, matrix],
-        (fwd_state, strips, xp, e, *m, *n, *n_other, lo_p), [own, blocks16, blocks16, piece, matrix, piece], 23,
+    hi_q, lo = small(
+        second_kernel, "second", [piece, piece], (fwd_state, strips, xp, e, *m, *n, *n_other, lo_p),
+        [own, blocks16, blocks16, piece, matrix, matrix, piece], 26,
     )
     part = jnp.sum(parts.astype(F32), axis=0)
     part16 = part.astype(HF)
@@ -502,21 +558,19 @@
     xq_all = [xq] + gather(xq)
 
     y_b, r = small(
-        third_kernel, "third", [blocks, piece32], (part, far, e, w),
-        [piece32, piece32, matrix, matrix], 4,
+        third_kernel, "third", [blocks, piece32], (part, far, e, strips, *n, *n_other),
+        [piece32, piece32, matrix, matrix], 13,
     )
     r = down(r)
     lo_own = exchange(after(lo, y_b)).reshape(4, span, quarter)
-    state = update(update_one_kernel, 0, lambda s: 0, after(s, y_b), fwd_state, strips, xp_all)
-    (y,) = small(
-        fourth_kernel, "fourth", [blocks], (part, far, r, e, after(y_b, state, *xq_all)),
-        [piece32, piece32, piece32, matrix], 4,
-    )
-    y_own = exchange(y.reshape(4 * span, quarter)).reshape(4, span, quarter)
-    fwd_out = update(
-        update_two_kernel, 1, lambda s: s[LOW], after(s, y), state, strips, xq_all, (*xp_all, lo_own), {1: 0}
-    )
-    back_out = place(s, copy, y_own)
+    state = update(update_one_kernel, after(s, y_b), fwd_state, strips, xp_all)
+    y = small(
+        fourth_kernel, "fourth", [own] * 4, (part, far, r, e, after(y_b, state, *xq_all)),
+        [piece32, piece32, piece32, matrix], 7,
+    )
+    y = [y[0]] + deal(y[1:])
+    fwd_out = update(update_two_kernel, after(s, y[0]), state, strips, xq_all, (*xp_all, lo_own), {1: 0})
+    back_out = place(s, copy, y)
     return fwd_out, back_out
 
 
@@ -530,7 +584,6 @@
         and width == 4 * span
         and span % 256 == 0
         and columns % 512 == 0
-        and tiles % 2 == 0
     )
     chosen = plane_body if regular else plain_body
     return chosen(panel, strips, dinv_rows, fwd_state, back_state)

time: 139 us -> 137 us (0.986)
  Pallas kernels: 51.2 us -> 40.1 us
  waiting for transfers between devices: 30.6 us -> 37.7 us
    ppermute x16 -> x19, waiting for transfers between devices: 16.1 us -> 29 us  [permute(): return lax.ppermute(x, 'blk', [(i, to(i)) for i in range(16)])]
    pallas_call x10, Pallas kernels: 51.2 us -> 40.1 us  [call(): pl.pallas_call(kernel, grid_spec=pltpu.PrefetchScalarGridSpec(num_scalar_...]
    ppermute x16 -> x19, starting transfers between devices: 24.1 us -> 29.5 us  [permute(): return lax.ppermute(x, 'blk', [(i, to(i)) for i in range(16)])]
    ppermute x4, waiting for transfers between devices: 13.3 us -> 8.39 us  [send(): lax.ppermute(x, 'blk', [(4 * a + j, 4 * b + j) for a, b in pairs for j in...]
    all_to_all x3 -> x2, starting transfers between devices: 11.4 us -> 7.65 us  [exchange(): return lax.all_to_all(x, 'blk', 0, 0, axis_index_groups=groups, tiled=True)]
  transfers between devices with their start and end apart: 29 -> 31, of which waited for: 9 -> 10; matrix products, arithmetic and copies ran while one was open for 3% -> 4% of each run, Pallas kernels for 27% -> 22%
where the time goes in v1:
time: 137 us; the launch traced here: 135 us
  starting transfers between devices  42.2 us (31%)
  Pallas kernels  40.1 us (29%)
  waiting for transfers between devices  37.7 us (28%)
  other arithmetic  10.6 us (8%)
  local copies, waits for them, and re-layouts  3.12 us (2%)
  between operations  1.76 us (1%)
    pallas_call x10, Pallas kernels, call(): pl.pallas_call(kernel, grid_spec=pltpu.PrefetchScalarGridSpec(num_scalar_...  40.1 us
    ppermute x19, starting transfers between devices, permute(): return lax.ppermute(x, 'blk', [(i, to(i)) for i in range(16)])  29.5 us
    ppermute x19, waiting for transfers between devices, permute(): return lax.ppermute(x, 'blk', [(i, to(i)) for i in range(16)])  29 us
    ppermute x4, waiting for transfers between devices, send(): lax.ppermute(x, 'blk', [(4 * a + j, 4 * b + j) for a, b in pairs for j in...  8.39 us
    all_to_all x2, starting transfers between devices, exchange(): return lax.all_to_all(x, 'blk', 0, 0, axis_index_groups=groups, tiled=True)  7.65 us
    ppermute x4, starting transfers between devices, send(): lax.ppermute(x, 'blk', [(4 * a + j, 4 * b + j) for a, b in pairs for j in...  3.93 us
    convert_element_type x1, other arithmetic, plane_body(): pair = (after(kept, hi_p) + got.astype(F32)).astype(HF)  3.17 us
    unnamed x26, local copies, waits for them, and re-layouts  3.12 us
  transfers between devices with their start and end apart: 31, of which 10 were waited for; matrix products, arithmetic and copies ran while one was open for 4% of the time, Pallas kernels for 22%

profile of v1, /device:TPU:0, one launch (start us, length us, event | category | flops | bytes accessed | tf_op | source)
XLA Modules:
  0.0 135.5 jit_solution(12667736787968529760)
XLA Ops:
  1.9 3.8 %sums.2 = f32[512,1024]{1,0:T(8,128)} custom-call(s32[16]{0:T(128)} %compare_select_fusion.7.s, bf16[2,6,256,1024]{3,2,1,0:T(8,128)(2,1)} %strips.11, f32[6,256,512]{2,1,0:T(8,128)} %state.3), custom_call_target="tpu_custom_call" | custom-call | tf_op jit(solution)/shard_map/sums/pallas_call | solution.py:93
  5.7 2.7 %convert_element_type.49 = f16[512,1024]{1,0:T(8,128)(2,1)} convert(f32[512,1024]{1,0:T(8,128)} %sums.2) | non-fusion elementwise | flops 524288 | bytes 3145728 | tf_op jit(solution)/shard_map/convert_element_type | solution.py:515
  8.5 3.0 %collective-permute-start.34 = (f16[512,1024]{1,0:T(8,128)(2,1)}, f16[512,1024]{1,0:T(8,128)(2,1)}, u32[]{:S(2)}, u32[]{:S(2)}) collective-permute-start(f16[512,1024]{1,0:T(8,128)(2,1)} %convert_element_type.49), channel_id=1, source_target_pairs={{0,8},{2,10},{4,12},{6,14},{8,0},{10,2},{12,4},{14,6},{16,24},{18,... | collective-permute-start | bytes 3145736 | tf_op jit(solution)/shard_map/ppermute | solution.py:476
  11.5 3.2 %prep.1 = (bf16[128,1280]{1,0:T(8,128)(2,1)}, bf16[128,1280]{1,0:T(8,128)(2,1)}, bf16[128,1280]{1,0:T(8,128)(2,1)}, bf16[128,1280]{1,0:T(8,128)(2,1)}, bf16[128,...) custom-call(s32[16]{0:T(128)} %compare_select_fusion.7.s, bf16[6,256,1024]{2,1,0:T(8,128)(2,1)} %own.1, ...), custom_call_target="tpu_custom_call" | custom-call | tf_op jit(solution)/shard_map/prep/pallas_call | solution.py:93
  14.7 1.5 %collective-permute-start.28 = (bf16[128,1280]{1,0:T(8,128)(2,1)}, bf16[128,1280]{1,0:T(8,128)(2,1)S(1)}, u32[]{:S(2)}, u32[]{:S(2)}) collective-permute-start(bf16[128,1280]{1,0:T(8,128)(2,1)} %get-tuple-element.99), channel_id=1, source_target_pairs={{0,2},{2,0},{4,6},{6,4},{8,10},{10,8},{12,14},{14,12},{16,18},{18,... | collective-permute-start | bytes 983048 | tf_op jit(solution)/shard_map/ppermute | solution.py:476
  16.2 1.5 %collective-permute-start.29 = (bf16[128,1280]{1,0:T(8,128)(2,1)}, bf16[128,1280]{1,0:T(8,128)(2,1)}, u32[]{:S(2)}, u32[]{:S(2)}) collective-permute-start(bf16[128,1280]{1,0:T(8,128)(2,1)} %get-tuple-element.100), channel_id=1, source_target_pairs={{0,4},{2,6},{4,0},{6,2},{8,12},{10,14},{12,8},{14,10},{16,20},{18,... | collective-permute-start | bytes 983048 | tf_op jit(solution)/shard_map/ppermute | solution.py:476
  18.2 5.0 %sums.3 = (f32[512,1024]{1,0:T(8,128)}, f32[6,256,512]{2,1,0:T(8,128)}) custom-call(s32[16]{0:T(128)} %compare_select_fusion.7.s, bf16[2,6,256,1024]{3,2,1,0:T(8,128)(2,1)} %strips.11, f32[6,256,512]{2,1,0:T(8,128)} %state.3), custom_call_target="tpu_custom_call" | custom-call | tf_op jit(solution)/shard_map/sums/pallas_call | solution.py:93
  23.2 2.4 %collective-permute-done.28.m1 = bf16[128,1280]{1,0:T(8,128)(2,1)S(1)} collective-permute-done((bf16[128,1280]{1,0:T(8,128)(2,1)}, bf16[128,1280]{1,0:T(8,128)(2,1)S(1)}, u32[]{:S(2)}, u32[]{:S(2)}) %collective-permute-start.28) | collective-permute-done | bytes 327712 | tf_op jit(solution)/shard_map/ppermute | solution.py:476
  25.6 6.9 %collective-permute-done.29.m2 = bf16[128,1280]{1,0:T(8,128)(2,1)} collective-permute-done((bf16[128,1280]{1,0:T(8,128)(2,1)}, bf16[128,1280]{1,0:T(8,128)(2,1)}, u32[]{:S(2)}, u32[]{:S(2)}) %collective-permute-start.29) | collective-permute-done | bytes 327712 | tf_op jit(solution)/shard_map/ppermute | solution.py:476
  35.2 1.5 %collective-permute-start.37 = (bf16[128,1280]{1,0:T(8,128)(2,1)}, bf16[128,1280]{1,0:T(8,128)(2,1)S(1)}, u32[]{:S(2)}, u32[]{:S(2)}) collective-permute-start(bf16[128,1280]{1,0:T(8,128)(2,1)} %get-tuple-element.111), channel_id=1, source_target_pairs={{0,4},{2,6},{4,0},{6,2},{8,12},{10,14},{12,8},{14,10},{16,20},{18,... | collective-permute-start | bytes 983048 | tf_op jit(solution)/shard_map/ppermute | solution.py:476
  37.9 4.4 %first.1 = (bf16[1024,128]{1,0:T(8,128)(2,1)}, bf16[1024,128]{1,0:T(8,128)(2,1)}, bf16[4,256,1024]{2,1,0:T(8,128)(2,1)}) custom-call(s32[16]{0:T(128)} %compare_select_fusion.7.s, f32[6,256,512]{2,1,0:T(8,128)} %f.5, bf16[6,256,1024]{2,1,0:T(8,128)(2,1)} %own.1, bf16[128,1280]{1,0:T(8,128)(2,1)} %copy-done.9, bf16[128,1280]{1,0:T(8,128)(2,1)} %collective-permute-done.29.m2, ...), custom_call_target="tpu_custom_call" | custom-call | tf_op jit(solution)/shard_map/first/pallas_call | solution.py:93
  42.8 3.2 %add_convert_fusion = f16[512,1024]{1,0:T(8,128)(2,1)} fusion(f32[512,1024]{1,0:T(8,128)} %get-tuple-element.108, f16[512,1024]{1,0:T(8,128)(2,1)} %collective-permute-done.34), kind=kLoop, calls=%fused_computation.5 | loop fusion | flops 1572864 | bytes 4194304 | tf_op jit(solution)/shard_map/convert_element_type | solution.py:529
  46.0 4.3 %all-to-all-start = ((f16[4,128,1024]{2,1,0:T(8,128)(2,1)}), f16[4,128,1024]{2,1,0:T(8,128)(2,1)}, u32[]{:S(2)}, u32[]{:S(2)}) async-start(f16[4,128,1024]{2,1,0:T(8,128)(2,1)} %bitcast.1), calls=%async_computation | async-start | bytes 2097152 | tf_op jit(solution)/shard_map/all_to_all | solution.py:473
  50.4 5.9 %collective-permute-done.37.n2 = bf16[128,1280]{1,0:T(8,128)(2,1)S(1)} collective-permute-done((bf16[128,1280]{1,0:T(8,128)(2,1)}, bf16[128,1280]{1,0:T(8,128)(2,1)S(1)}, u32[]{:S(2)}, u32[]{:S(2)}) %collective-permute-start.37) | collective-permute-done | bytes 327712 | tf_op jit(solution)/shard_map/ppermute | solution.py:476
  56.9 3.1 %collective-permute-start.42 = (bf16[1024,128]{1,0:T(8,128)(2,1)S(1)}, bf16[1024,128]{1,0:T(8,128)(2,1)}, u32[]{:S(2)}, u32[]{:S(2)}) collective-permute-start(bf16[1024,128]{1,0:T(8,128)(2,1)S(1)} %broadcast_select_fusion.1.xp), channel_id=1, source_target_pairs={{0,16},{2,18},{4,20},{6,22},{8,24},{10,26},{12,28},{14,30},{16,0},... | collective-permute-start | bytes 786440 | tf_op jit(solution)/shard_map/ppermute | solution.py:476
  61.0 5.0 %second.1 = (bf16[1024,128]{1,0:T(8,128)(2,1)S(1)}, bf16[1024,128]{1,0:T(8,128)(2,1)}) custom-call(s32[16]{0:T(128)} %compare_select_fusion.7.s, f32[6,256,512]{2,1,0:T(8,128)} %f.5, bf16[2,6,256,1024]{3,2,1,0:T(8,128)(2,1)} %strips.11, bf16[1024,128]{1,0:T(8,128)(2,1)} %copy-done.3, bf16[4,256,1024]{2,1,0:T(8,128)(2,1)} %get-tuple-element.109.e, ...), custom_call_target="tpu_custom_call" | custom-call | tf_op jit(solution)/shard_map/second/pallas_call | solution.py:93
  66.0 3.0 %collective-permute-done.42 = bf16[1024,128]{1,0:T(8,128)(2,1)} collective-permute-done((bf16[1024,128]{1,0:T(8,128)(2,1)S(1)}, bf16[1024,128]{1,0:T(8,128)(2,1)}, u32[]{:S(2)}, u32[]{:S(2)}) %collective-permute-start.42) | collective-permute-done | bytes 262176 | tf_op jit(solution)/shard_map/ppermute | solution.py:476
  69.0 1.7 %broadcast_select_fusion.x0.p0 = bf16[1024,128]{1,0:T(8,128)(2,1)} fusion(bf16[1024,128]{1,0:T(8,128)(2,1)} %copy-done.3, bf16[1024,128]{1,0:T(8,128)(2,1)} %collective-permute-done.42, pred[]{:T(512)S(6)} %or.4), kind=kLoop, calls=%fused_computation.6 | loop fusion | flops 131072 | bytes 786433 | tf_op jit(solution)/shard_map/jit(_where)/select_n | solution.py:555
  70.7 1.5 %convert_reduce_fusion.part = f32[128,1024]{1,0:T(8,128)S(1)} fusion(f16[4,128,1024]{2,1,0:T(8,128)(2,1)} %all-to-all-done), kind=kLoop, calls=%fused_computation.4 | loop fusion | flops 917504 | bytes 1572864 | tf_op jit(solution)/shard_map/reduce_sum | solution.py:539
  73.0 28.8 %conditional.4 = (bf16[1024,128]{1,0:T(8,128)(2,1)}, bf16[1024,128]{1,0:T(8,128)(2,1)}, bf16[1024,128]{1,0:T(8,128)(2,1)}, bf16[1024,128]{1,0:T(8,128)(2,1)}, f32[128,1024]{1,0:T(8,128)S(1)}) conditional(s32[]{:T(128)} %clamp.3, (pred[]{:T(512)}, bf16[1024,128]{1,0:T(8,128)(2,1)S(1)}, bf16[1024,128]{1,0:T(8,128)(2,1)}, ...), branch_computations={%region_1.2_spmd, %region_2.3_spmd, %region_3.4_spmd, %region_4.5_... | conditional | flops 524288 | bytes 9437505
  77.7 8.4 %collective-permute-done.6 = f16[128,1024]{1,0:T(8,128)(2,1)S(1)} collective-permute-done((f16[128,1024]{1,0:T(8,128)(2,1)S(1)}, f16[128,1024]{1,0:T(8,128)(2,1)S(1)}, u32[]{:S(2)}, u32[]{:S(2)}) %collective-permute-start.6) | collective-permute-done | bytes 262176 | tf_op jit(solution)/shard_map/cond/branch_0_fun/ppermute | solution.py:546
  86.1 7.4 %collective-permute-start.4 = (bf16[1024,128]{1,0:T(8,128)(2,1)}, bf16[1024,128]{1,0:T(8,128)(2,1)}, u32[]{:S(2)}, u32[]{:S(2)}) collective-permute-start(bf16[1024,128]{1,0:T(8,128)(2,1)} %get-tuple-element.48), channel_id=1, source_target_pairs={{0,4},{2,6},{4,0},{6,2},{8,12},{10,14},{12,8},{14,10},{16,20},{18,... | collective-permute-start | bytes 786440 | tf_op jit(solution)/shard_map/cond/branch_0_fun/ppermute | solution.py:476
  94.5 5.9 %collective-permute-done.4 = bf16[1024,128]{1,0:T(8,128)(2,1)} collective-permute-done((bf16[1024,128]{1,0:T(8,128)(2,1)}, bf16[1024,128]{1,0:T(8,128)(2,1)}, u32[]{:S(2)}, u32[]{:S(2)}) %collective-permute-start.4) | collective-permute-done | bytes 262176 | tf_op jit(solution)/shard_map/cond/branch_0_fun/ppermute | solution.py:476
  101.8 4.8 %third.1 = (f32[4,256,128]{2,1,0:T(8,128)}, f32[128,1024]{1,0:T(8,128)}) custom-call(s32[16]{0:T(128)} %compare_select_fusion.7.s, f32[128,1024]{1,0:T(8,128)} %copy-done.2, f32[128,1024]{1,0:T(8,128)S(1)} %get-tuple-element.138.far, bf16[4,256,1024]{2,1,0:T(8,128)(2,1)} %get-tuple-element.109.e, bf16[2,6,256,1024]{3,2,1,0:T(8,128)(2,1)} %strips.11, ...), custom_call_target="tpu_custom_call" | custom-call | tf_op jit(solution)/shard_map/third/pallas_call | solution.py:93
  106.7 1.7 %collective-permute-start.45 = (bf16[1024,128]{1,0:T(8,128)(2,1)}, bf16[1024,128]{1,0:T(8,128)(2,1)}, u32[]{:S(2)}, u32[]{:S(2)}) collective-permute-start(bf16[1024,128]{1,0:T(8,128)(2,1)} %get-tuple-element.122.x0), channel_id=1, source_target_pairs={{0,4},{2,6},{4,0},{6,2},{8,12},{10,14},{12,8},{14,10},{16,20},{18,... | collective-permute-start | bytes 786440 | tf_op jit(solution)/shard_map/ppermute | solution.py:476
  108.4 1.7 %collective-permute-start.44 = (bf16[1024,128]{1,0:T(8,128)(2,1)}, bf16[1024,128]{1,0:T(8,128)(2,1)}, u32[]{:S(2)}, u32[]{:S(2)}) collective-permute-start(bf16[1024,128]{1,0:T(8,128)(2,1)} %get-tuple-element.122.x0), channel_id=1, source_target_pairs={{0,2},{2,0},{4,6},{6,4},{8,10},{10,8},{12,14},{14,12},{16,18},{18,... | collective-permute-start | bytes 786440 | tf_op jit(solution)/shard_map/ppermute | solution.py:476
  110.2 3.4 %all-to-all-start.1 = ((bf16[4,256,128]{2,1,0:T(8,128)(2,1)}), bf16[4,256,128]{2,1,0:T(8,128)(2,1)S(1)}, u32[]{:S(2)}, u32[]{:S(2)}) async-start(bf16[4,256,128]{2,1,0:T(8,128)(2,1)} %bitcast.10), calls=%async_computation.1 | async-start | bytes 524288 | tf_op jit(solution)/shard_map/all_to_all | solution.py:473
  113.6 4.5 %update.2.f = f32[6,256,512]{2,1,0:T(8,128)} custom-call(s32[16]{0:T(128)} %compare_select_fusion.7.s, f32[6,256,512]{2,1,0:T(8,128)} %f.5, bf16[2,6,256,1024]{3,2,1,0:T(8,128)(2,1)} %strips.11, bf16[1024,128]{1,0:T(8,128)(2,1)} %broadcast_select_fusion.x0.p0, bf16[1024,128]{1,0:T(8,128)(2,1)} %get-tuple-element.119.x1.p1, ...), custom_call_target="tpu_custom_call" | custom-call | tf_op jit(solution)/shard_map/update/pallas_call | solution.py:93
  118.1 3.3 %collective-permute-done.45.x2 = bf16[1024,128]{1,0:T(8,128)(2,1)} collective-permute-done((bf16[1024,128]{1,0:T(8,128)(2,1)}, bf16[1024,128]{1,0:T(8,128)(2,1)}, u32[]{:S(2)}, u32[]{:S(2)}) %collective-permute-start.45) | collective-permute-done | bytes 262176 | tf_op jit(solution)/shard_map/ppermute | solution.py:476
  121.4 4.1 %fourth.1 = (f32[256,128]{1,0:T(8,128)}, f32[256,128]{1,0:T(8,128)}, f32[256,128]{1,0:T(8,128)}, f32[256,128]{1,0:T(8,128)}) custom-call(s32[16]{0:T(128)} %compare_select_fusion.7.s, f32[128,1024]{1,0:T(8,128)} %copy-done.2, f32[128,1024]{1,0:T(8,128)S(1)} %get-tuple-element.138.far, f32[128,1024]{1,0:T(8,128)} %collective-permute-done.43.r, ...), custom_call_target="tpu_custom_call" | custom-call | tf_op jit(solution)/shard_map/fourth/pallas_call | solution.py:93
  127.3 1.7 %collective-permute-start.49 = (f32[256,128]{1,0:T(8,128)}, f32[256,128]{1,0:T(8,128)S(1)}, u32[]{:S(2)}, u32[]{:S(2)}) collective-permute-start(f32[256,128]{1,0:T(8,128)} %get-tuple-element.131), channel_id=1, source_target_pairs={{0,6},{2,4},{4,2},{6,0},{8,14},{10,12},{12,10},{14,8},{16,22},{18,... | collective-permute-start | bytes 393224 | tf_op jit(solution)/shard_map/ppermute | solution.py:476
  129.7 3.9 %update.3 = f32[6,256,512]{2,1,0:T(8,128)} custom-call(s32[16]{0:T(128)} %compare_select_fusion.7.s, f32[6,256,512]{2,1,0:T(8,128)} %update.2.f, bf16[2,6,256,1024]{3,2,1,0:T(8,128)(2,1)} %strips.11, bf16[1024,128]{1,0:T(8,128)(2,1)} %get-tuple-element.122.x0, bf16[1024,128]{1,0:T(8,128)(2,1)} %collective-permute-done.44.x1, ...), custom_call_target="tpu_custom_call", output_to_operand_aliasing={{}: (1, {})} | custom-call | tf_op jit(solution)/shard_map/update/pallas_call | solution.py:93
  (76 shorter events, 19.2 us)
Async XLA Ops:
  8.5 34.4 %collective-permute-start.34 = (f16[512,1024]{1,0:T(8,128)(2,1)}, f16[512,1024]{1,0:T(8,128)(2,1)}, u32[]{:S(2)}, u32[]{:S(2)}) collective-permute-start(f16[512,1024]{1,0:T(8,128)(2,1)} %convert_element_type.49), channel_id=1, source_target_pairs={{0,8},{2,10},{4,12},{6,14},{8,0},{10,2},{12,4},{14,6},{16,24},{18,... | collective-permute-start | bytes 3145736 | tf_op jit(solution)/shard_map/ppermute | solution.py:476
  14.7 10.9 %collective-permute-start.28 = (bf16[128,1280]{1,0:T(8,128)(2,1)}, bf16[128,1280]{1,0:T(8,128)(2,1)S(1)}, u32[]{:S(2)}, u32[]{:S(2)}) collective-permute-start(bf16[128,1280]{1,0:T(8,128)(2,1)} %get-tuple-element.99), channel_id=1, source_target_pairs={{0,2},{2,0},{4,6},{6,4},{8,10},{10,8},{12,14},{14,12},{16,18},{18,... | collective-permute-start | bytes 983048 | tf_op jit(solution)/shard_map/ppermute | solution.py:476
  16.2 16.2 %collective-permute-start.29 = (bf16[128,1280]{1,0:T(8,128)(2,1)}, bf16[128,1280]{1,0:T(8,128)(2,1)}, u32[]{:S(2)}, u32[]{:S(2)}) collective-permute-start(bf16[128,1280]{1,0:T(8,128)(2,1)} %get-tuple-element.100), channel_id=1, source_target_pairs={{0,4},{2,6},{4,0},{6,2},{8,12},{10,14},{12,8},{14,10},{16,20},{18,... | collective-permute-start | bytes 983048 | tf_op jit(solution)/shard_map/ppermute | solution.py:476
  17.7 14.7 %collective-permute-start.30 = (bf16[128,1280]{1,0:T(8,128)(2,1)}, bf16[128,1280]{1,0:T(8,128)(2,1)}, u32[]{:S(2)}, u32[]{:S(2)}) collective-permute-start(bf16[128,1280]{1,0:T(8,128)(2,1)} %get-tuple-element.101), channel_id=1, source_target_pairs={{0,6},{2,4},{4,2},{6,0},{8,14},{10,12},{12,10},{14,8},{16,22},{18,... | collective-permute-start | bytes 983048 | tf_op jit(solution)/shard_map/ppermute | solution.py:476
  32.4 2.1 %collective-permute-start.31 = (bf16[128,1280]{1,0:T(8,128)(2,1)S(1)}, bf16[128,1280]{1,0:T(8,128)(2,1)S(1)}, u32[]{:S(2)}, u32[]{:S(2)}) collective-permute-start(bf16[128,1280]{1,0:T(8,128)(2,1)S(1)} %collective-permute-done.28.m1), channel_id=1, source_target_pairs={{0,1},{1,0},{2,3},{3,2},{4,5},{5,4},{6,7},{7,6},{8,9},{9,8},{10,11... | collective-permute-start | bytes 983048 | tf_op jit(solution)/shard_map/ppermute | solution.py:494
  32.4 4.3 %collective-permute-start.32 = (bf16[128,1280]{1,0:T(8,128)(2,1)}, bf16[128,1280]{1,0:T(8,128)(2,1)}, u32[]{:S(2)}, u32[]{:S(2)}) collective-permute-start(bf16[128,1280]{1,0:T(8,128)(2,1)} %collective-permute-done.29.m2), channel_id=1, source_target_pairs={{0,1},{1,0},{2,3},{3,2},{4,5},{5,4},{6,7},{7,6},{8,9},{9,8},{10,11... | collective-permute-start | bytes 983048 | tf_op jit(solution)/shard_map/ppermute | solution.py:494
  32.9 5.0 %collective-permute-start.33 = (bf16[128,1280]{1,0:T(8,128)(2,1)}, bf16[128,1280]{1,0:T(8,128)(2,1)}, u32[]{:S(2)}, u32[]{:S(2)}) collective-permute-start(bf16[128,1280]{1,0:T(8,128)(2,1)} %collective-permute-done.30.m3), channel_id=1, source_target_pairs={{0,1},{1,0},{2,3},{3,2},{4,5},{5,4},{6,7},{7,6},{8,9},{9,8},{10,11... | collective-permute-start | bytes 983048 | tf_op jit(solution)/shard_map/ppermute | solution.py:494
  32.9 17.3 %collective-permute-start.36 = (bf16[128,1280]{1,0:T(8,128)(2,1)}, bf16[128,1280]{1,0:T(8,128)(2,1)S(1)}, u32[]{:S(2)}, u32[]{:S(2)}) collective-permute-start(bf16[128,1280]{1,0:T(8,128)(2,1)} %get-tuple-element.110), channel_id=1, source_target_pairs={{0,2},{2,0},{4,6},{6,4},{8,10},{10,8},{12,14},{14,12},{16,18},{18,... | collective-permute-start | bytes 983048 | tf_op jit(solution)/shard_map/ppermute | solution.py:476
  35.2 21.1 %collective-permute-start.37 = (bf16[128,1280]{1,0:T(8,128)(2,1)}, bf16[128,1280]{1,0:T(8,128)(2,1)S(1)}, u32[]{:S(2)}, u32[]{:S(2)}) collective-permute-start(bf16[128,1280]{1,0:T(8,128)(2,1)} %get-tuple-element.111), channel_id=1, source_target_pairs={{0,4},{2,6},{4,0},{6,2},{8,12},{10,14},{12,8},{14,10},{16,20},{18,... | collective-permute-start | bytes 983048 | tf_op jit(solution)/shard_map/ppermute | solution.py:476
  36.7 19.6 %collective-permute-start.38 = (bf16[128,1280]{1,0:T(8,128)(2,1)}, bf16[128,1280]{1,0:T(8,128)(2,1)}, u32[]{:S(2)}, u32[]{:S(2)}) collective-permute-start(bf16[128,1280]{1,0:T(8,128)(2,1)} %get-tuple-element.112), channel_id=1, source_target_pairs={{0,6},{2,4},{4,2},{6,0},{8,14},{10,12},{12,10},{14,8},{16,22},{18,... | collective-permute-start | bytes 983048 | tf_op jit(solution)/shard_map/ppermute | solution.py:476
  42.3 14.5 %copy-start.12 = (bf16[1024,128]{1,0:T(8,128)(2,1)S(1)}, bf16[1024,128]{1,0:T(8,128)(2,1)}, u32[]{:S(2)}) copy-start(bf16[1024,128]{1,0:T(8,128)(2,1)} %get-tuple-element.107) | copy-start | bytes 786436
  42.3 14.5 %collective-permute-start.35 = (bf16[1024,128]{1,0:T(8,128)(2,1)}, bf16[1024,128]{1,0:T(8,128)(2,1)S(1)}, u32[]{:S(2)}, u32[]{:S(2)}) collective-permute-start(bf16[1024,128]{1,0:T(8,128)(2,1)} %get-tuple-element.107), channel_id=1, source_target_pairs={{0,8},{2,10},{4,12},{6,14},{8,16},{10,18},{12,20},{14,22},{16,24},... | collective-permute-start | bytes 786440 | tf_op jit(solution)/shard_map/ppermute | solution.py:476
  46.0 24.7 %all-to-all-start = ((f16[4,128,1024]{2,1,0:T(8,128)(2,1)}), f16[4,128,1024]{2,1,0:T(8,128)(2,1)}, u32[]{:S(2)}, u32[]{:S(2)}) async-start(f16[4,128,1024]{2,1,0:T(8,128)(2,1)} %bitcast.1), calls=%async_computation | async-start | bytes 2097152 | tf_op jit(solution)/shard_map/all_to_all | solution.py:473
  50.3 9.7 %collective-permute-start.39 = (bf16[128,1280]{1,0:T(8,128)(2,1)S(1)}, bf16[128,1280]{1,0:T(8,128)(2,1)S(1)}, u32[]{:S(2)}, u32[]{:S(2)}) collective-permute-start(bf16[128,1280]{1,0:T(8,128)(2,1)S(1)} %collective-permute-done.36.n1), channel_id=1, source_target_pairs={{0,1},{1,0},{2,3},{3,2},{4,5},{5,4},{6,7},{7,6},{8,9},{9,8},{10,11... | collective-permute-start | bytes 983048 | tf_op jit(solution)/shard_map/ppermute | solution.py:494
  56.3 3.7 %collective-permute-start.40 = (bf16[128,1280]{1,0:T(8,128)(2,1)S(1)}, bf16[128,1280]{1,0:T(8,128)(2,1)S(1)}, u32[]{:S(2)}, u32[]{:S(2)}) collective-permute-start(bf16[128,1280]{1,0:T(8,128)(2,1)S(1)} %collective-permute-done.37.n2), channel_id=1, source_target_pairs={{0,1},{1,0},{2,3},{3,2},{4,5},{5,4},{6,7},{7,6},{8,9},{9,8},{10,11... | collective-permute-start | bytes 983048 | tf_op jit(solution)/shard_map/ppermute | solution.py:494
  56.3 3.7 %collective-permute-start.41 = (bf16[128,1280]{1,0:T(8,128)(2,1)}, bf16[128,1280]{1,0:T(8,128)(2,1)S(1)}, u32[]{:S(2)}, u32[]{:S(2)}) collective-permute-start(bf16[128,1280]{1,0:T(8,128)(2,1)} %collective-permute-done.38.n3), channel_id=1, source_target_pairs={{0,1},{1,0},{2,3},{3,2},{4,5},{5,4},{6,7},{7,6},{8,9},{9,8},{10,11... | collective-permute-start | bytes 983048 | tf_op jit(solution)/shard_map/ppermute | solution.py:494
  56.9 12.1 %collective-permute-start.42 = (bf16[1024,128]{1,0:T(8,128)(2,1)S(1)}, bf16[1024,128]{1,0:T(8,128)(2,1)}, u32[]{:S(2)}, u32[]{:S(2)}) collective-permute-start(bf16[1024,128]{1,0:T(8,128)(2,1)S(1)} %broadcast_select_fusion.1.xp), channel_id=1, source_target_pairs={{0,16},{2,18},{4,20},{6,22},{8,24},{10,26},{12,28},{14,30},{16,0},... | collective-permute-start | bytes 786440 | tf_op jit(solution)/shard_map/ppermute | solution.py:476
  73.0 13.2 %collective-permute-start.6 = (f16[128,1024]{1,0:T(8,128)(2,1)S(1)}, f16[128,1024]{1,0:T(8,128)(2,1)S(1)}, u32[]{:S(2)}, u32[]{:S(2)}) collective-permute-start(f16[128,1024]{1,0:T(8,128)(2,1)S(1)} %get-tuple-element.49), channel_id=1, source_target_pairs={{16,0},{18,2},{20,4},{22,6},{24,8},{26,10},{28,12},{30,14},{17,1},... | collective-permute-start | bytes 786440 | tf_op jit(solution)/shard_map/cond/branch_0_fun/ppermute | solution.py:546
  74.3 19.3 %collective-permute-start.2 = (bf16[1024,128]{1,0:T(8,128)(2,1)S(1)}, bf16[1024,128]{1,0:T(8,128)(2,1)S(1)}, u32[]{:S(2)}, u32[]{:S(2)}) collective-permute-start(bf16[1024,128]{1,0:T(8,128)(2,1)S(1)} %get-tuple-element.47), channel_id=1, source_target_pairs={{8,24},{10,26},{12,28},{14,30},{9,25},{11,27},{13,29},{15,31}} | collective-permute-start | bytes 786440 | tf_op jit(solution)/shard_map/cond/branch_0_fun/ppermute | solution.py:546
  74.9 18.7 %collective-permute-start.1 = (bf16[1024,128]{1,0:T(8,128)(2,1)S(1)}, bf16[1024,128]{1,0:T(8,128)(2,1)S(1)}, u32[]{:S(2)}, u32[]{:S(2)}) collective-permute-start(bf16[1024,128]{1,0:T(8,128)(2,1)S(1)} %get-tuple-element.47), channel_id=1, source_target_pairs={{8,16},{10,18},{12,20},{14,22},{9,17},{11,19},{13,21},{15,23}} | collective-permute-start | bytes 786440 | tf_op jit(solution)/shard_map/cond/branch_0_fun/ppermute | solution.py:546
  75.6 18.0 %collective-permute-start = (bf16[1024,128]{1,0:T(8,128)(2,1)S(1)}, bf16[1024,128]{1,0:T(8,128)(2,1)S(1)}, u32[]{:S(2)}, u32[]{:S(2)}) collective-permute-start(bf16[1024,128]{1,0:T(8,128)(2,1)S(1)} %get-tuple-element.47), channel_id=1, source_target_pairs={{8,0},{10,2},{12,4},{14,6},{9,1},{11,3},{13,5},{15,7}} | collective-permute-start | bytes 786440 | tf_op jit(solution)/shard_map/cond/branch_0_fun/ppermute | solution.py:546
  76.9 17.5 %collective-permute-start.5 = (bf16[1024,128]{1,0:T(8,128)(2,1)}, bf16[1024,128]{1,0:T(8,128)(2,1)}, u32[]{:S(2)}, u32[]{:S(2)}) collective-permute-start(bf16[1024,128]{1,0:T(8,128)(2,1)} %get-tuple-element.48), channel_id=1, source_target_pairs={{0,6},{2,4},{4,2},{6,0},{8,14},{10,12},{12,10},{14,8},{16,22},{18,... | collective-permute-start | bytes 786440 | tf_op jit(solution)/shard_map/cond/branch_0_fun/ppermute | solution.py:476
  86.1 14.2 %collective-permute-start.4 = (bf16[1024,128]{1,0:T(8,128)(2,1)}, bf16[1024,128]{1,0:T(8,128)(2,1)}, u32[]{:S(2)}, u32[]{:S(2)}) collective-permute-start(bf16[1024,128]{1,0:T(8,128)(2,1)} %get-tuple-element.48), channel_id=1, source_target_pairs={{0,4},{2,6},{4,0},{6,2},{8,12},{10,14},{12,8},{14,10},{16,20},{18,... | collective-permute-start | bytes 786440 | tf_op jit(solution)/shard_map/cond/branch_0_fun/ppermute | solution.py:476
  93.6 8.2 %collective-permute-start.3 = (bf16[1024,128]{1,0:T(8,128)(2,1)}, bf16[1024,128]{1,0:T(8,128)(2,1)}, u32[]{:S(2)}, u32[]{:S(2)}) collective-permute-start(bf16[1024,128]{1,0:T(8,128)(2,1)} %get-tuple-element.48), channel_id=1, source_target_pairs={{0,2},{2,0},{4,6},{6,4},{8,10},{10,8},{12,14},{14,12},{16,18},{18,... | collective-permute-start | bytes 786440 | tf_op jit(solution)/shard_map/cond/branch_0_fun/ppermute | solution.py:476
  106.5 14.8 %collective-permute-start.43 = (f32[128,1024]{1,0:T(8,128)}, f32[128,1024]{1,0:T(8,128)}, u32[]{:S(2)}, u32[]{:S(2)}) collective-permute-start(f32[128,1024]{1,0:T(8,128)} %get-tuple-element.116), channel_id=1, source_target_pairs={{0,24},{2,26},{4,28},{6,30},{8,0},{10,2},{12,4},{14,6},{16,8},{18,... | collective-permute-start | bytes 1572872 | tf_op jit(solution)/shard_map/ppermute | solution.py:476
  106.6 11.5 %collective-permute-start.46 = (bf16[1024,128]{1,0:T(8,128)(2,1)}, bf16[1024,128]{1,0:T(8,128)(2,1)}, u32[]{:S(2)}, u32[]{:S(2)}) collective-permute-start(bf16[1024,128]{1,0:T(8,128)(2,1)} %get-tuple-element.122.x0), channel_id=1, source_target_pairs={{0,6},{2,4},{4,2},{6,0},{8,14},{10,12},{12,10},{14,8},{16,22},{18,... | collective-permute-start | bytes 786440 | tf_op jit(solution)/shard_map/ppermute | solution.py:476
  106.7 14.7 %collective-permute-start.45 = (bf16[1024,128]{1,0:T(8,128)(2,1)}, bf16[1024,128]{1,0:T(8,128)(2,1)}, u32[]{:S(2)}, u32[]{:S(2)}) collective-permute-start(bf16[1024,128]{1,0:T(8,128)(2,1)} %get-tuple-element.122.x0), channel_id=1, source_target_pairs={{0,4},{2,6},{4,0},{6,2},{8,12},{10,14},{12,8},{14,10},{16,20},{18,... | collective-permute-start | bytes 786440 | tf_op jit(solution)/shard_map/ppermute | solution.py:476
  108.4 12.9 %collective-permute-start.44 = (bf16[1024,128]{1,0:T(8,128)(2,1)}, bf16[1024,128]{1,0:T(8,128)(2,1)}, u32[]{:S(2)}, u32[]{:S(2)}) collective-permute-start(bf16[1024,128]{1,0:T(8,128)(2,1)} %get-tuple-element.122.x0), channel_id=1, source_target_pairs={{0,2},{2,0},{4,6},{6,4},{8,10},{10,8},{12,14},{14,12},{16,18},{18,... | collective-permute-start | bytes 786440 | tf_op jit(solution)/shard_map/ppermute | solution.py:476
  110.2 18.9 %all-to-all-start.1 = ((bf16[4,256,128]{2,1,0:T(8,128)(2,1)}), bf16[4,256,128]{2,1,0:T(8,128)(2,1)S(1)}, u32[]{:S(2)}, u32[]{:S(2)}) async-start(bf16[4,256,128]{2,1,0:T(8,128)(2,1)} %bitcast.10), calls=%async_computation.1 | async-start | bytes 524288 | tf_op jit(solution)/shard_map/all_to_all | solution.py:473
  125.5 8.2 %collective-permute-start.47 = (f32[256,128]{1,0:T(8,128)}, f32[256,128]{1,0:T(8,128)S(1)}, u32[]{:S(2)}, u32[]{:S(2)}) collective-permute-start(f32[256,128]{1,0:T(8,128)} %get-tuple-element.129), channel_id=1, source_target_pairs={{0,2},{2,0},{4,6},{6,4},{8,10},{10,8},{12,14},{14,12},{16,18},{18,... | collective-permute-start | bytes 393224 | tf_op jit(solution)/shard_map/ppermute | solution.py:476
  125.9 7.8 %collective-permute-start.48 = (f32[256,128]{1,0:T(8,128)}, f32[256,128]{1,0:T(8,128)S(1)}, u32[]{:S(2)}, u32[]{:S(2)}) collective-permute-start(f32[256,128]{1,0:T(8,128)} %get-tuple-element.130), channel_id=1, source_target_pairs={{0,4},{2,6},{4,0},{6,2},{8,12},{10,14},{12,8},{14,10},{16,20},{18,... | collective-permute-start | bytes 393224 | tf_op jit(solution)/shard_map/ppermute | solution.py:476
  127.3 6.5 %collective-permute-start.49 = (f32[256,128]{1,0:T(8,128)}, f32[256,128]{1,0:T(8,128)S(1)}, u32[]{:S(2)}, u32[]{:S(2)}) collective-permute-start(f32[256,128]{1,0:T(8,128)} %get-tuple-element.131), channel_id=1, source_target_pairs={{0,6},{2,4},{4,2},{6,0},{8,14},{10,12},{12,10},{14,8},{16,22},{18,... | collective-permute-start | bytes 393224 | tf_op jit(solution)/shard_map/ppermute | solution.py:476
  (12 other events, 41.0 us)

commit v2 on v1

--- a/solution.py
+++ b/solution.py
@@ -113,41 +113,11 @@
     return jax.ShapeDtypeStruct(shape, dtype)
 
 
-def prep_kernel(s, e_ref, w_ref, f_ref, *outs):
-    half, width = e_ref.shape[1:]
-    quarter = (outs[0].shape[1] - width) // 2
-    for d in (1, 2, 3):
-        at = pl.ds(pl.multiple_of((s[CHIP] ^ d) * quarter, quarter), quarter)
-        high, low = split(f_ref[0, :, at])
-        for out, matrix, f in ((outs[d - 1], e_ref[0], high), (outs[d + 2], w_ref[0, 0], low)):
-            out[:, :width] = matrix
-            out[:, width:width + quarter] = f[:half]
-            out[:, width + quarter:] = f[half:]
-
-
-def prep(s, strips, dinv_rows, fwd_state):
-    tiles, span, columns = fwd_state.shape
-    width = strips.shape[3]
-    half, quarter = span // 2, columns // 4
-    outs = call(
-        prep_kernel, "prep", s, (1,),
-        [
-            pl.BlockSpec((1, half, width), lambda i, s: (s[SLOT], s[CORE], 0)),
-            pl.BlockSpec((1, 1, half, width), lambda i, s: (0, s[SLOT], s[CORE], 0)),
-            pl.BlockSpec((1, span, columns), lambda i, s: (s[SLOT], 0, 0)),
-        ],
-        [whole(half, width + 2 * quarter)] * 6,
-        [shaped(BF, half, width + 2 * quarter)] * 6,
-        (dinv_rows, strips, fwd_state),
-    )
-    return outs[:3], outs[3:]
-
-
 def later(s, slot):
     return 4 * slot + s[PLANE] > s[PANEL] + 1
 
 
-def sums_kernel(own, s, strips, state, out_ref, *rest):
+def sums_kernel(own, s, strips, state, out_ref, *rest, between=None):
     copies, (bv, wv, sb, sw, so) = rest[:own], rest[own:]
     tiles, span, _ = bv.shape
     which = s[KEEP] if own else 1 - s[KEEP]
@@ -172,6 +142,8 @@
             strip(a).start()
 
     out_ref[...] = jnp.zeros_like(out_ref)
+    if between is not None:
+        between()
     for a in range(tiles):
         if own:
             rows(a).wait()
@@ -192,6 +164,50 @@
 
         for a in range(tiles):
             back(a).wait()
+
+
+def sent_kernel(s, strips, state, dinv, f, out_ref, *rest):
+    outs, (bv, wv, ev, sv, fv, sb, sw, so, sp) = rest[:6], rest[6:]
+    half, width = ev.shape
+    quarter = (outs[0].shape[1] - width) // 2
+    at = pl.ds(pl.multiple_of(s[CORE] * half, half), half)
+    copies = begin(
+        sp,
+        [(f.at[s[SLOT]], fv), (dinv.at[s[SLOT], at, :], ev), (strips.at[0, s[SLOT], at, :], sv)],
+    )
+
+    def payloads():
+        finish(copies)
+        for d in (1, 2, 3):
+            at = pl.ds(pl.multiple_of((s[CHIP] ^ d) * quarter, quarter), quarter)
+            high, low = split(fv[:, at])
+            for out, matrix, part in ((outs[d - 1], ev, high), (outs[d + 2], sv, low)):
+                out[:, :width] = matrix[...]
+                out[:, width:width + quarter] = part[:half]
+                out[:, width + quarter:] = part[half:]
+
+    sums_kernel(False, s, strips, state, out_ref, bv, wv, sb, sw, so, between=payloads)
+
+
+def sums_and_payloads(s, strips, dinv_rows, fwd_state, back_state):
+    tiles, span, columns = back_state.shape
+    width = strips.shape[3]
+    half, quarter = span // 2, columns // 4
+    payload = (half, width + 2 * quarter)
+    dma = pltpu.SemaphoreType.DMA
+    outs = call(
+        sent_kernel, "sums", s, (1,), [HBM] * 4,
+        [whole(columns, width)] + [whole(*payload)] * 6,
+        [shaped(F32, columns, width)] + [shaped(BF, *payload)] * 6,
+        (strips, back_state, dinv_rows, fwd_state),
+        scratch=[
+            pltpu.VMEM((tiles, span, columns), F32), pltpu.VMEM((tiles, span, width), BF),
+            pltpu.VMEM((half, width), BF), pltpu.VMEM((half, width), BF), pltpu.VMEM((span, columns), F32),
+            dma((tiles,)), dma((tiles,)), dma((tiles,)), dma((3,)),
+        ],
+        limit=60,
+    )
+    return outs[0], outs[1:4], outs[4:]
 
 
 def sums(s, own, strips, back_state):
@@ -205,6 +221,7 @@
         (strips, back_state),
         scratch=[pltpu.VMEM((tiles, span, columns), F32), pltpu.VMEM((tiles, span, width), BF)]
         + [pltpu.SemaphoreType.DMA((tiles,))] * 3,
+        limit=60,
     )
 
 
@@ -511,11 +528,9 @@
             limit=limit,
         )
 
-    (sent,) = sums(s, 0, strips, back_state)
+    sent, to_e, to_w = sums_and_payloads(s, strips, dinv_rows, fwd_state, back_state)
     sent = sent.astype(HF)
     got = permute(sent, lambda i: i ^ 4)
-
-    to_e, to_w = prep(after(s, sent), strips, dinv_rows, fwd_state)
     m = deal(to_e)
     kept, copy = sums(after(s, *to_e), 1, strips, back_state)
     m = after_all(m, kept)
@@ -526,7 +541,7 @@
     )
     below = up(hi_p)
 
-    pair = (after(kept, hi_p) + got.astype(F32)).astype(HF)
+    pair = (after(kept, hi_p, n[0]) + got.astype(F32)).astype(HF)
     parts = exchange(pair).reshape(4, quarter, width)
 
     xp = jnp.where(is_a, hi_p, below)

time: 137 us -> 135 us (0.985)
  waiting for transfers between devices: 37.7 us -> 33.3 us
  Pallas kernels: 40.1 us -> 42.9 us
    ppermute x19, waiting for transfers between devices: 29 us -> 23.8 us  [permute(): return lax.ppermute(x, 'blk', [(i, to(i)) for i in range(16)])]
    pallas_call x10 -> x9, Pallas kernels: 40.1 us -> 42.9 us  [call(): pl.pallas_call(kernel, grid_spec=pltpu.PrefetchScalarGridSpec(num_scalar_...]
    ppermute x19, starting transfers between devices: 29.5 us -> 27.6 us  [permute(): return lax.ppermute(x, 'blk', [(i, to(i)) for i in range(16)])]
    unnamed x26 -> x38, local copies, waits for them, and re-layouts: 3.12 us -> 2.54 us
  transfers between devices with their start and end apart: 31 -> 31, of which waited for: 10 -> 10; matrix products, arithmetic and copies ran while one was open for 4% -> 4% of each run, Pallas kernels for 22% -> 23%
where the time goes in v2:
time: 135 us; the launch traced here: 132 us
  Pallas kernels  42.9 us (32%)
  starting transfers between devices  41.1 us (30%)
  waiting for transfers between devices  33.3 us (25%)
  other arithmetic  10.8 us (8%)
  local copies, waits for them, and re-layouts  2.54 us (2%)
  between operations  1.79 us (1%)
    pallas_call x9, Pallas kernels, call(): pl.pallas_call(kernel, grid_spec=pltpu.PrefetchScalarGridSpec(num_scalar_...  42.9 us
    ppermute x19, starting transfers between devices, permute(): return lax.ppermute(x, 'blk', [(i, to(i)) for i in range(16)])  27.6 us
    ppermute x19, waiting for transfers between devices, permute(): return lax.ppermute(x, 'blk', [(i, to(i)) for i in range(16)])  23.8 us
    ppermute x4, waiting for transfers between devices, send(): lax.ppermute(x, 'blk', [(4 * a + j, 4 * b + j) for a, b in pairs for j in...  9.55 us
    all_to_all x2, starting transfers between devices, exchange(): return lax.all_to_all(x, 'blk', 0, 0, axis_index_groups=groups, tiled=True)  8.28 us
    ppermute x4, starting transfers between devices, send(): lax.ppermute(x, 'blk', [(4 * a + j, 4 * b + j) for a, b in pairs for j in...  3.93 us
    convert_element_type x1, other arithmetic, plane_body(): pair = (after(kept, hi_p, n[0]) + got.astype(F32)).astype(HF)  3.3 us
    convert_element_type x1, other arithmetic, plane_body(): sent = sent.astype(HF)  2.83 us
  transfers between devices with their start and end apart: 31, of which 10 were waited for; matrix products, arithmetic and copies ran while one was open for 4% of the time, Pallas kernels for 23%

profile of v2, /device:TPU:0, one launch (start us, length us, event | category | flops | bytes accessed | tf_op | source)
XLA Modules:
  0.0 132.5 jit_solution(7555373521706513695)
XLA Ops:
  1.9 6.3 %sums.2 = (f32[512,1024]{1,0:T(8,128)}, bf16[128,1280]{1,0:T(8,128)(2,1)}, bf16[128,1280]{1,0:T(8,128)(2,1)}, bf16[128,1280]{1,0:T(8,128)(2,1)}, bf16[128,1280]{...) custom-call(s32[16]{0:T(128)} %compare_select_fusion.7.s, bf16[2,6,256,1024]{3,2,1,0:T(8,128)(2,1)} %strips.11, ...), custom_call_target="tpu_custom_call" | custom-call | tf_op jit(solution)/shard_map/sums/pallas_call | solution.py:93
  8.2 2.8 %convert_element_type.49 = f16[512,1024]{1,0:T(8,128)(2,1)} convert(f32[512,1024]{1,0:T(8,128)} %get-tuple-element.109) | non-fusion elementwise | flops 524288 | bytes 3145728 | tf_op jit(solution)/shard_map/convert_element_type | solution.py:532
  11.0 3.0 %collective-permute-start.35 = (f16[512,1024]{1,0:T(8,128)(2,1)}, f16[512,1024]{1,0:T(8,128)(2,1)}, u32[]{:S(2)}, u32[]{:S(2)}) collective-permute-start(f16[512,1024]{1,0:T(8,128)(2,1)} %convert_element_type.49), channel_id=1, source_target_pairs={{0,8},{2,10},{4,12},{6,14},{8,0},{10,2},{12,4},{14,6},{16,24},{18,... | collective-permute-start | bytes 3145736 | tf_op jit(solution)/shard_map/ppermute | solution.py:493
  14.1 1.5 %collective-permute-start.28 = (bf16[128,1280]{1,0:T(8,128)(2,1)S(1)}, bf16[128,1280]{1,0:T(8,128)(2,1)S(1)}, u32[]{:S(2)}, u32[]{:S(2)}) collective-permute-start(bf16[128,1280]{1,0:T(8,128)(2,1)S(1)} %copy-done.18), channel_id=1, source_target_pairs={{0,2},{2,0},{4,6},{6,4},{8,10},{10,8},{12,14},{14,12},{16,18},{18,... | collective-permute-start | bytes 983048 | tf_op jit(solution)/shard_map/ppermute | solution.py:493
  15.6 1.5 %collective-permute-start.29 = (bf16[128,1280]{1,0:T(8,128)(2,1)S(1)}, bf16[128,1280]{1,0:T(8,128)(2,1)S(1)}, u32[]{:S(2)}, u32[]{:S(2)}) collective-permute-start(bf16[128,1280]{1,0:T(8,128)(2,1)S(1)} %copy-done.17), channel_id=1, source_target_pairs={{0,4},{2,6},{4,0},{6,2},{8,12},{10,14},{12,8},{14,10},{16,20},{18,... | collective-permute-start | bytes 983048 | tf_op jit(solution)/shard_map/ppermute | solution.py:493
  17.6 5.9 %sums.3 = (f32[512,1024]{1,0:T(8,128)}, f32[6,256,512]{2,1,0:T(8,128)}) custom-call(s32[16]{0:T(128)} %compare_select_fusion.7.s, bf16[2,6,256,1024]{3,2,1,0:T(8,128)(2,1)} %strips.11, f32[6,256,512]{2,1,0:T(8,128)} %state.3), custom_call_target="tpu_custom_call" | custom-call | tf_op jit(solution)/shard_map/sums/pallas_call | solution.py:93
  24.7 6.8 %collective-permute-done.29.m2 = bf16[128,1280]{1,0:T(8,128)(2,1)S(1)} collective-permute-done((bf16[128,1280]{1,0:T(8,128)(2,1)S(1)}, bf16[128,1280]{1,0:T(8,128)(2,1)S(1)}, u32[]{:S(2)}, u32[]{:S(2)}) %collective-permute-start.29) | collective-permute-done | bytes 327712 | tf_op jit(solution)/shard_map/ppermute | solution.py:493
  35.9 4.4 %first.1 = (bf16[1024,128]{1,0:T(8,128)(2,1)}, bf16[1024,128]{1,0:T(8,128)(2,1)}, bf16[4,256,1024]{2,1,0:T(8,128)(2,1)}) custom-call(s32[16]{0:T(128)} %compare_select_fusion.7.s, f32[6,256,512]{2,1,0:T(8,128)} %f.7, bf16[6,256,1024]{2,1,0:T(8,128)(2,1)} %own.1, bf16[128,1280]{1,0:T(8,128)(2,1)} %copy-done.8, bf16[128,1280]{1,0:T(8,128)(2,1)} %copy-done.9, ...), custom_call_target="tpu_custom_call" | custom-call | tf_op jit(solution)/shard_map/first/pallas_call | solution.py:93
  40.8 2.0 %collective-permute-done.34.n1 = bf16[128,1280]{1,0:T(8,128)(2,1)S(1)} collective-permute-done((bf16[128,1280]{1,0:T(8,128)(2,1)}, bf16[128,1280]{1,0:T(8,128)(2,1)S(1)}, u32[]{:S(2)}, u32[]{:S(2)}) %collective-permute-start.34) | collective-permute-done | bytes 327712 | tf_op jit(solution)/shard_map/ppermute | solution.py:493
  42.9 3.3 %add_convert_fusion = f16[512,1024]{1,0:T(8,128)(2,1)} fusion(f32[512,1024]{1,0:T(8,128)} %get-tuple-element.108, f16[512,1024]{1,0:T(8,128)(2,1)} %collective-permute-done.35), kind=kLoop, calls=%fused_computation.5 | loop fusion | flops 1572864 | bytes 4194304 | tf_op jit(solution)/shard_map/convert_element_type | solution.py:544
  46.2 4.2 %all-to-all-start = ((f16[4,128,1024]{2,1,0:T(8,128)(2,1)}), f16[4,128,1024]{2,1,0:T(8,128)(2,1)}, u32[]{:S(2)}, u32[]{:S(2)}) async-start(f16[4,128,1024]{2,1,0:T(8,128)(2,1)} %bitcast.1), calls=%async_computation | async-start | bytes 2097152 | tf_op jit(solution)/shard_map/all_to_all | solution.py:490
  51.1 3.4 %collective-permute-start.42 = (bf16[1024,128]{1,0:T(8,128)(2,1)S(1)}, bf16[1024,128]{1,0:T(8,128)(2,1)}, u32[]{:S(2)}, u32[]{:S(2)}) collective-permute-start(bf16[1024,128]{1,0:T(8,128)(2,1)S(1)} %broadcast_select_fusion.1.xp), channel_id=1, source_target_pairs={{0,16},{2,18},{4,20},{6,22},{8,24},{10,26},{12,28},{14,30},{16,0},... | collective-permute-start | bytes 786440 | tf_op jit(solution)/shard_map/ppermute | solution.py:493
  55.5 5.0 %second.1 = (bf16[1024,128]{1,0:T(8,128)(2,1)S(1)}, bf16[1024,128]{1,0:T(8,128)(2,1)}) custom-call(s32[16]{0:T(128)} %compare_select_fusion.7.s, f32[6,256,512]{2,1,0:T(8,128)} %f.7, bf16[2,6,256,1024]{3,2,1,0:T(8,128)(2,1)} %strips.11, bf16[1024,128]{1,0:T(8,128)(2,1)} %copy-done.3, bf16[4,256,1024]{2,1,0:T(8,128)(2,1)} %get-tuple-element.110.e, ...), custom_call_target="tpu_custom_call" | custom-call | tf_op jit(solution)/shard_map/second/pallas_call | solution.py:93
  60.5 6.7 %collective-permute-done.42 = bf16[1024,128]{1,0:T(8,128)(2,1)} collective-permute-done((bf16[1024,128]{1,0:T(8,128)(2,1)S(1)}, bf16[1024,128]{1,0:T(8,128)(2,1)}, u32[]{:S(2)}, u32[]{:S(2)}) %collective-permute-start.42) | collective-permute-done | bytes 262176 | tf_op jit(solution)/shard_map/ppermute | solution.py:493
  67.2 1.7 %broadcast_select_fusion.x0.p0 = bf16[1024,128]{1,0:T(8,128)(2,1)} fusion(bf16[1024,128]{1,0:T(8,128)(2,1)} %copy-done.3, bf16[1024,128]{1,0:T(8,128)(2,1)} %collective-permute-done.42, pred[]{:T(512)S(6)} %or.4), kind=kLoop, calls=%fused_computation.6 | loop fusion | flops 131072 | bytes 786433 | tf_op jit(solution)/shard_map/jit(_where)/select_n | solution.py:570
  68.9 1.5 %convert_reduce_fusion.part = f32[128,1024]{1,0:T(8,128)S(1)} fusion(f16[4,128,1024]{2,1,0:T(8,128)(2,1)} %all-to-all-done), kind=kLoop, calls=%fused_computation.4 | loop fusion | flops 917504 | bytes 1572864 | tf_op jit(solution)/shard_map/reduce_sum | solution.py:554
  71.2 25.7 %conditional.4 = (bf16[1024,128]{1,0:T(8,128)(2,1)S(1)}, bf16[1024,128]{1,0:T(8,128)(2,1)}, bf16[1024,128]{1,0:T(8,128)(2,1)}, bf16[1024,128]{1,0:T(8,128)(2,1)}, f32[128,1024]{1,0:T(8,128)}) conditional(s32[]{:T(128)} %clamp.3, (pred[]{:T(512)}, bf16[1024,128]{1,0:T(8,128)(2,1)S(1)}, bf16[1024,128]{1,0:T(8,128)(2,1)}, ...), branch_computations={%region_1.2_spmd, %region_2.3_spmd, %region_3.4_spmd, %region_4.5_... | conditional | flops 524288 | bytes 9437505
  75.2 2.9 %collective-permute-start.5 = (bf16[1024,128]{1,0:T(8,128)(2,1)}, bf16[1024,128]{1,0:T(8,128)(2,1)}, u32[]{:S(2)}, u32[]{:S(2)}) collective-permute-start(bf16[1024,128]{1,0:T(8,128)(2,1)} %get-tuple-element.48), channel_id=1, source_target_pairs={{0,6},{2,4},{4,2},{6,0},{8,14},{10,12},{12,10},{14,8},{16,22},{18,... | collective-permute-start | bytes 786440 | tf_op jit(solution)/shard_map/cond/branch_0_fun/ppermute | solution.py:493
  78.1 8.8 %collective-permute-done.6 = f16[128,1024]{1,0:T(8,128)(2,1)S(1)} collective-permute-done((f16[128,1024]{1,0:T(8,128)(2,1)S(1)}, f16[128,1024]{1,0:T(8,128)(2,1)S(1)}, u32[]{:S(2)}, u32[]{:S(2)}) %collective-permute-start.6) | collective-permute-done | bytes 262176 | tf_op jit(solution)/shard_map/cond/branch_0_fun/ppermute | solution.py:561
  86.9 1.9 %collective-permute-start.4 = (bf16[1024,128]{1,0:T(8,128)(2,1)}, bf16[1024,128]{1,0:T(8,128)(2,1)}, u32[]{:S(2)}, u32[]{:S(2)}) collective-permute-start(bf16[1024,128]{1,0:T(8,128)(2,1)} %get-tuple-element.48), channel_id=1, source_target_pairs={{0,4},{2,6},{4,0},{6,2},{8,12},{10,14},{12,8},{14,10},{16,20},{18,... | collective-permute-start | bytes 786440 | tf_op jit(solution)/shard_map/cond/branch_0_fun/ppermute | solution.py:493
  88.8 1.5 %collective-permute-start.3 = (bf16[1024,128]{1,0:T(8,128)(2,1)}, bf16[1024,128]{1,0:T(8,128)(2,1)}, u32[]{:S(2)}, u32[]{:S(2)}) collective-permute-start(bf16[1024,128]{1,0:T(8,128)(2,1)} %get-tuple-element.48), channel_id=1, source_target_pairs={{0,2},{2,0},{4,6},{6,4},{8,10},{10,8},{12,14},{14,12},{16,18},{18,... | collective-permute-start | bytes 786440 | tf_op jit(solution)/shard_map/cond/branch_0_fun/ppermute | solution.py:493
  91.9 3.6 %collective-permute-done.4 = bf16[1024,128]{1,0:T(8,128)(2,1)} collective-permute-done((bf16[1024,128]{1,0:T(8,128)(2,1)}, bf16[1024,128]{1,0:T(8,128)(2,1)}, u32[]{:S(2)}, u32[]{:S(2)}) %collective-permute-start.4) | collective-permute-done | bytes 262176 | tf_op jit(solution)/shard_map/cond/branch_0_fun/ppermute | solution.py:493
  95.5 1.5 %collective-permute-done.3 = bf16[1024,128]{1,0:T(8,128)(2,1)} collective-permute-done((bf16[1024,128]{1,0:T(8,128)(2,1)}, bf16[1024,128]{1,0:T(8,128)(2,1)}, u32[]{:S(2)}, u32[]{:S(2)}) %collective-permute-start.3) | collective-permute-done | bytes 262176 | tf_op jit(solution)/shard_map/cond/branch_0_fun/ppermute | solution.py:493
  97.0 4.9 %third.1 = (f32[4,256,128]{2,1,0:T(8,128)}, f32[128,1024]{1,0:T(8,128)}) custom-call(s32[16]{0:T(128)} %compare_select_fusion.7.s, f32[128,1024]{1,0:T(8,128)} %copy-done.2, f32[128,1024]{1,0:T(8,128)} %get-tuple-element.138.far, bf16[4,256,1024]{2,1,0:T(8,128)(2,1)} %get-tuple-element.110.e, bf16[2,6,256,1024]{3,2,1,0:T(8,128)(2,1)} %strips.11, ...), custom_call_target="tpu_custom_call" | custom-call | tf_op jit(solution)/shard_map/third/pallas_call | solution.py:93
  102.0 1.5 %collective-permute-start.46 = (bf16[1024,128]{1,0:T(8,128)(2,1)S(1)}, bf16[1024,128]{1,0:T(8,128)(2,1)}, u32[]{:S(2)}, u32[]{:S(2)}) collective-permute-start(bf16[1024,128]{1,0:T(8,128)(2,1)S(1)} %get-tuple-element.122.x0), channel_id=1, source_target_pairs={{0,6},{2,4},{4,2},{6,0},{8,14},{10,12},{12,10},{14,8},{16,22},{18,... | collective-permute-start | bytes 786440 | tf_op jit(solution)/shard_map/ppermute | solution.py:493
  103.5 1.5 %collective-permute-start.45 = (bf16[1024,128]{1,0:T(8,128)(2,1)S(1)}, bf16[1024,128]{1,0:T(8,128)(2,1)}, u32[]{:S(2)}, u32[]{:S(2)}) collective-permute-start(bf16[1024,128]{1,0:T(8,128)(2,1)S(1)} %get-tuple-element.122.x0), channel_id=1, source_target_pairs={{0,4},{2,6},{4,0},{6,2},{8,12},{10,14},{12,8},{14,10},{16,20},{18,... | collective-permute-start | bytes 786440 | tf_op jit(solution)/shard_map/ppermute | solution.py:493
  105.5 4.0 %all-to-all-start.1 = ((bf16[4,256,128]{2,1,0:T(8,128)(2,1)}), bf16[4,256,128]{2,1,0:T(8,128)(2,1)}, u32[]{:S(2)}, u32[]{:S(2)}) async-start(bf16[4,256,128]{2,1,0:T(8,128)(2,1)} %bitcast.10), calls=%async_computation.1 | async-start | bytes 524288 | tf_op jit(solution)/shard_map/all_to_all | solution.py:490
  109.6 5.3 %update.2.f = f32[6,256,512]{2,1,0:T(8,128)} custom-call(s32[16]{0:T(128)} %compare_select_fusion.7.s, f32[6,256,512]{2,1,0:T(8,128)} %f.7, bf16[2,6,256,1024]{3,2,1,0:T(8,128)(2,1)} %strips.11, bf16[1024,128]{1,0:T(8,128)(2,1)} %broadcast_select_fusion.x0.p0, bf16[1024,128]{1,0:T(8,128)(2,1)} %get-tuple-element.119.x1.p1, ...), custom_call_target="tpu_custom_call" | custom-call | tf_op jit(solution)/shard_map/update/pallas_call | solution.py:93
  114.9 1.5 %collective-permute-done.45.x2 = bf16[1024,128]{1,0:T(8,128)(2,1)} collective-permute-done((bf16[1024,128]{1,0:T(8,128)(2,1)S(1)}, bf16[1024,128]{1,0:T(8,128)(2,1)}, u32[]{:S(2)}, u32[]{:S(2)}) %collective-permute-start.45) | collective-permute-done | bytes 262176 | tf_op jit(solution)/shard_map/ppermute | solution.py:493
  117.2 4.2 %fourth.1 = (f32[256,128]{1,0:T(8,128)}, f32[256,128]{1,0:T(8,128)}, f32[256,128]{1,0:T(8,128)}, f32[256,128]{1,0:T(8,128)}) custom-call(s32[16]{0:T(128)} %compare_select_fusion.7.s, f32[128,1024]{1,0:T(8,128)} %copy-done.2, f32[128,1024]{1,0:T(8,128)} %get-tuple-element.138.far, f32[128,1024]{1,0:T(8,128)} %copy-done.11, ...), custom_call_target="tpu_custom_call" | custom-call | tf_op jit(solution)/shard_map/fourth/pallas_call | solution.py:93
  121.5 1.6 %collective-permute-start.47 = (f32[256,128]{1,0:T(8,128)}, f32[256,128]{1,0:T(8,128)S(1)}, u32[]{:S(2)}, u32[]{:S(2)}) collective-permute-start(f32[256,128]{1,0:T(8,128)} %get-tuple-element.129), channel_id=1, source_target_pairs={{0,2},{2,0},{4,6},{6,4},{8,10},{10,8},{12,14},{14,12},{16,18},{18,... | collective-permute-start | bytes 393224 | tf_op jit(solution)/shard_map/ppermute | solution.py:493
  125.0 5.4 %update.3 = f32[6,256,512]{2,1,0:T(8,128)} custom-call(s32[16]{0:T(128)} %compare_select_fusion.7.s, f32[6,256,512]{2,1,0:T(8,128)} %update.2.f, bf16[2,6,256,1024]{3,2,1,0:T(8,128)(2,1)} %strips.11, bf16[1024,128]{1,0:T(8,128)(2,1)S(1)} %get-tuple-element.122.x0, bf16[1024,128]{1,0:T(8,128)(2,1)} %collective-permute-done.44.x1, ...), custom_call_target="tpu_custom_call", output_to_operand_aliasing={{}: (1, {})} | custom-call | tf_op jit(solution)/shard_map/update/pallas_call | solution.py:93
  (87 shorter events, 20.5 us)
Async XLA Ops:
  11.0 31.8 %collective-permute-start.35 = (f16[512,1024]{1,0:T(8,128)(2,1)}, f16[512,1024]{1,0:T(8,128)(2,1)}, u32[]{:S(2)}, u32[]{:S(2)}) collective-permute-start(f16[512,1024]{1,0:T(8,128)(2,1)} %convert_element_type.49), channel_id=1, source_target_pairs={{0,8},{2,10},{4,12},{6,14},{8,0},{10,2},{12,4},{14,6},{16,24},{18,... | collective-permute-start | bytes 3145736 | tf_op jit(solution)/shard_map/ppermute | solution.py:493
  14.1 10.6 %collective-permute-start.28 = (bf16[128,1280]{1,0:T(8,128)(2,1)S(1)}, bf16[128,1280]{1,0:T(8,128)(2,1)S(1)}, u32[]{:S(2)}, u32[]{:S(2)}) collective-permute-start(bf16[128,1280]{1,0:T(8,128)(2,1)S(1)} %copy-done.18), channel_id=1, source_target_pairs={{0,2},{2,0},{4,6},{6,4},{8,10},{10,8},{12,14},{14,12},{16,18},{18,... | collective-permute-start | bytes 983048 | tf_op jit(solution)/shard_map/ppermute | solution.py:493
  15.6 15.9 %collective-permute-start.29 = (bf16[128,1280]{1,0:T(8,128)(2,1)S(1)}, bf16[128,1280]{1,0:T(8,128)(2,1)S(1)}, u32[]{:S(2)}, u32[]{:S(2)}) collective-permute-start(bf16[128,1280]{1,0:T(8,128)(2,1)S(1)} %copy-done.17), channel_id=1, source_target_pairs={{0,4},{2,6},{4,0},{6,2},{8,12},{10,14},{12,8},{14,10},{16,20},{18,... | collective-permute-start | bytes 983048 | tf_op jit(solution)/shard_map/ppermute | solution.py:493
  17.1 17.6 %copy-start.15 = (bf16[128,1280]{1,0:T(8,128)(2,1)S(1)}, bf16[128,1280]{1,0:T(8,128)(2,1)}, u32[]{:S(2)}) copy-start(bf16[128,1280]{1,0:T(8,128)(2,1)} %get-tuple-element.112) | copy-start | bytes 983044
  17.1 14.4 %collective-permute-start.30 = (bf16[128,1280]{1,0:T(8,128)(2,1)S(1)}, bf16[128,1280]{1,0:T(8,128)(2,1)S(1)}, u32[]{:S(2)}, u32[]{:S(2)}) collective-permute-start(bf16[128,1280]{1,0:T(8,128)(2,1)S(1)} %copy-done.16), channel_id=1, source_target_pairs={{0,6},{2,4},{4,2},{6,0},{8,14},{10,12},{12,10},{14,8},{16,22},{18,... | collective-permute-start | bytes 983048 | tf_op jit(solution)/shard_map/ppermute | solution.py:493
  31.5 1.7 %collective-permute-start.31 = (bf16[128,1280]{1,0:T(8,128)(2,1)S(1)}, bf16[128,1280]{1,0:T(8,128)(2,1)S(1)}, u32[]{:S(2)}, u32[]{:S(2)}) collective-permute-start(bf16[128,1280]{1,0:T(8,128)(2,1)S(1)} %collective-permute-done.28.m1), channel_id=1, source_target_pairs={{0,1},{1,0},{2,3},{3,2},{4,5},{5,4},{6,7},{7,6},{8,9},{9,8},{10,11... | collective-permute-start | bytes 983048 | tf_op jit(solution)/shard_map/ppermute | solution.py:511
  31.6 3.1 %collective-permute-start.32 = (bf16[128,1280]{1,0:T(8,128)(2,1)S(1)}, bf16[128,1280]{1,0:T(8,128)(2,1)S(1)}, u32[]{:S(2)}, u32[]{:S(2)}) collective-permute-start(bf16[128,1280]{1,0:T(8,128)(2,1)S(1)} %collective-permute-done.29.m2), channel_id=1, source_target_pairs={{0,1},{1,0},{2,3},{3,2},{4,5},{5,4},{6,7},{7,6},{8,9},{9,8},{10,11... | collective-permute-start | bytes 983048 | tf_op jit(solution)/shard_map/ppermute | solution.py:511
  32.1 3.8 %collective-permute-start.33 = (bf16[128,1280]{1,0:T(8,128)(2,1)S(1)}, bf16[128,1280]{1,0:T(8,128)(2,1)}, u32[]{:S(2)}, u32[]{:S(2)}) collective-permute-start(bf16[128,1280]{1,0:T(8,128)(2,1)S(1)} %collective-permute-done.30.m3), channel_id=1, source_target_pairs={{0,1},{1,0},{2,3},{3,2},{4,5},{5,4},{6,7},{7,6},{8,9},{9,8},{10,11... | collective-permute-start | bytes 983048 | tf_op jit(solution)/shard_map/ppermute | solution.py:511
  32.1 10.7 %collective-permute-start.34 = (bf16[128,1280]{1,0:T(8,128)(2,1)}, bf16[128,1280]{1,0:T(8,128)(2,1)S(1)}, u32[]{:S(2)}, u32[]{:S(2)}) collective-permute-start(bf16[128,1280]{1,0:T(8,128)(2,1)} %get-tuple-element.107), channel_id=1, source_target_pairs={{0,2},{2,0},{4,6},{6,4},{8,10},{10,8},{12,14},{14,12},{16,18},{18,... | collective-permute-start | bytes 983048 | tf_op jit(solution)/shard_map/ppermute | solution.py:493
  33.2 17.3 %collective-permute-start.37 = (bf16[128,1280]{1,0:T(8,128)(2,1)}, bf16[128,1280]{1,0:T(8,128)(2,1)}, u32[]{:S(2)}, u32[]{:S(2)}) collective-permute-start(bf16[128,1280]{1,0:T(8,128)(2,1)} %get-tuple-element.111), channel_id=1, source_target_pairs={{0,4},{2,6},{4,0},{6,2},{8,12},{10,14},{12,8},{14,10},{16,20},{18,... | collective-permute-start | bytes 983048 | tf_op jit(solution)/shard_map/ppermute | solution.py:493
  34.7 16.3 %collective-permute-start.38 = (bf16[128,1280]{1,0:T(8,128)(2,1)S(1)}, bf16[128,1280]{1,0:T(8,128)(2,1)}, u32[]{:S(2)}, u32[]{:S(2)}) collective-permute-start(bf16[128,1280]{1,0:T(8,128)(2,1)S(1)} %copy-done.15), channel_id=1, source_target_pairs={{0,6},{2,4},{4,2},{6,0},{8,14},{10,12},{12,10},{14,8},{16,22},{18,... | collective-permute-start | bytes 983048 | tf_op jit(solution)/shard_map/ppermute | solution.py:493
  40.3 10.8 %collective-permute-start.36 = (bf16[1024,128]{1,0:T(8,128)(2,1)}, bf16[1024,128]{1,0:T(8,128)(2,1)S(1)}, u32[]{:S(2)}, u32[]{:S(2)}) collective-permute-start(bf16[1024,128]{1,0:T(8,128)(2,1)} %get-tuple-element.106), channel_id=1, source_target_pairs={{0,8},{2,10},{4,12},{6,14},{8,16},{10,18},{12,20},{14,22},{16,24},... | collective-permute-start | bytes 786440 | tf_op jit(solution)/shard_map/ppermute | solution.py:493
  46.2 22.7 %all-to-all-start = ((f16[4,128,1024]{2,1,0:T(8,128)(2,1)}), f16[4,128,1024]{2,1,0:T(8,128)(2,1)}, u32[]{:S(2)}, u32[]{:S(2)}) async-start(f16[4,128,1024]{2,1,0:T(8,128)(2,1)} %bitcast.1), calls=%async_computation | async-start | bytes 2097152 | tf_op jit(solution)/shard_map/all_to_all | solution.py:490
  50.4 4.2 %collective-permute-start.39 = (bf16[128,1280]{1,0:T(8,128)(2,1)S(1)}, bf16[128,1280]{1,0:T(8,128)(2,1)S(1)}, u32[]{:S(2)}, u32[]{:S(2)}) collective-permute-start(bf16[128,1280]{1,0:T(8,128)(2,1)S(1)} %collective-permute-done.34.n1), channel_id=1, source_target_pairs={{0,1},{1,0},{2,3},{3,2},{4,5},{5,4},{6,7},{7,6},{8,9},{9,8},{10,11... | collective-permute-start | bytes 983048 | tf_op jit(solution)/shard_map/ppermute | solution.py:511
  50.5 4.1 %collective-permute-start.40 = (bf16[128,1280]{1,0:T(8,128)(2,1)}, bf16[128,1280]{1,0:T(8,128)(2,1)S(1)}, u32[]{:S(2)}, u32[]{:S(2)}) collective-permute-start(bf16[128,1280]{1,0:T(8,128)(2,1)} %collective-permute-done.37.n2), channel_id=1, source_target_pairs={{0,1},{1,0},{2,3},{3,2},{4,5},{5,4},{6,7},{7,6},{8,9},{9,8},{10,11... | collective-permute-start | bytes 983048 | tf_op jit(solution)/shard_map/ppermute | solution.py:511
  51.0 3.6 %collective-permute-start.41 = (bf16[128,1280]{1,0:T(8,128)(2,1)}, bf16[128,1280]{1,0:T(8,128)(2,1)S(1)}, u32[]{:S(2)}, u32[]{:S(2)}) collective-permute-start(bf16[128,1280]{1,0:T(8,128)(2,1)} %collective-permute-done.38.n3), channel_id=1, source_target_pairs={{0,1},{1,0},{2,3},{3,2},{4,5},{5,4},{6,7},{7,6},{8,9},{9,8},{10,11... | collective-permute-start | bytes 983048 | tf_op jit(solution)/shard_map/ppermute | solution.py:511
  51.1 16.1 %collective-permute-start.42 = (bf16[1024,128]{1,0:T(8,128)(2,1)S(1)}, bf16[1024,128]{1,0:T(8,128)(2,1)}, u32[]{:S(2)}, u32[]{:S(2)}) collective-permute-start(bf16[1024,128]{1,0:T(8,128)(2,1)S(1)} %broadcast_select_fusion.1.xp), channel_id=1, source_target_pairs={{0,16},{2,18},{4,20},{6,22},{8,24},{10,26},{12,28},{14,30},{16,0},... | collective-permute-start | bytes 786440 | tf_op jit(solution)/shard_map/ppermute | solution.py:493
  71.2 15.6 %collective-permute-start.6 = (f16[128,1024]{1,0:T(8,128)(2,1)S(1)}, f16[128,1024]{1,0:T(8,128)(2,1)S(1)}, u32[]{:S(2)}, u32[]{:S(2)}) collective-permute-start(f16[128,1024]{1,0:T(8,128)(2,1)S(1)} %get-tuple-element.49), channel_id=1, source_target_pairs={{16,0},{18,2},{20,4},{22,6},{24,8},{26,10},{28,12},{30,14},{17,1},... | collective-permute-start | bytes 786440 | tf_op jit(solution)/shard_map/cond/branch_0_fun/ppermute | solution.py:561
  72.5 16.2 %collective-permute-start.2 = (bf16[1024,128]{1,0:T(8,128)(2,1)S(1)}, bf16[1024,128]{1,0:T(8,128)(2,1)S(1)}, u32[]{:S(2)}, u32[]{:S(2)}) collective-permute-start(bf16[1024,128]{1,0:T(8,128)(2,1)S(1)} %get-tuple-element.47), channel_id=1, source_target_pairs={{8,24},{10,26},{12,28},{14,30},{9,25},{11,27},{13,29},{15,31}} | collective-permute-start | bytes 786440 | tf_op jit(solution)/shard_map/cond/branch_0_fun/ppermute | solution.py:561
  73.2 17.9 %collective-permute-start.1 = (bf16[1024,128]{1,0:T(8,128)(2,1)S(1)}, bf16[1024,128]{1,0:T(8,128)(2,1)S(1)}, u32[]{:S(2)}, u32[]{:S(2)}) collective-permute-start(bf16[1024,128]{1,0:T(8,128)(2,1)S(1)} %get-tuple-element.47), channel_id=1, source_target_pairs={{8,16},{10,18},{12,20},{14,22},{9,17},{11,19},{13,21},{15,23}} | collective-permute-start | bytes 786440 | tf_op jit(solution)/shard_map/cond/branch_0_fun/ppermute | solution.py:561
  73.9 17.9 %collective-permute-start = (bf16[1024,128]{1,0:T(8,128)(2,1)S(1)}, bf16[1024,128]{1,0:T(8,128)(2,1)S(1)}, u32[]{:S(2)}, u32[]{:S(2)}) collective-permute-start(bf16[1024,128]{1,0:T(8,128)(2,1)S(1)} %get-tuple-element.47), channel_id=1, source_target_pairs={{8,0},{10,2},{12,4},{14,6},{9,1},{11,3},{13,5},{15,7}} | collective-permute-start | bytes 786440 | tf_op jit(solution)/shard_map/cond/branch_0_fun/ppermute | solution.py:561
  75.2 16.7 %collective-permute-start.5 = (bf16[1024,128]{1,0:T(8,128)(2,1)}, bf16[1024,128]{1,0:T(8,128)(2,1)}, u32[]{:S(2)}, u32[]{:S(2)}) collective-permute-start(bf16[1024,128]{1,0:T(8,128)(2,1)} %get-tuple-element.48), channel_id=1, source_target_pairs={{0,6},{2,4},{4,2},{6,0},{8,14},{10,12},{12,10},{14,8},{16,22},{18,... | collective-permute-start | bytes 786440 | tf_op jit(solution)/shard_map/cond/branch_0_fun/ppermute | solution.py:493
  86.9 8.6 %collective-permute-start.4 = (bf16[1024,128]{1,0:T(8,128)(2,1)}, bf16[1024,128]{1,0:T(8,128)(2,1)}, u32[]{:S(2)}, u32[]{:S(2)}) collective-permute-start(bf16[1024,128]{1,0:T(8,128)(2,1)} %get-tuple-element.48), channel_id=1, source_target_pairs={{0,4},{2,6},{4,0},{6,2},{8,12},{10,14},{12,8},{14,10},{16,20},{18,... | collective-permute-start | bytes 786440 | tf_op jit(solution)/shard_map/cond/branch_0_fun/ppermute | solution.py:493
  88.8 8.2 %collective-permute-start.3 = (bf16[1024,128]{1,0:T(8,128)(2,1)}, bf16[1024,128]{1,0:T(8,128)(2,1)}, u32[]{:S(2)}, u32[]{:S(2)}) collective-permute-start(bf16[1024,128]{1,0:T(8,128)(2,1)} %get-tuple-element.48), channel_id=1, source_target_pairs={{0,2},{2,0},{4,6},{6,4},{8,10},{10,8},{12,14},{14,12},{16,18},{18,... | collective-permute-start | bytes 786440 | tf_op jit(solution)/shard_map/cond/branch_0_fun/ppermute | solution.py:493
  101.9 14.5 %collective-permute-start.43 = (f32[128,1024]{1,0:T(8,128)}, f32[128,1024]{1,0:T(8,128)S(1)}, u32[]{:S(2)}, u32[]{:S(2)}) collective-permute-start(f32[128,1024]{1,0:T(8,128)} %get-tuple-element.116), channel_id=1, source_target_pairs={{0,24},{2,26},{4,28},{6,30},{8,0},{10,2},{12,4},{14,6},{16,8},{18,... | collective-permute-start | bytes 1572872 | tf_op jit(solution)/shard_map/ppermute | solution.py:493
  102.0 12.9 %collective-permute-start.46 = (bf16[1024,128]{1,0:T(8,128)(2,1)S(1)}, bf16[1024,128]{1,0:T(8,128)(2,1)}, u32[]{:S(2)}, u32[]{:S(2)}) collective-permute-start(bf16[1024,128]{1,0:T(8,128)(2,1)S(1)} %get-tuple-element.122.x0), channel_id=1, source_target_pairs={{0,6},{2,4},{4,2},{6,0},{8,14},{10,12},{12,10},{14,8},{16,22},{18,... | collective-permute-start | bytes 786440 | tf_op jit(solution)/shard_map/ppermute | solution.py:493
  103.5 12.9 %collective-permute-start.45 = (bf16[1024,128]{1,0:T(8,128)(2,1)S(1)}, bf16[1024,128]{1,0:T(8,128)(2,1)}, u32[]{:S(2)}, u32[]{:S(2)}) collective-permute-start(bf16[1024,128]{1,0:T(8,128)(2,1)S(1)} %get-tuple-element.122.x0), channel_id=1, source_target_pairs={{0,4},{2,6},{4,0},{6,2},{8,12},{10,14},{12,8},{14,10},{16,20},{18,... | collective-permute-start | bytes 786440 | tf_op jit(solution)/shard_map/ppermute | solution.py:493
  105.0 11.5 %collective-permute-start.44 = (bf16[1024,128]{1,0:T(8,128)(2,1)S(1)}, bf16[1024,128]{1,0:T(8,128)(2,1)}, u32[]{:S(2)}, u32[]{:S(2)}) collective-permute-start(bf16[1024,128]{1,0:T(8,128)(2,1)S(1)} %get-tuple-element.122.x0), channel_id=1, source_target_pairs={{0,2},{2,0},{4,6},{6,4},{8,10},{10,8},{12,14},{14,12},{16,18},{18,... | collective-permute-start | bytes 786440 | tf_op jit(solution)/shard_map/ppermute | solution.py:493
  105.5 19.5 %all-to-all-start.1 = ((bf16[4,256,128]{2,1,0:T(8,128)(2,1)}), bf16[4,256,128]{2,1,0:T(8,128)(2,1)}, u32[]{:S(2)}, u32[]{:S(2)}) async-start(bf16[4,256,128]{2,1,0:T(8,128)(2,1)} %bitcast.10), calls=%async_computation.1 | async-start | bytes 524288 | tf_op jit(solution)/shard_map/all_to_all | solution.py:490
  121.5 9.0 %collective-permute-start.47 = (f32[256,128]{1,0:T(8,128)}, f32[256,128]{1,0:T(8,128)S(1)}, u32[]{:S(2)}, u32[]{:S(2)}) collective-permute-start(f32[256,128]{1,0:T(8,128)} %get-tuple-element.129), channel_id=1, source_target_pairs={{0,2},{2,0},{4,6},{6,4},{8,10},{10,8},{12,14},{14,12},{16,18},{18,... | collective-permute-start | bytes 393224 | tf_op jit(solution)/shard_map/ppermute | solution.py:493
  123.0 7.8 %collective-permute-start.48 = (f32[256,128]{1,0:T(8,128)}, f32[256,128]{1,0:T(8,128)S(1)}, u32[]{:S(2)}, u32[]{:S(2)}) collective-permute-start(f32[256,128]{1,0:T(8,128)} %get-tuple-element.130), channel_id=1, source_target_pairs={{0,4},{2,6},{4,0},{6,2},{8,12},{10,14},{12,8},{14,10},{16,20},{18,... | collective-permute-start | bytes 393224 | tf_op jit(solution)/shard_map/ppermute | solution.py:493
  124.2 6.7 %collective-permute-start.49 = (f32[256,128]{1,0:T(8,128)}, f32[256,128]{1,0:T(8,128)S(1)}, u32[]{:S(2)}, u32[]{:S(2)}) collective-permute-start(f32[256,128]{1,0:T(8,128)} %get-tuple-element.131), channel_id=1, source_target_pairs={{0,6},{2,4},{4,2},{6,0},{8,14},{10,12},{12,10},{14,8},{16,22},{18,... | collective-permute-start | bytes 393224 | tf_op jit(solution)/shard_map/ppermute | solution.py:493
  (18 other events, 79.5 us)

commit v3 on v2

--- a/solution.py
+++ b/solution.py
@@ -560,15 +560,16 @@
         def send(x, *pairs):
             return lax.ppermute(x, "blk", [(4 * a + j, 4 * b + j) for a, b in pairs for j in range(4)])
 
-        def run(x, xp, part):
+        def run(x, xp, part, lo):
             far = send(part, (first ^ 2, first), (source ^ 2, source))
             got = [send(x, (source, z)) for z in range(4) if z != source]
-            return jnp.where(is_b, x, sum(got)), gather(xp), far.astype(F32)
+            own = exchange(lo).reshape(4, span, quarter)
+            return jnp.where(is_b, x, sum(got)), gather(xp), far.astype(F32), own
 
         return run
 
     xp = jnp.where(is_a | is_b, xp, xp_far)
-    xq, xp_rest, far = lax.switch(home, [last(z) for z in range(4)], hi_q, xp, part16)
+    xq, xp_rest, far, lo_own = lax.switch(home, [last(z) for z in range(4)], hi_q, xp, part16, lo)
     xp_all = [xp] + xp_rest
     xq_all = [xq] + gather(xq)
 
@@ -577,7 +578,6 @@
         [piece32, piece32, matrix, matrix], 13,
     )
     r = down(r)
-    lo_own = exchange(after(lo, y_b)).reshape(4, span, quarter)
     state = update(update_one_kernel, after(s, y_b), fwd_state, strips, xp_all)
     y = small(
         fourth_kernel, "fourth", [own] * 4, (part, far, r, e, after(y_b, state, *xq_all)),

time: 135 us -> 139 us (1.030)
  Pallas kernels: 42.9 us -> 47.5 us
    pallas_call x9, Pallas kernels: 42.9 us -> 47.5 us  [call(): pl.pallas_call(kernel, grid_spec=pltpu.PrefetchScalarGridSpec(num_scalar_...]
    all_to_all x2, waiting for transfers between devices: 0.01 us -> 4.6 us  [exchange(): return lax.all_to_all(x, 'blk', 0, 0, axis_index_groups=groups, tiled=True)]
    ppermute x19, waiting for transfers between devices: 23.8 us -> 20.1 us  [permute(): return lax.ppermute(x, 'blk', [(i, to(i)) for i in range(16)])]
  transfers between devices with their start and end apart: 31 -> 31, of which waited for: 10 -> 8; matrix products, arithmetic and copies ran while one was open for 4% -> 4% of each run, Pallas kernels for 23% -> 21%
where the time goes in v3:
time: 139 us; the launch traced here: 138 us
  Pallas kernels  47.5 us (34%)
  starting transfers between devices  41.1 us (30%)
  waiting for transfers between devices  33.5 us (24%)
  other arithmetic  10.9 us (8%)
  local copies, waits for them, and re-layouts  2.52 us (2%)
  between operations  1.81 us (1%)
    pallas_call x9, Pallas kernels, call(): pl.pallas_call(kernel, grid_spec=pltpu.PrefetchScalarGridSpec(num_scalar_...  47.5 us
    ppermute x19, starting transfers between devices, permute(): return lax.ppermute(x, 'blk', [(i, to(i)) for i in range(16)])  27.6 us
    ppermute x19, waiting for transfers between devices, permute(): return lax.ppermute(x, 'blk', [(i, to(i)) for i in range(16)])  20.1 us
    ppermute x4, waiting for transfers between devices, send(): lax.ppermute(x, 'blk', [(4 * a + j, 4 * b + j) for a, b in pairs for j in...  8.76 us
    all_to_all x2, starting transfers between devices, exchange(): return lax.all_to_all(x, 'blk', 0, 0, axis_index_groups=groups, tiled=True)  8.28 us
    all_to_all x2, waiting for transfers between devices, exchange(): return lax.all_to_all(x, 'blk', 0, 0, axis_index_groups=groups, tiled=True)  4.6 us
    ppermute x4, starting transfers between devices, send(): lax.ppermute(x, 'blk', [(4 * a + j, 4 * b + j) for a, b in pairs for j in...  3.93 us
    convert_element_type x1, other arithmetic, plane_body(): pair = (after(kept, hi_p, n[0]) + got.astype(F32)).astype(HF)  3.31 us
  transfers between devices with their start and end apart: 31, of which 8 were waited for; matrix products, arithmetic and copies ran while one was open for 4% of the time, Pallas kernels for 21%

profile of v3, /device:TPU:0, one launch (start us, length us, event | category | flops | bytes accessed | tf_op | source)
XLA Modules:
  0.0 137.6 jit_solution(1697477782565434398)
XLA Ops:
  1.9 7.9 %sums.2 = (f32[512,1024]{1,0:T(8,128)}, bf16[128,1280]{1,0:T(8,128)(2,1)}, bf16[128,1280]{1,0:T(8,128)(2,1)}, bf16[128,1280]{1,0:T(8,128)(2,1)}, bf16[128,1280]{...) custom-call(s32[16]{0:T(128)} %compare_select_fusion.7.s, bf16[2,6,256,1024]{3,2,1,0:T(8,128)(2,1)} %strips.11, ...), custom_call_target="tpu_custom_call" | custom-call | tf_op jit(solution)/shard_map/sums/pallas_call | solution.py:93
  9.8 2.8 %convert_element_type.49 = f16[512,1024]{1,0:T(8,128)(2,1)} convert(f32[512,1024]{1,0:T(8,128)} %get-tuple-element.123) | non-fusion elementwise | flops 524288 | bytes 3145728 | tf_op jit(solution)/shard_map/convert_element_type | solution.py:532
  12.7 3.0 %collective-permute-start.35 = (f16[512,1024]{1,0:T(8,128)(2,1)}, f16[512,1024]{1,0:T(8,128)(2,1)}, u32[]{:S(2)}, u32[]{:S(2)}) collective-permute-start(f16[512,1024]{1,0:T(8,128)(2,1)} %convert_element_type.49), channel_id=1, source_target_pairs={{0,8},{2,10},{4,12},{6,14},{8,0},{10,2},{12,4},{14,6},{16,24},{18,... | collective-permute-start | bytes 3145736 | tf_op jit(solution)/shard_map/ppermute | solution.py:493
  15.7 1.5 %collective-permute-start.28 = (bf16[128,1280]{1,0:T(8,128)(2,1)S(1)}, bf16[128,1280]{1,0:T(8,128)(2,1)S(1)}, u32[]{:S(2)}, u32[]{:S(2)}) collective-permute-start(bf16[128,1280]{1,0:T(8,128)(2,1)S(1)} %copy-done.18), channel_id=1, source_target_pairs={{0,2},{2,0},{4,6},{6,4},{8,10},{10,8},{12,14},{14,12},{16,18},{18,... | collective-permute-start | bytes 983048 | tf_op jit(solution)/shard_map/ppermute | solution.py:493
  17.2 1.5 %collective-permute-start.29 = (bf16[128,1280]{1,0:T(8,128)(2,1)S(1)}, bf16[128,1280]{1,0:T(8,128)(2,1)S(1)}, u32[]{:S(2)}, u32[]{:S(2)}) collective-permute-start(bf16[128,1280]{1,0:T(8,128)(2,1)S(1)} %copy-done.17), channel_id=1, source_target_pairs={{0,4},{2,6},{4,0},{6,2},{8,12},{10,14},{12,8},{14,10},{16,20},{18,... | collective-permute-start | bytes 983048 | tf_op jit(solution)/shard_map/ppermute | solution.py:493
  19.2 6.2 %sums.3 = (f32[512,1024]{1,0:T(8,128)}, f32[6,256,512]{2,1,0:T(8,128)}) custom-call(s32[16]{0:T(128)} %compare_select_fusion.7.s, bf16[2,6,256,1024]{3,2,1,0:T(8,128)(2,1)} %strips.11, f32[6,256,512]{2,1,0:T(8,128)} %state.3), custom_call_target="tpu_custom_call" | custom-call | tf_op jit(solution)/shard_map/sums/pallas_call | solution.py:93
  26.3 6.8 %collective-permute-done.29.m2 = bf16[128,1280]{1,0:T(8,128)(2,1)S(1)} collective-permute-done((bf16[128,1280]{1,0:T(8,128)(2,1)S(1)}, bf16[128,1280]{1,0:T(8,128)(2,1)S(1)}, u32[]{:S(2)}, u32[]{:S(2)}) %collective-permute-start.29) | collective-permute-done | bytes 327712 | tf_op jit(solution)/shard_map/ppermute | solution.py:493
  34.9 1.5 %collective-permute-start.37 = (bf16[128,1280]{1,0:T(8,128)(2,1)}, bf16[128,1280]{1,0:T(8,128)(2,1)}, u32[]{:S(2)}, u32[]{:S(2)}) collective-permute-start(bf16[128,1280]{1,0:T(8,128)(2,1)} %get-tuple-element.125), channel_id=1, source_target_pairs={{0,4},{2,6},{4,0},{6,2},{8,12},{10,14},{12,8},{14,10},{16,20},{18,... | collective-permute-start | bytes 983048 | tf_op jit(solution)/shard_map/ppermute | solution.py:493
  37.6 4.4 %first.1 = (bf16[1024,128]{1,0:T(8,128)(2,1)}, bf16[1024,128]{1,0:T(8,128)(2,1)}, bf16[4,256,1024]{2,1,0:T(8,128)(2,1)}) custom-call(s32[16]{0:T(128)} %compare_select_fusion.7.s, f32[6,256,512]{2,1,0:T(8,128)} %f.7, bf16[6,256,1024]{2,1,0:T(8,128)(2,1)} %own.1, bf16[128,1280]{1,0:T(8,128)(2,1)} %copy-done.8, bf16[128,1280]{1,0:T(8,128)(2,1)} %copy-done.9, ...), custom_call_target="tpu_custom_call" | custom-call | tf_op jit(solution)/shard_map/first/pallas_call | solution.py:93
  42.4 2.1 %collective-permute-done.34.n1 = bf16[128,1280]{1,0:T(8,128)(2,1)S(1)} collective-permute-done((bf16[128,1280]{1,0:T(8,128)(2,1)}, bf16[128,1280]{1,0:T(8,128)(2,1)S(1)}, u32[]{:S(2)}, u32[]{:S(2)}) %collective-permute-start.34) | collective-permute-done | bytes 327712 | tf_op jit(solution)/shard_map/ppermute | solution.py:493
  44.5 3.3 %add_convert_fusion = f16[512,1024]{1,0:T(8,128)(2,1)} fusion(f32[512,1024]{1,0:T(8,128)} %get-tuple-element.122, f16[512,1024]{1,0:T(8,128)(2,1)} %collective-permute-done.35), kind=kLoop, calls=%fused_computation.5 | loop fusion | flops 1572864 | bytes 4194304 | tf_op jit(solution)/shard_map/convert_element_type | solution.py:544
  47.8 4.2 %all-to-all-start.4 = ((f16[4,128,1024]{2,1,0:T(8,128)(2,1)}), f16[4,128,1024]{2,1,0:T(8,128)(2,1)}, u32[]{:S(2)}, u32[]{:S(2)}) async-start(f16[4,128,1024]{2,1,0:T(8,128)(2,1)} %bitcast.5), calls=%async_computation.4 | async-start | bytes 2097152 | tf_op jit(solution)/shard_map/all_to_all | solution.py:490
  52.8 3.5 %collective-permute-start.42 = (bf16[1024,128]{1,0:T(8,128)(2,1)S(1)}, bf16[1024,128]{1,0:T(8,128)(2,1)}, u32[]{:S(2)}, u32[]{:S(2)}) collective-permute-start(bf16[1024,128]{1,0:T(8,128)(2,1)S(1)} %broadcast_select_fusion.1.xp), channel_id=1, source_target_pairs={{0,16},{2,18},{4,20},{6,22},{8,24},{10,26},{12,28},{14,30},{16,0},... | collective-permute-start | bytes 786440 | tf_op jit(solution)/shard_map/ppermute | solution.py:493
  57.2 5.0 %second.1 = (bf16[1024,128]{1,0:T(8,128)(2,1)S(1)}, bf16[1024,128]{1,0:T(8,128)(2,1)}) custom-call(s32[16]{0:T(128)} %compare_select_fusion.7.s, f32[6,256,512]{2,1,0:T(8,128)} %f.7, bf16[2,6,256,1024]{3,2,1,0:T(8,128)(2,1)} %strips.11, bf16[1024,128]{1,0:T(8,128)(2,1)} %copy-done.3, bf16[4,256,1024]{2,1,0:T(8,128)(2,1)} %get-tuple-element.124.e, ...), custom_call_target="tpu_custom_call" | custom-call | tf_op jit(solution)/shard_map/second/pallas_call | solution.py:93
  62.3 6.7 %collective-permute-done.42 = bf16[1024,128]{1,0:T(8,128)(2,1)} collective-permute-done((bf16[1024,128]{1,0:T(8,128)(2,1)S(1)}, bf16[1024,128]{1,0:T(8,128)(2,1)}, u32[]{:S(2)}, u32[]{:S(2)}) %collective-permute-start.42) | collective-permute-done | bytes 262176 | tf_op jit(solution)/shard_map/ppermute | solution.py:493
  68.9 1.7 %broadcast_select_fusion.x0.p0 = bf16[1024,128]{1,0:T(8,128)(2,1)} fusion(bf16[1024,128]{1,0:T(8,128)(2,1)} %copy-done.3, bf16[1024,128]{1,0:T(8,128)(2,1)} %collective-permute-done.42, pred[]{:T(512)S(6)} %or.4), kind=kLoop, calls=%fused_computation.6 | loop fusion | flops 131072 | bytes 786433 | tf_op jit(solution)/shard_map/jit(_where)/select_n | solution.py:571
  70.6 1.5 %convert_reduce_fusion.part = f32[128,1024]{1,0:T(8,128)S(1)} fusion(f16[4,128,1024]{2,1,0:T(8,128)(2,1)} %all-to-all-done.4), kind=kLoop, calls=%fused_computation.4 | loop fusion | flops 917504 | bytes 1572864 | tf_op jit(solution)/shard_map/reduce_sum | solution.py:554
  72.9 28.7 %conditional.4 = (bf16[1024,128]{1,0:T(8,128)(2,1)S(1)}, bf16[1024,128]{1,0:T(8,128)(2,1)}, bf16[1024,128]{1,0:T(8,128)(2,1)}, bf16[1024,128]{1,0:T(8,128)(2,1)}...) conditional(s32[]{:T(128)} %clamp.3, (pred[]{:T(512)}, ...), branch_computations={%region_1.2_spmd, %region_2.3_spmd, %region_3.4_spmd, %region_4.5_... | conditional | flops 524288 | bytes 10223977
  75.6 1.3 collective-permute-start
  76.9 2.9 %collective-permute-start.5 = (bf16[1024,128]{1,0:T(8,128)(2,1)}, bf16[1024,128]{1,0:T(8,128)(2,1)}, u32[]{:S(2)}, u32[]{:S(2)}) collective-permute-start(bf16[1024,128]{1,0:T(8,128)(2,1)} %get-tuple-element.58), channel_id=1, source_target_pairs={{0,6},{2,4},{4,2},{6,0},{8,14},{10,12},{12,10},{14,8},{16,22},{18,... | collective-permute-start | bytes 786440 | tf_op jit(solution)/shard_map/cond/branch_0_fun/ppermute | solution.py:493
  79.8 8.8 %collective-permute-done.6 = f16[128,1024]{1,0:T(8,128)(2,1)S(1)} collective-permute-done((f16[128,1024]{1,0:T(8,128)(2,1)S(1)}, f16[128,1024]{1,0:T(8,128)(2,1)S(1)}, u32[]{:S(2)}, u32[]{:S(2)}) %collective-permute-start.6) | collective-permute-done | bytes 262176 | tf_op jit(solution)/shard_map/cond/branch_0_fun/ppermute | solution.py:561
  88.5 1.9 %collective-permute-start.4 = (bf16[1024,128]{1,0:T(8,128)(2,1)}, bf16[1024,128]{1,0:T(8,128)(2,1)}, u32[]{:S(2)}, u32[]{:S(2)}) collective-permute-start(bf16[1024,128]{1,0:T(8,128)(2,1)} %get-tuple-element.58), channel_id=1, source_target_pairs={{0,4},{2,6},{4,0},{6,2},{8,12},{10,14},{12,8},{14,10},{16,20},{18,... | collective-permute-start | bytes 786440 | tf_op jit(solution)/shard_map/cond/branch_0_fun/ppermute | solution.py:493
  90.4 1.5 %collective-permute-start.3 = (bf16[1024,128]{1,0:T(8,128)(2,1)}, bf16[1024,128]{1,0:T(8,128)(2,1)}, u32[]{:S(2)}, u32[]{:S(2)}) collective-permute-start(bf16[1024,128]{1,0:T(8,128)(2,1)} %get-tuple-element.58), channel_id=1, source_target_pairs={{0,2},{2,0},{4,6},{6,4},{8,10},{10,8},{12,14},{14,12},{16,18},{18,... | collective-permute-start | bytes 786440 | tf_op jit(solution)/shard_map/cond/branch_0_fun/ppermute | solution.py:493
  91.9 4.0 %all-to-all-start = ((bf16[4,256,128]{2,1,0:T(8,128)(2,1)}), bf16[4,256,128]{2,1,0:T(8,128)(2,1)}, u32[]{:S(2)}, u32[]{:S(2)}) async-start(bf16[4,256,128]{2,1,0:T(8,128)(2,1)} %bitcast), calls=%async_computation | async-start | bytes 524288 | tf_op jit(solution)/shard_map/cond/branch_0_fun/all_to_all | solution.py:490
  96.8 4.6 %all-to-all-done = bf16[4,256,128]{2,1,0:T(8,128)(2,1)} async-done(((bf16[4,256,128]{2,1,0:T(8,128)(2,1)}), bf16[4,256,128]{2,1,0:T(8,128)(2,1)}, u32[]{:S(2)}, u32[]{:S(2)}) %all-to-all-start) | async-done | bytes 262176 | tf_op jit(solution)/shard_map/cond/branch_0_fun/all_to_all | solution.py:490
  101.6 4.9 %third.1 = (f32[4,256,128]{2,1,0:T(8,128)}, f32[128,1024]{1,0:T(8,128)}) custom-call(s32[16]{0:T(128)} %compare_select_fusion.7.s, f32[128,1024]{1,0:T(8,128)} %copy-done.2, f32[128,1024]{1,0:T(8,128)} %get-tuple-element.153.far, bf16[4,256,1024]{2,1,0:T(8,128)(2,1)} %get-tuple-element.124.e, bf16[2,6,256,1024]{3,2,1,0:T(8,128)(2,1)} %strips.11, ...), custom_call_target="tpu_custom_call" | custom-call | tf_op jit(solution)/shard_map/third/pallas_call | solution.py:93
  106.6 2.4 %collective-permute-start.46 = (bf16[1024,128]{1,0:T(8,128)(2,1)S(1)}, bf16[1024,128]{1,0:T(8,128)(2,1)}, u32[]{:S(2)}, u32[]{:S(2)}) collective-permute-start(bf16[1024,128]{1,0:T(8,128)(2,1)S(1)} %get-tuple-element.137.x0), channel_id=1, source_target_pairs={{0,6},{2,4},{4,2},{6,0},{8,14},{10,12},{12,10},{14,8},{16,22},{18,... | collective-permute-start | bytes 786440 | tf_op jit(solution)/shard_map/ppermute | solution.py:493
  110.2 6.5 %update.2.f = f32[6,256,512]{2,1,0:T(8,128)} custom-call(s32[16]{0:T(128)} %compare_select_fusion.7.s, f32[6,256,512]{2,1,0:T(8,128)} %f.7, bf16[2,6,256,1024]{3,2,1,0:T(8,128)(2,1)} %strips.11, bf16[1024,128]{1,0:T(8,128)(2,1)} %broadcast_select_fusion.x0.p0, bf16[1024,128]{1,0:T(8,128)(2,1)} %get-tuple-element.134.x1.p1, ...), custom_call_target="tpu_custom_call" | custom-call | tf_op jit(solution)/shard_map/update/pallas_call | solution.py:93
  117.0 3.4 %collective-permute-done.45.x2 = bf16[1024,128]{1,0:T(8,128)(2,1)} collective-permute-done((bf16[1024,128]{1,0:T(8,128)(2,1)S(1)}, bf16[1024,128]{1,0:T(8,128)(2,1)}, u32[]{:S(2)}, u32[]{:S(2)}) %collective-permute-start.45) | collective-permute-done | bytes 262176 | tf_op jit(solution)/shard_map/ppermute | solution.py:493
  121.2 4.2 %fourth.1 = (f32[256,128]{1,0:T(8,128)}, f32[256,128]{1,0:T(8,128)}, f32[256,128]{1,0:T(8,128)}, f32[256,128]{1,0:T(8,128)}) custom-call(s32[16]{0:T(128)} %compare_select_fusion.7.s, f32[128,1024]{1,0:T(8,128)} %copy-done.2, f32[128,1024]{1,0:T(8,128)} %get-tuple-element.153.far, f32[128,1024]{1,0:T(8,128)} %copy-done.11, ...), custom_call_target="tpu_custom_call" | custom-call | tf_op jit(solution)/shard_map/fourth/pallas_call | solution.py:93
  129.0 6.9 %update.3 = f32[6,256,512]{2,1,0:T(8,128)} custom-call(s32[16]{0:T(128)} %compare_select_fusion.7.s, f32[6,256,512]{2,1,0:T(8,128)} %update.2.f, bf16[2,6,256,1024]{3,2,1,0:T(8,128)(2,1)} %strips.11, bf16[1024,128]{1,0:T(8,128)(2,1)S(1)} %get-tuple-element.137.x0, bf16[1024,128]{1,0:T(8,128)(2,1)} %collective-permute-done.44.x1, ...), custom_call_target="tpu_custom_call", output_to_operand_aliasing={{}: (1, {})} | custom-call | tf_op jit(solution)/shard_map/update/pallas_call | solution.py:93
  135.9 1.5 %place.1 = f32[6,256,512]{2,1,0:T(8,128)} custom-call(s32[16]{0:T(128)S(1)} %copy-done.1, f32[6,256,512]{2,1,0:T(8,128)} %get-tuple-element.142.copy, f32[256,128]{1,0:T(8,128)S(1)} %copy-done, f32[256,128]{1,0:T(8,128)S(1)} %collective-permute-done.47.y1, f32[256,128]{1,0:T(8,128)S(1)} %collective-permute-done.48.y2, ...), custom_call_target="tpu_custom_call", output_to_operand_aliasing={{}: (1, {})} | custom-call | tf_op jit(solution)/shard_map/place/pallas_call | solution.py:93
  (87 shorter events, 17.1 us)
Async XLA Ops:
  12.7 31.8 %collective-permute-start.35 = (f16[512,1024]{1,0:T(8,128)(2,1)}, f16[512,1024]{1,0:T(8,128)(2,1)}, u32[]{:S(2)}, u32[]{:S(2)}) collective-permute-start(f16[512,1024]{1,0:T(8,128)(2,1)} %convert_element_type.49), channel_id=1, source_target_pairs={{0,8},{2,10},{4,12},{6,14},{8,0},{10,2},{12,4},{14,6},{16,24},{18,... | collective-permute-start | bytes 3145736 | tf_op jit(solution)/shard_map/ppermute | solution.py:493
  15.7 10.6 %collective-permute-start.28 = (bf16[128,1280]{1,0:T(8,128)(2,1)S(1)}, bf16[128,1280]{1,0:T(8,128)(2,1)S(1)}, u32[]{:S(2)}, u32[]{:S(2)}) collective-permute-start(bf16[128,1280]{1,0:T(8,128)(2,1)S(1)} %copy-done.18), channel_id=1, source_target_pairs={{0,2},{2,0},{4,6},{6,4},{8,10},{10,8},{12,14},{14,12},{16,18},{18,... | collective-permute-start | bytes 983048 | tf_op jit(solution)/shard_map/ppermute | solution.py:493
  17.2 15.9 %collective-permute-start.29 = (bf16[128,1280]{1,0:T(8,128)(2,1)S(1)}, bf16[128,1280]{1,0:T(8,128)(2,1)S(1)}, u32[]{:S(2)}, u32[]{:S(2)}) collective-permute-start(bf16[128,1280]{1,0:T(8,128)(2,1)S(1)} %copy-done.17), channel_id=1, source_target_pairs={{0,4},{2,6},{4,0},{6,2},{8,12},{10,14},{12,8},{14,10},{16,20},{18,... | collective-permute-start | bytes 983048 | tf_op jit(solution)/shard_map/ppermute | solution.py:493
  18.7 17.6 %copy-start.15 = (bf16[128,1280]{1,0:T(8,128)(2,1)S(1)}, bf16[128,1280]{1,0:T(8,128)(2,1)}, u32[]{:S(2)}) copy-start(bf16[128,1280]{1,0:T(8,128)(2,1)} %get-tuple-element.126) | copy-start | bytes 983044
  18.7 14.4 %collective-permute-start.30 = (bf16[128,1280]{1,0:T(8,128)(2,1)S(1)}, bf16[128,1280]{1,0:T(8,128)(2,1)S(1)}, u32[]{:S(2)}, u32[]{:S(2)}) collective-permute-start(bf16[128,1280]{1,0:T(8,128)(2,1)S(1)} %copy-done.16), channel_id=1, source_target_pairs={{0,6},{2,4},{4,2},{6,0},{8,14},{10,12},{12,10},{14,8},{16,22},{18,... | collective-permute-start | bytes 983048 | tf_op jit(solution)/shard_map/ppermute | solution.py:493
  33.1 1.7 %collective-permute-start.31 = (bf16[128,1280]{1,0:T(8,128)(2,1)S(1)}, bf16[128,1280]{1,0:T(8,128)(2,1)S(1)}, u32[]{:S(2)}, u32[]{:S(2)}) collective-permute-start(bf16[128,1280]{1,0:T(8,128)(2,1)S(1)} %collective-permute-done.28.m1), channel_id=1, source_target_pairs={{0,1},{1,0},{2,3},{3,2},{4,5},{5,4},{6,7},{7,6},{8,9},{9,8},{10,11... | collective-permute-start | bytes 983048 | tf_op jit(solution)/shard_map/ppermute | solution.py:511
  33.2 3.1 %collective-permute-start.32 = (bf16[128,1280]{1,0:T(8,128)(2,1)S(1)}, bf16[128,1280]{1,0:T(8,128)(2,1)S(1)}, u32[]{:S(2)}, u32[]{:S(2)}) collective-permute-start(bf16[128,1280]{1,0:T(8,128)(2,1)S(1)} %collective-permute-done.29.m2), channel_id=1, source_target_pairs={{0,1},{1,0},{2,3},{3,2},{4,5},{5,4},{6,7},{7,6},{8,9},{9,8},{10,11... | collective-permute-start | bytes 983048 | tf_op jit(solution)/shard_map/ppermute | solution.py:511
  33.7 3.8 %collective-permute-start.33 = (bf16[128,1280]{1,0:T(8,128)(2,1)S(1)}, bf16[128,1280]{1,0:T(8,128)(2,1)}, u32[]{:S(2)}, u32[]{:S(2)}) collective-permute-start(bf16[128,1280]{1,0:T(8,128)(2,1)S(1)} %collective-permute-done.30.m3), channel_id=1, source_target_pairs={{0,1},{1,0},{2,3},{3,2},{4,5},{5,4},{6,7},{7,6},{8,9},{9,8},{10,11... | collective-permute-start | bytes 983048 | tf_op jit(solution)/shard_map/ppermute | solution.py:511
  33.8 10.7 %collective-permute-start.34 = (bf16[128,1280]{1,0:T(8,128)(2,1)}, bf16[128,1280]{1,0:T(8,128)(2,1)S(1)}, u32[]{:S(2)}, u32[]{:S(2)}) collective-permute-start(bf16[128,1280]{1,0:T(8,128)(2,1)} %get-tuple-element.121), channel_id=1, source_target_pairs={{0,2},{2,0},{4,6},{6,4},{8,10},{10,8},{12,14},{14,12},{16,18},{18,... | collective-permute-start | bytes 983048 | tf_op jit(solution)/shard_map/ppermute | solution.py:493
  34.9 17.3 %collective-permute-start.37 = (bf16[128,1280]{1,0:T(8,128)(2,1)}, bf16[128,1280]{1,0:T(8,128)(2,1)}, u32[]{:S(2)}, u32[]{:S(2)}) collective-permute-start(bf16[128,1280]{1,0:T(8,128)(2,1)} %get-tuple-element.125), channel_id=1, source_target_pairs={{0,4},{2,6},{4,0},{6,2},{8,12},{10,14},{12,8},{14,10},{16,20},{18,... | collective-permute-start | bytes 983048 | tf_op jit(solution)/shard_map/ppermute | solution.py:493
  36.4 16.3 %collective-permute-start.38 = (bf16[128,1280]{1,0:T(8,128)(2,1)S(1)}, bf16[128,1280]{1,0:T(8,128)(2,1)}, u32[]{:S(2)}, u32[]{:S(2)}) collective-permute-start(bf16[128,1280]{1,0:T(8,128)(2,1)S(1)} %copy-done.15), channel_id=1, source_target_pairs={{0,6},{2,4},{4,2},{6,0},{8,14},{10,12},{12,10},{14,8},{16,22},{18,... | collective-permute-start | bytes 983048 | tf_op jit(solution)/shard_map/ppermute | solution.py:493
  41.9 10.8 %collective-permute-start.36 = (bf16[1024,128]{1,0:T(8,128)(2,1)}, bf16[1024,128]{1,0:T(8,128)(2,1)S(1)}, u32[]{:S(2)}, u32[]{:S(2)}) collective-permute-start(bf16[1024,128]{1,0:T(8,128)(2,1)} %get-tuple-element.120), channel_id=1, source_target_pairs={{0,8},{2,10},{4,12},{6,14},{8,16},{10,18},{12,20},{14,22},{16,24},... | collective-permute-start | bytes 786440 | tf_op jit(solution)/shard_map/ppermute | solution.py:493
  47.8 22.8 %all-to-all-start.4 = ((f16[4,128,1024]{2,1,0:T(8,128)(2,1)}), f16[4,128,1024]{2,1,0:T(8,128)(2,1)}, u32[]{:S(2)}, u32[]{:S(2)}) async-start(f16[4,128,1024]{2,1,0:T(8,128)(2,1)} %bitcast.5), calls=%async_computation.4 | async-start | bytes 2097152 | tf_op jit(solution)/shard_map/all_to_all | solution.py:490
  52.1 4.2 %collective-permute-start.39 = (bf16[128,1280]{1,0:T(8,128)(2,1)S(1)}, bf16[128,1280]{1,0:T(8,128)(2,1)S(1)}, u32[]{:S(2)}, u32[]{:S(2)}) collective-permute-start(bf16[128,1280]{1,0:T(8,128)(2,1)S(1)} %collective-permute-done.34.n1), channel_id=1, source_target_pairs={{0,1},{1,0},{2,3},{3,2},{4,5},{5,4},{6,7},{7,6},{8,9},{9,8},{10,11... | collective-permute-start | bytes 983048 | tf_op jit(solution)/shard_map/ppermute | solution.py:511
  52.2 4.1 %collective-permute-start.40 = (bf16[128,1280]{1,0:T(8,128)(2,1)}, bf16[128,1280]{1,0:T(8,128)(2,1)S(1)}, u32[]{:S(2)}, u32[]{:S(2)}) collective-permute-start(bf16[128,1280]{1,0:T(8,128)(2,1)} %collective-permute-done.37.n2), channel_id=1, source_target_pairs={{0,1},{1,0},{2,3},{3,2},{4,5},{5,4},{6,7},{7,6},{8,9},{9,8},{10,11... | collective-permute-start | bytes 983048 | tf_op jit(solution)/shard_map/ppermute | solution.py:511
  52.7 3.7 %collective-permute-start.41 = (bf16[128,1280]{1,0:T(8,128)(2,1)}, bf16[128,1280]{1,0:T(8,128)(2,1)S(1)}, u32[]{:S(2)}, u32[]{:S(2)}) collective-permute-start(bf16[128,1280]{1,0:T(8,128)(2,1)} %collective-permute-done.38.n3), channel_id=1, source_target_pairs={{0,1},{1,0},{2,3},{3,2},{4,5},{5,4},{6,7},{7,6},{8,9},{9,8},{10,11... | collective-permute-start | bytes 983048 | tf_op jit(solution)/shard_map/ppermute | solution.py:511
  52.8 16.1 %collective-permute-start.42 = (bf16[1024,128]{1,0:T(8,128)(2,1)S(1)}, bf16[1024,128]{1,0:T(8,128)(2,1)}, u32[]{:S(2)}, u32[]{:S(2)}) collective-permute-start(bf16[1024,128]{1,0:T(8,128)(2,1)S(1)} %broadcast_select_fusion.1.xp), channel_id=1, source_target_pairs={{0,16},{2,18},{4,20},{6,22},{8,24},{10,26},{12,28},{14,30},{16,0},... | collective-permute-start | bytes 786440 | tf_op jit(solution)/shard_map/ppermute | solution.py:493
  72.9 15.6 %collective-permute-start.6 = (f16[128,1024]{1,0:T(8,128)(2,1)S(1)}, f16[128,1024]{1,0:T(8,128)(2,1)S(1)}, u32[]{:S(2)}, u32[]{:S(2)}) collective-permute-start(f16[128,1024]{1,0:T(8,128)(2,1)S(1)} %get-tuple-element.60), channel_id=1, source_target_pairs={{16,0},{18,2},{20,4},{22,6},{24,8},{26,10},{28,12},{30,14},{17,1},... | collective-permute-start | bytes 786440 | tf_op jit(solution)/shard_map/cond/branch_0_fun/ppermute | solution.py:561
  74.2 16.2 %collective-permute-start.2 = (bf16[1024,128]{1,0:T(8,128)(2,1)S(1)}, bf16[1024,128]{1,0:T(8,128)(2,1)S(1)}, u32[]{:S(2)}, u32[]{:S(2)}) collective-permute-start(bf16[1024,128]{1,0:T(8,128)(2,1)S(1)} %get-tuple-element.57), channel_id=1, source_target_pairs={{8,24},{10,26},{12,28},{14,30},{9,25},{11,27},{13,29},{15,31}} | collective-permute-start | bytes 786440 | tf_op jit(solution)/shard_map/cond/branch_0_fun/ppermute | solution.py:561
  74.9 21.9 %collective-permute-start.1 = (bf16[1024,128]{1,0:T(8,128)(2,1)S(1)}, bf16[1024,128]{1,0:T(8,128)(2,1)S(1)}, u32[]{:S(2)}, u32[]{:S(2)}) collective-permute-start(bf16[1024,128]{1,0:T(8,128)(2,1)S(1)} %get-tuple-element.57), channel_id=1, source_target_pairs={{8,16},{10,18},{12,20},{14,22},{9,17},{11,19},{13,21},{15,23}} | collective-permute-start | bytes 786440 | tf_op jit(solution)/shard_map/cond/branch_0_fun/ppermute | solution.py:561
  75.6 21.2 %collective-permute-start = (bf16[1024,128]{1,0:T(8,128)(2,1)S(1)}, bf16[1024,128]{1,0:T(8,128)(2,1)S(1)}, u32[]{:S(2)}, u32[]{:S(2)}) collective-permute-start(bf16[1024,128]{1,0:T(8,128)(2,1)S(1)} %get-tuple-element.57), channel_id=1, source_target_pairs={{8,0},{10,2},{12,4},{14,6},{9,1},{11,3},{13,5},{15,7}} | collective-permute-start | bytes 786440 | tf_op jit(solution)/shard_map/cond/branch_0_fun/ppermute | solution.py:561
  76.9 24.5 %collective-permute-start.5 = (bf16[1024,128]{1,0:T(8,128)(2,1)}, bf16[1024,128]{1,0:T(8,128)(2,1)}, u32[]{:S(2)}, u32[]{:S(2)}) collective-permute-start(bf16[1024,128]{1,0:T(8,128)(2,1)} %get-tuple-element.58), channel_id=1, source_target_pairs={{0,6},{2,4},{4,2},{6,0},{8,14},{10,12},{12,10},{14,8},{16,22},{18,... | collective-permute-start | bytes 786440 | tf_op jit(solution)/shard_map/cond/branch_0_fun/ppermute | solution.py:493
  88.5 12.9 %collective-permute-start.4 = (bf16[1024,128]{1,0:T(8,128)(2,1)}, bf16[1024,128]{1,0:T(8,128)(2,1)}, u32[]{:S(2)}, u32[]{:S(2)}) collective-permute-start(bf16[1024,128]{1,0:T(8,128)(2,1)} %get-tuple-element.58), channel_id=1, source_target_pairs={{0,4},{2,6},{4,0},{6,2},{8,12},{10,14},{12,8},{14,10},{16,20},{18,... | collective-permute-start | bytes 786440 | tf_op jit(solution)/shard_map/cond/branch_0_fun/ppermute | solution.py:493
  90.4 11.0 %collective-permute-start.3 = (bf16[1024,128]{1,0:T(8,128)(2,1)}, bf16[1024,128]{1,0:T(8,128)(2,1)}, u32[]{:S(2)}, u32[]{:S(2)}) collective-permute-start(bf16[1024,128]{1,0:T(8,128)(2,1)} %get-tuple-element.58), channel_id=1, source_target_pairs={{0,2},{2,0},{4,6},{6,4},{8,10},{10,8},{12,14},{14,12},{16,18},{18,... | collective-permute-start | bytes 786440 | tf_op jit(solution)/shard_map/cond/branch_0_fun/ppermute | solution.py:493
  91.9 9.5 %all-to-all-start = ((bf16[4,256,128]{2,1,0:T(8,128)(2,1)}), bf16[4,256,128]{2,1,0:T(8,128)(2,1)}, u32[]{:S(2)}, u32[]{:S(2)}) async-start(bf16[4,256,128]{2,1,0:T(8,128)(2,1)} %bitcast), calls=%async_computation | async-start | bytes 524288 | tf_op jit(solution)/shard_map/cond/branch_0_fun/all_to_all | solution.py:490
  106.5 13.9 %collective-permute-start.43 = (f32[128,1024]{1,0:T(8,128)}, f32[128,1024]{1,0:T(8,128)S(1)}, u32[]{:S(2)}, u32[]{:S(2)}) collective-permute-start(f32[128,1024]{1,0:T(8,128)} %get-tuple-element.131), channel_id=1, source_target_pairs={{0,24},{2,26},{4,28},{6,30},{8,0},{10,2},{12,4},{14,6},{16,8},{18,... | collective-permute-start | bytes 1572872 | tf_op jit(solution)/shard_map/ppermute | solution.py:493
  106.6 10.4 %collective-permute-start.46 = (bf16[1024,128]{1,0:T(8,128)(2,1)S(1)}, bf16[1024,128]{1,0:T(8,128)(2,1)}, u32[]{:S(2)}, u32[]{:S(2)}) collective-permute-start(bf16[1024,128]{1,0:T(8,128)(2,1)S(1)} %get-tuple-element.137.x0), channel_id=1, source_target_pairs={{0,6},{2,4},{4,2},{6,0},{8,14},{10,12},{12,10},{14,8},{16,22},{18,... | collective-permute-start | bytes 786440 | tf_op jit(solution)/shard_map/ppermute | solution.py:493
  109.0 11.4 %collective-permute-start.45 = (bf16[1024,128]{1,0:T(8,128)(2,1)S(1)}, bf16[1024,128]{1,0:T(8,128)(2,1)}, u32[]{:S(2)}, u32[]{:S(2)}) collective-permute-start(bf16[1024,128]{1,0:T(8,128)(2,1)S(1)} %get-tuple-element.137.x0), channel_id=1, source_target_pairs={{0,4},{2,6},{4,0},{6,2},{8,12},{10,14},{12,8},{14,10},{16,20},{18,... | collective-permute-start | bytes 786440 | tf_op jit(solution)/shard_map/ppermute | solution.py:493
  109.6 10.8 %collective-permute-start.44 = (bf16[1024,128]{1,0:T(8,128)(2,1)S(1)}, bf16[1024,128]{1,0:T(8,128)(2,1)}, u32[]{:S(2)}, u32[]{:S(2)}) collective-permute-start(bf16[1024,128]{1,0:T(8,128)(2,1)S(1)} %get-tuple-element.137.x0), channel_id=1, source_target_pairs={{0,2},{2,0},{4,6},{6,4},{8,10},{10,8},{12,14},{14,12},{16,18},{18,... | collective-permute-start | bytes 786440 | tf_op jit(solution)/shard_map/ppermute | solution.py:493
  125.5 10.4 %collective-permute-start.47 = (f32[256,128]{1,0:T(8,128)}, f32[256,128]{1,0:T(8,128)S(1)}, u32[]{:S(2)}, u32[]{:S(2)}) collective-permute-start(f32[256,128]{1,0:T(8,128)} %get-tuple-element.143), channel_id=1, source_target_pairs={{0,2},{2,0},{4,6},{6,4},{8,10},{10,8},{12,14},{14,12},{16,18},{18,... | collective-permute-start | bytes 393224 | tf_op jit(solution)/shard_map/ppermute | solution.py:493
  126.6 9.3 %collective-permute-start.48 = (f32[256,128]{1,0:T(8,128)}, f32[256,128]{1,0:T(8,128)S(1)}, u32[]{:S(2)}, u32[]{:S(2)}) collective-permute-start(f32[256,128]{1,0:T(8,128)} %get-tuple-element.144), channel_id=1, source_target_pairs={{0,4},{2,6},{4,0},{6,2},{8,12},{10,14},{12,8},{14,10},{16,20},{18,... | collective-permute-start | bytes 393224 | tf_op jit(solution)/shard_map/ppermute | solution.py:493
  127.8 8.1 %collective-permute-start.49 = (f32[256,128]{1,0:T(8,128)}, f32[256,128]{1,0:T(8,128)S(1)}, u32[]{:S(2)}, u32[]{:S(2)}) collective-permute-start(f32[256,128]{1,0:T(8,128)} %get-tuple-element.145), channel_id=1, source_target_pairs={{0,6},{2,4},{4,2},{6,0},{8,14},{10,12},{12,10},{14,8},{16,22},{18,... | collective-permute-start | bytes 393224 | tf_op jit(solution)/shard_map/ppermute | solution.py:493
  (18 other events, 81.8 us)
